TPU v7x, 128 devices: a whole 4x4x4 slice. The times are simulated.
128 devices in a mesh: row: 16 (over y, z), col: 8 (over x, core).
Axes of the slice: x: 4, y: 4, z: 4, core: 2. Of those that a mesh axis runs over, the one named last changes fastest.
Arguments:
- x_points: float32 [64, 262144], P(None, ('row', 'col')), as said below
- y_points: float32 [64, 262144], P(None, ('row', 'col')), as said below
- x_logmass: float32 [262144], P(('row', 'col')), may hold values from -1 to 1
- y_logmass: float32 [262144], P(('row', 'col')), may hold values from -1 to 1
- x_sizes: int32 [128, 8], P(('row', 'col')), may hold values from 1 to 256, 1664 in all within a row
- y_sizes: int32 [128, 8], P(('row', 'col')), may hold values from 1 to 256, 1664 in all within a row
- cross_pairs: int32 [1024, 7], P(('row', 'col')), may hold values from 0 to 1023, as said below
- xself_pairs: int32 [1024, 2], P(('row', 'col')), may hold values from 0 to 1023, as said below
- yself_pairs: int32 [1024, 2], P(('row', 'col')), may hold values from 0 to 1023, as said below
Outputs:
- x_cross: float32 [262144], P(('row', 'col'))
- y_cross: float32 [262144], P(('row', 'col'))
- x_self: float32 [262144], P(('row', 'col'))
- y_self: float32 [262144], P(('row', 'col'))
Inputs may be any that keep to these rules, and one draw needn't show every extreme that they name: Each row of a device's lists names different clusters, none held by the device itself. Counting the entries of cross_pairs, xself_pairs and yself_pairs in the rows of one device's 8 clusters, a device is named either never or exactly 1 times; the named clusters of one device in these entries are all different. A self partner lies on the device 1 to 63 places after the lister's device, cyclically, so no unordered pair is listed twice. `xself_pairs`: as stated for cross_pairs. `yself_pairs`: as stated for cross_pairs. `x_sizes`: each row sums to 1664. `y_sizes`: each row sums to 1664. `x_points`: points of a cluster scatter around a common centre. `y_points`: points of a cluster scatter around a common centre.
All inputs are finite; a program needn't handle non-finite values.
Results may differ from a plain program's by a relative error of at most 0.0003.
Values sent between devices are 32-bit elements; how exact they have to be, the bound alone decides.
No kernel may reach another device: no remote copies, remote signals or barrier semaphores. Data moves between devices by JAX's collectives and lax.ppermute only.
A program may use at most 128 MiB of HBM per device.

v0:
```python
import math

import jax
import jax.numpy as jnp
from jax import lax
from jax.sharding import PartitionSpec as P

ITERS = 3


EPSILON = 0.5
DAMPING = 2.0 / (2.0 + 0.5)
NEGATIVE = -1e30
HIGHEST = lax.Precision.HIGHEST


def tile_terms(row_coords, row_half, row_offset, col_coords, col_half, col_offset):
    inner = jnp.einsum("ndi,ndj->nij", row_coords, col_coords, precision=HIGHEST)
    scaled = (row_half[:, :, None] + col_half[:, None, :] - inner) / EPSILON
    row_score = col_offset[:, None, :] - scaled
    row_peak = jnp.max(row_score, axis=2)
    row_total = jnp.sum(jnp.exp(row_score - row_peak[:, :, None]), axis=2)
    col_score = row_offset[:, :, None] - scaled
    col_peak = jnp.max(col_score, axis=1)
    col_total = jnp.sum(jnp.exp(col_score - col_peak[:, None, :]), axis=1)
    return (row_peak, row_total, col_peak, col_total)


def block_view(points, clusters):
    return points.reshape(points.shape[0], clusters, -1).transpose(1, 0, 2)


def move_blocks(reply_coords, reply_mass, devices, capacity):
    fetched_coords, fetched_mass = (
        lax.all_to_all(reply_coords, ("row", "col"), split_axis=0, concat_axis=0, tiled=True),
        lax.all_to_all(reply_mass, ("row", "col"), split_axis=0, concat_axis=0, tiled=True),
    )
    return (
        fetched_coords.reshape((devices * capacity,) + reply_coords.shape[2:]),
        fetched_mass.reshape(devices * capacity, reply_mass.shape[2]),
    )


def move_potentials(reply_potential, devices, capacity):
    fetched_potential = lax.all_to_all(
        reply_potential, ("row", "col"), split_axis=0, concat_axis=0, tiled=True
    )
    return fetched_potential.reshape(devices * capacity, reply_potential.shape[2])


def stacked_log(peak_list, total_list):
    peaks = jnp.stack(peak_list)
    totals = jnp.stack(total_list)
    top = jnp.max(peaks, axis=0)
    return (top, jnp.sum(totals * jnp.exp(peaks - top[None]), axis=0))


def local(
    x_points,
    y_points,
    x_logmass,
    y_logmass,
    x_sizes,
    y_sizes,
    cross_pairs,
    xself_pairs,
    yself_pairs,
):
    clusters = x_sizes.shape[1]
    feature_dim = x_points.shape[0]
    members = x_points.shape[1] // clusters
    devices = lax.axis_size(("row", "col"))
    capacity = clusters * 16 // devices
    stacked = jnp.concatenate(
        [block_view(x_points, clusters), block_view(y_points, clusters)], axis=0
    )
    halves = 0.5 * jnp.sum(stacked * stacked, axis=1)
    counts = jnp.concatenate([x_sizes.reshape(clusters), y_sizes.reshape(clusters)])
    position = lax.broadcasted_iota(jnp.int32, (2 * clusters, members), 1)
    valid_mask = position < counts[:, None]
    masses = jnp.where(
        valid_mask, jnp.concatenate([x_logmass, y_logmass]).reshape(2 * clusters, members), NEGATIVE
    )
    cross_count = cross_pairs.shape[1]
    self_count = xself_pairs.shape[1]
    wanted = jnp.concatenate(
        [cross_pairs.reshape(-1), xself_pairs.reshape(-1), yself_pairs.reshape(-1)]
    )
    request_kind = jnp.concatenate(
        [
            jnp.zeros((clusters * cross_count,), jnp.int32),
            jnp.ones((clusters * self_count,), jnp.int32),
            jnp.full((clusters * self_count,), 2, jnp.int32),
        ]
    )
    owners = wanted // clusters
    request_code = request_kind * clusters + wanted % clusters
    request_total = wanted.shape[0]
    earlier = lax.broadcasted_iota(
        jnp.int32, (request_total, request_total), 1
    ) < lax.broadcasted_iota(jnp.int32, (request_total, request_total), 0)
    same_owner = owners[None, :] == owners[:, None]
    slot_rank = jnp.sum((same_owner & earlier).astype(jnp.int32), axis=1)
    slot_index = owners * capacity + slot_rank
    outgoing = (
        jnp.full((devices * capacity,), -1, jnp.int32)
        .at[slot_index]
        .set(request_code)
        .reshape(devices, capacity)
    )
    incoming = lax.all_to_all(
        outgoing, ("row", "col"), split_axis=0, concat_axis=0, tiled=True
    ).reshape(-1)
    asked_kind = incoming // clusters
    asked_local = incoming % clusters
    asked_block = jnp.where(asked_kind == 1, asked_local, clusters + asked_local)
    asked_potential = (asked_kind + 1) * clusters + asked_local
    back_target = jnp.where(incoming >= 0, asked_potential, 4 * clusters)
    reply_coords = stacked[asked_block].reshape(devices, capacity, feature_dim, members)
    reply_mass = masses[asked_block].reshape(devices, capacity, members)
    fetched_coords, fetched_mass = move_blocks(reply_coords, reply_mass, devices, capacity)
    cross_total = clusters * cross_count
    self_total = clusters * self_count
    cross_slots = slot_index[:cross_total].reshape(clusters, cross_count).T.reshape(-1)
    xself_slots = (
        slot_index[cross_total : cross_total + self_total]
        .reshape(clusters, self_count)
        .T.reshape(-1)
    )
    yself_slots = slot_index[cross_total + self_total :].reshape(clusters, self_count).T.reshape(-1)
    order_slots = jnp.concatenate([cross_slots, xself_slots, yself_slots])
    group_count = cross_count + 2 * self_count
    remote_coords = fetched_coords[order_slots].reshape(group_count, clusters, feature_dim, members)
    remote_half = 0.5 * jnp.sum(remote_coords * remote_coords, axis=2)
    remote_mass = fetched_mass[order_slots].reshape(group_count, clusters, members)
    x_coords = stacked[:clusters]
    y_coords = stacked[clusters:]
    x_half = halves[:clusters]
    y_half = halves[clusters:]
    x_mass = masses[:clusters]
    y_mass = masses[clusters:]
    slot_total = devices * capacity
    block_size = math.gcd(slot_total, 128)
    block_count = slot_total // block_size
    segment_ids = lax.broadcasted_iota(jnp.int32, (3 * clusters, slot_total), 0)
    back_mask = (back_target - clusters)[None, :] == segment_ids
    back_hot = back_mask.astype(jnp.float32)
    back_hot_t = back_hot.T
    mask_blocks = back_mask.reshape(3 * clusters, block_count, block_size).transpose(1, 0, 2)

    def block_top(carry, pieces):
        mask_piece, peak_piece = pieces
        masked = jnp.where(mask_piece[:, :, None], peak_piece[None, :, :], NEGATIVE)
        return (jnp.maximum(carry, jnp.max(masked, axis=1)), None)

    potentials = jnp.zeros((4 * clusters, members), jnp.float32)
    for iteration in range(ITERS):
        reply_potential = potentials[asked_potential].reshape(devices, capacity, members)
        fetched_potential = move_potentials(reply_potential, devices, capacity)
        remote_potential = fetched_potential[order_slots].reshape(group_count, clusters, members)
        remote_offset = remote_mass + remote_potential / EPSILON
        f_offset = x_mass + potentials[:clusters] / EPSILON
        g_offset = y_mass + potentials[clusters : 2 * clusters] / EPSILON
        p_offset = x_mass + potentials[2 * clusters : 3 * clusters] / EPSILON
        q_offset = y_mass + potentials[3 * clusters :] / EPSILON
        a_row_peak, a_row_total, a_col_peak, a_col_total = tile_terms(
            x_coords, x_half, f_offset, y_coords, y_half, g_offset
        )
        f_peaks, f_totals = ([a_row_peak], [a_row_total])
        p_peaks, p_totals = ([], [])
        q_peaks, q_totals = ([], [])
        send_peaks, send_totals = ([], [])
        for group in range(group_count):
            if group < cross_count:
                row_coords, row_half, row_offset = (x_coords, x_half, f_offset)
                peak_list, total_list = (f_peaks, f_totals)
            elif group < cross_count + self_count:
                row_coords, row_half, row_offset = (x_coords, x_half, p_offset)
                peak_list, total_list = (p_peaks, p_totals)
            else:
                row_coords, row_half, row_offset = (y_coords, y_half, q_offset)
                peak_list, total_list = (q_peaks, q_totals)
            row_peak, row_total, col_peak, col_total = tile_terms(
                row_coords,
                row_half,
                row_offset,
                remote_coords[group],
                remote_half[group],
                remote_offset[group],
            )
            peak_list.append(row_peak)
            total_list.append(row_total)
            send_peaks.append(col_peak)
            send_totals.append(col_total)
        self_x = tile_terms(x_coords, x_half, p_offset, x_coords, x_half, p_offset)
        p_peaks.append(self_x[0])
        p_totals.append(self_x[1])
        self_y = tile_terms(y_coords, y_half, q_offset, y_coords, y_half, q_offset)
        q_peaks.append(self_y[0])
        q_totals.append(self_y[1])
        sent_peak = jnp.concatenate(send_peaks, axis=0)
        sent_total = jnp.concatenate(send_totals, axis=0)
        send_peak = (
            jnp.full((slot_total, members), NEGATIVE, jnp.float32).at[order_slots].set(sent_peak)
        )
        send_total = jnp.ones((slot_total, members), jnp.float32).at[order_slots].set(sent_total)
        back_peak, back_total = (
            lax.all_to_all(
                send_peak.reshape(devices, capacity, members),
                ("row", "col"),
                split_axis=0,
                concat_axis=0,
                tiled=True,
            ),
            lax.all_to_all(
                send_total.reshape(devices, capacity, members),
                ("row", "col"),
                split_axis=0,
                concat_axis=0,
                tiled=True,
            ),
        )
        back_peak = back_peak.reshape(-1, members)
        back_total = back_total.reshape(-1, members)
        f_top, f_sum = stacked_log(f_peaks, f_totals)
        f_log = f_top + jnp.log(f_sum)
        p_top = jnp.max(jnp.stack(p_peaks), axis=0)
        q_top = jnp.max(jnp.stack(q_peaks), axis=0)
        local_top = jnp.concatenate([a_col_peak, p_top, q_top], axis=0)
        remote_top, _ = lax.scan(
            block_top,
            jnp.full((3 * clusters, members), NEGATIVE, jnp.float32),
            (mask_blocks, back_peak.reshape(block_count, block_size, members)),
        )
        top_all = jnp.maximum(local_top, remote_top)
        g_top = top_all[:clusters]
        p_top = top_all[clusters : 2 * clusters]
        q_top = top_all[2 * clusters :]
        g_local = a_col_total * jnp.exp(a_col_peak - g_top)
        p_local = jnp.sum(jnp.stack(p_totals) * jnp.exp(jnp.stack(p_peaks) - p_top[None]), axis=0)
        q_local = jnp.sum(jnp.stack(q_totals) * jnp.exp(jnp.stack(q_peaks) - q_top[None]), axis=0)
        slot_top = jnp.dot(
            back_hot_t, top_all, precision=HIGHEST, preferred_element_type=jnp.float32
        )
        back_weighted = back_total * jnp.exp(back_peak - slot_top)
        back_sum = jnp.dot(
            back_hot, back_weighted, precision=HIGHEST, preferred_element_type=jnp.float32
        )
        gpq_log = top_all + jnp.log(jnp.concatenate([g_local, p_local, q_local], axis=0) + back_sum)
        log_total = jnp.concatenate([f_log, gpq_log], axis=0)
        potentials = 0.5 * (potentials - DAMPING * EPSILON * log_total)
    finals = jnp.where(jnp.concatenate([valid_mask, valid_mask], axis=0), potentials, 0.0)
    return (
        finals[:clusters].reshape(-1),
        finals[clusters : 2 * clusters].reshape(-1),
        finals[2 * clusters : 3 * clusters].reshape(-1),
        finals[3 * clusters :].reshape(-1),
    )


def solution(mesh):
    placed = (
        P(None, ("row", "col")),
        P(None, ("row", "col")),
        P(("row", "col")),
        P(("row", "col")),
        P(("row", "col"), None),
        P(("row", "col"), None),
        P(("row", "col"), None),
        P(("row", "col"), None),
        P(("row", "col"), None),
    )
    return jax.shard_map(
        local,
        mesh=mesh,
        in_specs=placed,
        out_specs=(P(("row", "col")), P(("row", "col")), P(("row", "col")), P(("row", "col"))),
        check_vma=False,
    )
```

profile of v0, /device:TPU:1, one launch (start us, length us, event | category | flops | bytes accessed | tf_op | source)
XLA Modules:
  0.0 418.1 jit_solution(3101386689253287475)
XLA Ops:
  6.7 11.5 %all-to-all-start = ((s32[128,1,1]{2,1,0:T(1,128)}), s32[128,1,1]{2,1,0:T(1,128)S(1)}, u32[]{:S(2)}, u32[]{:S(2)}) async-start(s32[128,1,1]{2,1,0:T(1,128)} %copy.125), calls=%async_computation | async-start | bytes 131072 | tf_op jit(solution)/shard_map/all_to_all | solution.py:111
  20.4 7.3 %all-to-all-done = s32[128,1,1]{2,1,0:T(1,128)S(1)} async-done(((s32[128,1,1]{2,1,0:T(1,128)}), s32[128,1,1]{2,1,0:T(1,128)S(1)}, u32[]{:S(2)}, u32[]{:S(2)}) %all-to-all-start) | async-done | bytes 544 | tf_op jit(solution)/shard_map/all_to_all | solution.py:111
  27.7 2.3 reduce.43
  31.7 4.6 %all-to-all-start.1 = ((f32[128,1,256]{2,1,0:T(1,128)}), f32[128,1,256]{2,1,0:T(1,128)S(1)}, u32[]{:S(2)}, u32[]{:S(2)}) async-start(f32[128,1,256]{2,1,0:T(1,128)} %copy.126), calls=%async_computation.1 | async-start | bytes 262144 | tf_op jit(solution)/shard_map/all_to_all | solution.py:36
  38.0 8.3 %all-to-all-done.1 = f32[128,1,256]{2,1,0:T(1,128)S(1)} async-done(((f32[128,1,256]{2,1,0:T(1,128)}), f32[128,1,256]{2,1,0:T(1,128)S(1)}, u32[]{:S(2)}, u32[]{:S(2)}) %all-to-all-start.1) | async-done | bytes 131104 | tf_op jit(solution)/shard_map/all_to_all | solution.py:36
  46.3 4.2 %all-to-all-start.2 = ((f32[128,1,256]{2,1,0:T(1,128)}), f32[128,1,256]{2,1,0:T(1,128)S(1)}, u32[]{:S(2)}, u32[]{:S(2)}) async-start(f32[128,1,256]{2,1,0:T(1,128)} %copy.130), calls=%async_computation.2 | async-start | bytes 262144 | tf_op jit(solution)/shard_map/all_to_all | solution.py:45
  50.7 4.3 %gather_fusion.4 = f32[128,64,256]{2,1,0:T(8,128)} fusion(f32[16,64,256]{2,1,0:T(8,128)S(1)} %get-tuple-element.217, s32[1024]{0:T(1024)S(1)} %get-tuple-element.376), kind=kCustom, calls=%fused_computation.4 | custom fusion | bytes 16777728 | tf_op jit(solution)/shard_map/gather | solution.py:119
  55.0 5.5 %all-to-all-done.2 = f32[128,1,256]{2,1,0:T(1,128)S(1)} async-done(((f32[128,1,256]{2,1,0:T(1,128)}), f32[128,1,256]{2,1,0:T(1,128)S(1)}, u32[]{:S(2)}, u32[]{:S(2)}) %all-to-all-start.2) | async-done | bytes 131104 | tf_op jit(solution)/shard_map/all_to_all | solution.py:45
  60.5 5.3 %all-to-all-start.3 = ((f32[128,1,64,256]{3,2,1,0:T(8,128)}), f32[128,1,64,256]{3,2,1,0:T(8,128)}, u32[]{:S(2)}, u32[]{:S(2)}) async-start(f32[128,1,64,256]{3,2,1,0:T(8,128)} %bitcast.348), calls=%async_computation.3 | async-start | bytes 16777216 | tf_op jit(solution)/shard_map/all_to_all | solution.py:35
  68.1 3.4 subtract_multiply_fusion.1
  71.5 2.1 subtract_multiply_fusion
  73.6 3.4 subtract_multiply_fusion.2
  79.1 86.0 %all-to-all-done.3 = f32[128,1,64,256]{3,2,1,0:T(8,128)} async-done(((f32[128,1,64,256]{3,2,1,0:T(8,128)}), f32[128,1,64,256]{3,2,1,0:T(8,128)}, u32[]{:S(2)}, u32[]{:S(2)}) %all-to-all-start.3) | async-done | bytes 8388640 | tf_op jit(solution)/shard_map/all_to_all | solution.py:35
  165.1 6.8 %gather_fusion.5 = f32[88,64,256]{2,1,0:T(8,128)} fusion(f32[128,64,256]{2,1,0:T(8,128)} %bitcast.16, s32[1024]{0:T(1024)S(1)} %pad_clamp_fusion.1), kind=kCustom, calls=%fused_computation.5 | custom fusion | bytes 11534688 | tf_op jit(solution)/shard_map/gather | solution.py:133
  172.0 3.7 multiply_reduce_fusion
  176.4 3.1 fusion.7
  179.5 2.2 fusion.8
  181.7 2.0 fusion.9
  183.8 2.0 fusion.4
  185.8 2.0 fusion
  187.8 2.0 fusion.2
  189.8 2.0 fusion.1
  192.8 7.8 %subtract_reduce_fusion.72 = (f32[8,256]{1,0:T(8,128)}, f32[8,256]{1,0:T(8,128)}, f32[8,256]{1,0:T(8,128)}, f32[8,256]{1,0:T(8,128)}, f32[8,256]{1,0:T(8,128)}, ...) fusion(f32[8,256]{1,0:T(8,128)} %get-tuple-element.246, ...), kind=kOutput, calls=%fused_computation.196 | convolution fusion | flops 420970496 | bytes 25378816 | tf_op jit(solution)/shard_map/ndi,ndj->nij/dot_general | solution.py:18
  201.4 8.1 %exponential_reduce_fusion.64 = (f32[8,256]{1,0:T(8,128)}, f32[8,256]{1,0:T(8,128)}, f32[8,256]{1,0:T(8,128)}, f32[8,256]{1,0:T(8,128)S(1)}, f32[8,256]{1,0:T(8,...) fusion(f32[8,256,256]{2,1,0:T(8,128)S(1)} %fusion, ...), kind=kOutput, calls=%fused_computation.107 | convolution fusion | flops 419930112 | bytes 21184512 | tf_op jit(solution)/shard_map/ndi,ndj->nij/dot_general | solution.py:18
  210.4 6.8 %exponential_reduce_fusion.67 = (f32[8,256]{1,0:T(8,128)}, f32[8,256]{1,0:T(8,128)}, f32[8,256]{1,0:T(8,128)S(1)}, f32[8,256]{1,0:T(8,128)S(1)}, f32[8,256]{1,0:...) fusion(f32[8,256,256]{2,1,0:T(8,128)S(1)} %fusion.2, ...), kind=kOutput, calls=%fused_computation.110 | convolution fusion | flops 418885632 | bytes 16990208 | tf_op jit(solution)/shard_map/ndi,ndj->nij/dot_general | solution.py:18
  217.3 6.5 %exponential_reduce_fusion.71 = (f32[8,256]{1,0:T(8,128)}, f32[8,256]{1,0:T(8,128)}, f32[8,256]{1,0:T(8,128)}, f32[8,256]{1,0:T(8,128)}, f32[8,256]{1,0:T(8,128)...) fusion(f32[8,256,256]{2,1,0:T(8,128)S(1)} %get-tuple-element.37, ...), kind=kOutput, calls=%fused_computation.116 | convolution fusion | flops 418885632 | bytes 16990208 | tf_op jit(solution)/shard_map/ndi,ndj->nij/dot_general | solution.py:18
  224.1 1.2 exponential_reduce_fusion.76
  225.7 1.2 exponential_reduce_fusion.65
  226.9 1.0 scatter_custom_fusion.1
  228.7 12.6 %all-to-all-start.4 = ((f32[128,1,256]{2,1,0:T(1,128)}), f32[128,1,256]{2,1,0:T(1,128)S(1)}, u32[]{:S(2)}, u32[]{:S(2)}) async-start(f32[128,1,256]{2,1,0:T(1,128)} %reshape.1227), calls=%async_computation.4 | async-start | bytes 262144 | tf_op jit(solution)/shard_map/all_to_all | solution.py:208
  241.6 1.0 scatter_custom_fusion.2
  244.4 7.0 %all-to-all-done.4 = f32[128,1,256]{2,1,0:T(1,128)S(1)} async-done(((f32[128,1,256]{2,1,0:T(1,128)}), f32[128,1,256]{2,1,0:T(1,128)S(1)}, u32[]{:S(2)}, u32[]{:S(2)}) %all-to-all-start.4) | async-done | bytes 131104 | tf_op jit(solution)/shard_map/all_to_all | solution.py:208
  251.4 4.2 %all-to-all-start.5 = ((f32[128,1,256]{2,1,0:T(1,128)}), f32[128,1,256]{2,1,0:T(1,128)S(1)}, u32[]{:S(2)}, u32[]{:S(2)}) async-start(f32[128,1,256]{2,1,0:T(1,128)} %reshape.1228), calls=%async_computation.5 | async-start | bytes 262144 | tf_op jit(solution)/shard_map/all_to_all | solution.py:215
  256.5 9.1 %all-to-all-done.5 = f32[128,1,256]{2,1,0:T(1,128)S(1)} async-done(((f32[128,1,256]{2,1,0:T(1,128)}), f32[128,1,256]{2,1,0:T(1,128)S(1)}, u32[]{:S(2)}, u32[]{:S(2)}) %all-to-all-start.5) | async-done | bytes 131104 | tf_op jit(solution)/shard_map/all_to_all | solution.py:215
  267.7 4.8 %all-to-all-start.6 = ((f32[128,1,256]{2,1,0:T(1,128)}), f32[128,1,256]{2,1,0:T(1,128)S(1)}, u32[]{:S(2)}, u32[]{:S(2)}) async-start(f32[128,1,256]{2,1,0:T(1,128)} %copy.144), calls=%async_computation.6 | async-start | bytes 262144 | tf_op jit(solution)/shard_map/all_to_all | solution.py:45
  272.5 2.2 subtract_reduce_fusion.51
  274.7 7.7 %all-to-all-done.6 = f32[128,1,256]{2,1,0:T(1,128)S(1)} async-done(((f32[128,1,256]{2,1,0:T(1,128)}), f32[128,1,256]{2,1,0:T(1,128)S(1)}, u32[]{:S(2)}, u32[]{:S(2)}) %all-to-all-start.6) | async-done | bytes 131104 | tf_op jit(solution)/shard_map/all_to_all | solution.py:45
  283.3 7.7 %exponential_reduce_fusion.51 = (f32[8,256]{1,0:T(8,128)S(1)}, f32[8,256]{1,0:T(8,128)S(1)}, f32[8,256]{1,0:T(8,128)S(1)}, f32[8,256]{1,0:T(8,128)S(1)}, f32[8,2...) fusion(f32[8,256,256]{2,1,0:T(8,128)} %subtract_multiply_fusion, ...), kind=kLoop, calls=%fused_computation.94 | loop fusion | flops 17793024 | bytes 16998400 | tf_op jit(solution)/shard_map/reduce_sum | solution.py:22
  291.1 3.3 exponential_reduce_fusion.48
  294.6 4.7 %exponential_reduce_fusion.44 = (f32[8,256]{1,0:T(8,128)S(1)}, f32[8,256]{1,0:T(8,128)S(1)}, f32[8,256]{1,0:T(8,128)S(1)}, f32[8,256]{1,0:T(8,128)S(1)}, f32[8,2...) fusion(f32[8,256,256]{2,1,0:T(8,128)S(1)} %copy-done.8, ...), kind=kLoop, calls=%fused_computation.87 | loop fusion | flops 12566528 | bytes 8560640 | tf_op jit(solution)/shard_map/reduce_sum | solution.py:22
  301.0 2.3 exponential_reduce_fusion.41
  303.4 1.2 exponential_reduce_fusion.42
  306.5 2.3 exponential_reduce_fusion.38
  308.8 1.2 exponential_reduce_fusion.39
  310.0 1.0 scatter_custom_fusion.3
  311.9 4.3 %all-to-all-start.7 = ((f32[128,1,256]{2,1,0:T(1,128)}), f32[128,1,256]{2,1,0:T(1,128)S(1)}, u32[]{:S(2)}, u32[]{:S(2)}) async-start(f32[128,1,256]{2,1,0:T(1,128)} %copy.145), calls=%async_computation.7 | async-start | bytes 262144 | tf_op jit(solution)/shard_map/all_to_all | solution.py:208
  316.3 1.0 scatter_custom_fusion.4
  318.2 7.9 %all-to-all-done.7 = f32[128,1,256]{2,1,0:T(1,128)S(1)} async-done(((f32[128,1,256]{2,1,0:T(1,128)}), f32[128,1,256]{2,1,0:T(1,128)S(1)}, u32[]{:S(2)}, u32[]{:S(2)}) %all-to-all-start.7) | async-done | bytes 131104 | tf_op jit(solution)/shard_map/all_to_all | solution.py:208
  326.2 4.2 %all-to-all-start.8 = ((f32[128,1,256]{2,1,0:T(1,128)}), f32[128,1,256]{2,1,0:T(1,128)S(1)}, u32[]{:S(2)}, u32[]{:S(2)}) async-start(f32[128,1,256]{2,1,0:T(1,128)} %copy.146), calls=%async_computation.8 | async-start | bytes 262144 | tf_op jit(solution)/shard_map/all_to_all | solution.py:215
  331.2 9.2 %all-to-all-done.8 = f32[128,1,256]{2,1,0:T(1,128)S(1)} async-done(((f32[128,1,256]{2,1,0:T(1,128)}), f32[128,1,256]{2,1,0:T(1,128)S(1)}, u32[]{:S(2)}, u32[]{:S(2)}) %all-to-all-start.8) | async-done | bytes 131104 | tf_op jit(solution)/shard_map/all_to_all | solution.py:215
  342.5 4.5 %all-to-all-start.9 = ((f32[128,1,256]{2,1,0:T(1,128)}), f32[128,1,256]{2,1,0:T(1,128)S(1)}, u32[]{:S(2)}, u32[]{:S(2)}) async-start(f32[128,1,256]{2,1,0:T(1,128)} %copy.147), calls=%async_computation.9 | async-start | bytes 262144 | tf_op jit(solution)/shard_map/all_to_all | solution.py:45
  347.1 2.2 subtract_reduce_fusion.25
  349.3 7.7 %all-to-all-done.9 = f32[128,1,256]{2,1,0:T(1,128)S(1)} async-done(((f32[128,1,256]{2,1,0:T(1,128)}), f32[128,1,256]{2,1,0:T(1,128)S(1)}, u32[]{:S(2)}, u32[]{:S(2)}) %all-to-all-start.9) | async-done | bytes 131104 | tf_op jit(solution)/shard_map/all_to_all | solution.py:45
  357.9 7.7 %exponential_reduce_fusion.25 = (f32[8,256]{1,0:T(8,128)S(1)}, f32[8,256]{1,0:T(8,128)S(1)}, f32[8,256]{1,0:T(8,128)S(1)}, f32[8,256]{1,0:T(8,128)S(1)}, f32[8,2...) fusion(f32[8,256,256]{2,1,0:T(8,128)} %subtract_multiply_fusion, ...), kind=kLoop, calls=%fused_computation.68 | loop fusion | flops 17793024 | bytes 16998400 | tf_op jit(solution)/shard_map/reduce_sum | solution.py:22
  365.7 3.3 exponential_reduce_fusion.22
  369.2 4.7 %exponential_reduce_fusion.18 = (f32[8,256]{1,0:T(8,128)S(1)}, f32[8,256]{1,0:T(8,128)S(1)}, f32[8,256]{1,0:T(8,128)S(1)}, f32[8,256]{1,0:T(8,128)S(1)}, f32[8,2...) fusion(f32[8,256,256]{2,1,0:T(8,128)S(1)} %copy-done.9, ...), kind=kLoop, calls=%fused_computation.61 | loop fusion | flops 12566528 | bytes 8560640 | tf_op jit(solution)/shard_map/reduce_sum | solution.py:22
  375.6 2.3 exponential_reduce_fusion.15
  377.9 1.2 exponential_reduce_fusion.16
  381.1 2.3 exponential_reduce_fusion.12
  383.4 1.2 exponential_reduce_fusion.13
  386.5 4.3 %all-to-all-start.10 = ((f32[128,1,256]{2,1,0:T(1,128)}), f32[128,1,256]{2,1,0:T(1,128)S(1)}, u32[]{:S(2)}, u32[]{:S(2)}) async-start(f32[128,1,256]{2,1,0:T(1,128)} %copy.148), calls=%async_computation.10 | async-start | bytes 262144 | tf_op jit(solution)/shard_map/all_to_all | solution.py:208
  392.8 7.9 %all-to-all-done.10 = f32[128,1,256]{2,1,0:T(1,128)S(1)} async-done(((f32[128,1,256]{2,1,0:T(1,128)}), f32[128,1,256]{2,1,0:T(1,128)S(1)}, u32[]{:S(2)}, u32[]{:S(2)}) %all-to-all-start.10) | async-done | bytes 131104 | tf_op jit(solution)/shard_map/all_to_all | solution.py:208
  400.7 4.2 %all-to-all-start.11 = ((f32[128,1,256]{2,1,0:T(1,128)}), f32[128,1,256]{2,1,0:T(1,128)S(1)}, u32[]{:S(2)}, u32[]{:S(2)}) async-start(f32[128,1,256]{2,1,0:T(1,128)} %copy.149), calls=%async_computation.11 | async-start | bytes 262144 | tf_op jit(solution)/shard_map/all_to_all | solution.py:215
  405.8 9.2 %all-to-all-done.11 = f32[128,1,256]{2,1,0:T(1,128)S(1)} async-done(((f32[128,1,256]{2,1,0:T(1,128)}), f32[128,1,256]{2,1,0:T(1,128)S(1)}, u32[]{:S(2)}, u32[]{:S(2)}) %all-to-all-start.11) | async-done | bytes 131104 | tf_op jit(solution)/shard_map/all_to_all | solution.py:215
  (470 shorter events, 45.4 us)
Async XLA Ops:
  0.6 35.7 %copy-start.38 = (f32[64,2048]{1,0:T(8,128)S(1)}, f32[64,2048]{1,0:T(8,128)}, u32[]{:S(2)}) copy-start(f32[64,2048]{1,0:T(8,128)} %param.9) | copy-start | bytes 1572868
  0.6 35.7 %copy-start.41 = (f32[64,2048]{1,0:T(8,128)S(1)}, f32[64,2048]{1,0:T(8,128)}, u32[]{:S(2)}) copy-start(f32[64,2048]{1,0:T(8,128)} %param.10) | copy-start | bytes 1572868
  6.7 21.0 %all-to-all-start = ((s32[128,1,1]{2,1,0:T(1,128)}), s32[128,1,1]{2,1,0:T(1,128)S(1)}, u32[]{:S(2)}, u32[]{:S(2)}) async-start(s32[128,1,1]{2,1,0:T(1,128)} %copy.125), calls=%async_computation | async-start | bytes 131072 | tf_op jit(solution)/shard_map/all_to_all | solution.py:111
  31.7 14.6 %all-to-all-start.1 = ((f32[128,1,256]{2,1,0:T(1,128)}), f32[128,1,256]{2,1,0:T(1,128)S(1)}, u32[]{:S(2)}, u32[]{:S(2)}) async-start(f32[128,1,256]{2,1,0:T(1,128)} %copy.126), calls=%async_computation.1 | async-start | bytes 262144 | tf_op jit(solution)/shard_map/all_to_all | solution.py:36
  46.3 14.2 %all-to-all-start.2 = ((f32[128,1,256]{2,1,0:T(1,128)}), f32[128,1,256]{2,1,0:T(1,128)S(1)}, u32[]{:S(2)}, u32[]{:S(2)}) async-start(f32[128,1,256]{2,1,0:T(1,128)} %copy.130), calls=%async_computation.2 | async-start | bytes 262144 | tf_op jit(solution)/shard_map/all_to_all | solution.py:45
  60.5 104.6 %all-to-all-start.3 = ((f32[128,1,64,256]{3,2,1,0:T(8,128)}), f32[128,1,64,256]{3,2,1,0:T(8,128)}, u32[]{:S(2)}, u32[]{:S(2)}) async-start(f32[128,1,64,256]{3,2,1,0:T(8,128)} %bitcast.348), calls=%async_computation.3 | async-start | bytes 16777216 | tf_op jit(solution)/shard_map/all_to_all | solution.py:35
  66.8 98.4 %copy-start.85 = (s32[1024]{0:T(1024)}, s32[1024]{0:T(1024)S(1)}, u32[]{:S(2)}) copy-start(s32[1024]{0:T(1024)S(1)} %pad_clamp_fusion.1) | copy-start | bytes 12292
  77.0 88.1 %copy-start.82 = (s32[128]{0:T(128)}, s32[128]{0:T(128)S(1)}, u32[]{:S(2)}) copy-start(s32[128]{0:T(128)S(1)} %fusion.84) | copy-start | bytes 1540
  179.5 37.7 %copy-start.4 = (f32[8,256,256]{2,1,0:T(8,128)}, f32[8,256,256]{2,1,0:T(8,128)S(1)}, u32[]{:S(2)}) copy-start(f32[8,256,256]{2,1,0:T(8,128)S(1)} %fusion.7) | copy-start | bytes 6291460
  181.7 35.5 %copy-start.10 = (f32[8,256,256]{2,1,0:T(8,128)}, f32[8,256,256]{2,1,0:T(8,128)S(1)}, u32[]{:S(2)}) copy-start(f32[8,256,256]{2,1,0:T(8,128)S(1)} %fusion.8) | copy-start | bytes 6291460
  183.7 33.5 %copy-start.16 = (f32[8,256,256]{2,1,0:T(8,128)}, f32[8,256,256]{2,1,0:T(8,128)S(1)}, u32[]{:S(2)}) copy-start(f32[8,256,256]{2,1,0:T(8,128)S(1)} %fusion.9) | copy-start | bytes 6291460
  185.7 24.4 %copy-start.7 = (f32[8,256,256]{2,1,0:T(8,128)}, f32[8,256,256]{2,1,0:T(8,128)S(1)}, u32[]{:S(2)}) copy-start(f32[8,256,256]{2,1,0:T(8,128)S(1)} %fusion.4) | copy-start | bytes 6291460
  187.8 13.5 %copy-start.22 = (f32[8,256,256]{2,1,0:T(8,128)}, f32[8,256,256]{2,1,0:T(8,128)S(1)}, u32[]{:S(2)}) copy-start(f32[8,256,256]{2,1,0:T(8,128)S(1)} %fusion) | copy-start | bytes 6291460
  189.8 20.4 %copy-start.31 = (f32[8,256,256]{2,1,0:T(8,128)}, f32[8,256,256]{2,1,0:T(8,128)S(1)}, u32[]{:S(2)}) copy-start(f32[8,256,256]{2,1,0:T(8,128)S(1)} %fusion.2) | copy-start | bytes 6291460
  191.8 33.7 %copy-start.25 = (f32[8,256,256]{2,1,0:T(8,128)}, f32[8,256,256]{2,1,0:T(8,128)S(1)}, u32[]{:S(2)}) copy-start(f32[8,256,256]{2,1,0:T(8,128)S(1)} %fusion.1) | copy-start | bytes 6291460
  200.6 9.6 %copy-start.13 = (f32[8,256,256]{2,1,0:T(8,128)}, f32[8,256,256]{2,1,0:T(8,128)S(1)}, u32[]{:S(2)}) copy-start(f32[8,256,256]{2,1,0:T(8,128)S(1)} %get-tuple-element.369) | copy-start | bytes 6291460
  201.3 8.9 %copy-start.47 = (f32[8,256]{1,0:T(8,128)S(1)}, f32[8,256]{1,0:T(8,128)}, u32[]{:S(2)}) copy-start(f32[8,256]{1,0:T(8,128)} %get-tuple-element.285) | copy-start | bytes 24580
  201.3 8.9 %copy-start.51 = (f32[8,256]{1,0:T(8,128)S(1)}, f32[8,256]{1,0:T(8,128)}, u32[]{:S(2)}) copy-start(f32[8,256]{1,0:T(8,128)} %get-tuple-element.355) | copy-start | bytes 24580
  201.3 8.9 %copy-start.52 = (f32[8,256]{1,0:T(8,128)S(1)}, f32[8,256]{1,0:T(8,128)}, u32[]{:S(2)}) copy-start(f32[8,256]{1,0:T(8,128)} %get-tuple-element.162) | copy-start | bytes 24580
  201.4 8.9 %copy-start.67 = (f32[8,256]{1,0:T(8,128)S(1)}, f32[8,256]{1,0:T(8,128)}, u32[]{:S(2)}) copy-start(f32[8,256]{1,0:T(8,128)} %get-tuple-element.245) | copy-start | bytes 24580
  201.4 8.9 %copy-start.68 = (f32[8,256]{1,0:T(8,128)S(1)}, f32[8,256]{1,0:T(8,128)}, u32[]{:S(2)}) copy-start(f32[8,256]{1,0:T(8,128)} %get-tuple-element.246) | copy-start | bytes 24580
  201.4 8.9 %copy-start.70 = (f32[8,256]{1,0:T(8,128)S(1)}, f32[8,256]{1,0:T(8,128)}, u32[]{:S(2)}) copy-start(f32[8,256]{1,0:T(8,128)} %get-tuple-element.354) | copy-start | bytes 24580
  201.4 8.9 %copy-start.71 = (f32[8,256]{1,0:T(8,128)S(1)}, f32[8,256]{1,0:T(8,128)}, u32[]{:S(2)}) copy-start(f32[8,256]{1,0:T(8,128)} %get-tuple-element.163) | copy-start | bytes 24580
  201.4 8.9 %copy-start.86 = (f32[8,256]{1,0:T(8,128)S(1)}, f32[8,256]{1,0:T(8,128)}, u32[]{:S(2)}) copy-start(f32[8,256]{1,0:T(8,128)} %get-tuple-element.240) | copy-start | bytes 24580
  209.5 16.0 %copy-start.62 = (f32[8,256]{1,0:T(8,128)}, f32[8,256]{1,0:T(8,128)S(1)}, u32[]{:S(2)}) copy-start(f32[8,256]{1,0:T(8,128)S(1)} %get-tuple-element.192) | copy-start | bytes 24580
  224.0 17.3 %copy-start.105 = (f32[8,256]{1,0:T(8,128)S(1)}, f32[8,256]{1,0:T(8,128)}, u32[]{:S(2)}) copy-start(f32[8,256]{1,0:T(8,128)} %get-tuple-element.349) | copy-start | bytes 24580
  224.0 17.4 %copy-start.104 = (f32[8,256]{1,0:T(8,128)S(1)}, f32[8,256]{1,0:T(8,128)}, u32[]{:S(2)}) copy-start(f32[8,256]{1,0:T(8,128)} %get-tuple-element.347) | copy-start | bytes 24580
  224.1 17.4 %copy-start.103 = (f32[8,256]{1,0:T(8,128)S(1)}, f32[8,256]{1,0:T(8,128)}, u32[]{:S(2)}) copy-start(f32[8,256]{1,0:T(8,128)} %get-tuple-element.345) | copy-start | bytes 24580
  224.1 17.4 %copy-start.101 = (f32[8,256]{1,0:T(8,128)S(1)}, f32[8,256]{1,0:T(8,128)}, u32[]{:S(2)}) copy-start(f32[8,256]{1,0:T(8,128)} %get-tuple-element.343) | copy-start | bytes 24580
  224.1 17.4 %copy-start.102 = (f32[8,256]{1,0:T(8,128)S(1)}, f32[8,256]{1,0:T(8,128)}, u32[]{:S(2)}) copy-start(f32[8,256]{1,0:T(8,128)} %get-tuple-element.139) | copy-start | bytes 24580
  225.3 16.2 %copy-start.99 = (f32[8,256]{1,0:T(8,128)S(1)}, f32[8,256]{1,0:T(8,128)}, u32[]{:S(2)}) copy-start(f32[8,256]{1,0:T(8,128)} %get-tuple-element.341) | copy-start | bytes 24580
  225.3 16.2 %copy-start.97 = (f32[8,256]{1,0:T(8,128)S(1)}, f32[8,256]{1,0:T(8,128)}, u32[]{:S(2)}) copy-start(f32[8,256]{1,0:T(8,128)} %get-tuple-element.339) | copy-start | bytes 24580
  225.3 16.2 %copy-start.95 = (f32[8,256]{1,0:T(8,128)S(1)}, f32[8,256]{1,0:T(8,128)}, u32[]{:S(2)}) copy-start(f32[8,256]{1,0:T(8,128)} %get-tuple-element.171) | copy-start | bytes 24580
  225.3 16.2 %copy-start.93 = (f32[8,256]{1,0:T(8,128)S(1)}, f32[8,256]{1,0:T(8,128)}, u32[]{:S(2)}) copy-start(f32[8,256]{1,0:T(8,128)} %get-tuple-element.175) | copy-start | bytes 24580
  225.3 18.1 %copy-start.100 = (f32[8,256]{1,0:T(8,128)S(1)}, f32[8,256]{1,0:T(8,128)}, u32[]{:S(2)}) copy-start(f32[8,256]{1,0:T(8,128)} %get-tuple-element.350) | copy-start | bytes 24580
  225.3 18.0 %copy-start.98 = (f32[8,256]{1,0:T(8,128)S(1)}, f32[8,256]{1,0:T(8,128)}, u32[]{:S(2)}) copy-start(f32[8,256]{1,0:T(8,128)} %get-tuple-element.348) | copy-start | bytes 24580
  225.3 18.1 %copy-start.96 = (f32[8,256]{1,0:T(8,128)S(1)}, f32[8,256]{1,0:T(8,128)}, u32[]{:S(2)}) copy-start(f32[8,256]{1,0:T(8,128)} %get-tuple-element.346) | copy-start | bytes 24580
  225.4 18.1 %copy-start.92 = (f32[8,256]{1,0:T(8,128)S(1)}, f32[8,256]{1,0:T(8,128)}, u32[]{:S(2)}) copy-start(f32[8,256]{1,0:T(8,128)} %get-tuple-element.344) | copy-start | bytes 24580
  225.4 18.1 %copy-start.94 = (f32[8,256]{1,0:T(8,128)S(1)}, f32[8,256]{1,0:T(8,128)}, u32[]{:S(2)}) copy-start(f32[8,256]{1,0:T(8,128)} %get-tuple-element.138) | copy-start | bytes 24580
  225.4 18.1 %copy-start.91 = (f32[8,256]{1,0:T(8,128)S(1)}, f32[8,256]{1,0:T(8,128)}, u32[]{:S(2)}) copy-start(f32[8,256]{1,0:T(8,128)} %get-tuple-element.342) | copy-start | bytes 24580
  225.6 30.7 %copy-start.57 = (f32[8,256]{1,0:T(8,128)S(1)}, f32[8,256]{1,0:T(8,128)}, u32[]{:S(2)}) copy-start(f32[8,256]{1,0:T(8,128)} %get-tuple-element.365) | copy-start | bytes 24580
  225.6 30.7 %copy-start.77 = (f32[8,256]{1,0:T(8,128)S(1)}, f32[8,256]{1,0:T(8,128)}, u32[]{:S(2)}) copy-start(f32[8,256]{1,0:T(8,128)} %maximum_maximum_fusion.10) | copy-start | bytes 24580
  225.6 30.7 %copy-start.109 = (f32[8,256]{1,0:T(8,128)S(1)}, f32[8,256]{1,0:T(8,128)}, u32[]{:S(2)}) copy-start(f32[8,256]{1,0:T(8,128)} %get-tuple-element.184) | copy-start | bytes 24580
  225.6 30.8 %copy-start.61 = (f32[8,256]{1,0:T(8,128)S(1)}, f32[8,256]{1,0:T(8,128)}, u32[]{:S(2)}) copy-start(f32[8,256]{1,0:T(8,128)} %get-tuple-element.353) | copy-start | bytes 24580
  225.6 30.8 %copy-start.79 = (f32[8,256]{1,0:T(8,128)S(1)}, f32[8,256]{1,0:T(8,128)}, u32[]{:S(2)}) copy-start(f32[8,256]{1,0:T(8,128)} %copy-done.78) | copy-start | bytes 24580
  225.6 30.8 %copy-start.81 = (f32[8,256]{1,0:T(8,128)S(1)}, f32[8,256]{1,0:T(8,128)}, u32[]{:S(2)}) copy-start(f32[8,256]{1,0:T(8,128)} %copy-done.80) | copy-start | bytes 24580
  225.6 30.8 %copy-start.108 = (f32[8,256]{1,0:T(8,128)S(1)}, f32[8,256]{1,0:T(8,128)}, u32[]{:S(2)}) copy-start(f32[8,256]{1,0:T(8,128)} %get-tuple-element.190) | copy-start | bytes 24580
  225.6 30.8 %copy-start.110 = (f32[8,256]{1,0:T(8,128)S(1)}, f32[8,256]{1,0:T(8,128)}, u32[]{:S(2)}) copy-start(f32[8,256]{1,0:T(8,128)} %get-tuple-element.170) | copy-start | bytes 24580
  225.6 30.8 %copy-start.111 = (f32[8,256]{1,0:T(8,128)S(1)}, f32[8,256]{1,0:T(8,128)}, u32[]{:S(2)}) copy-start(f32[8,256]{1,0:T(8,128)} %get-tuple-element.340) | copy-start | bytes 24580
  225.7 30.8 %copy-start.106 = (f32[8,256]{1,0:T(8,128)S(1)}, f32[8,256]{1,0:T(8,128)}, u32[]{:S(2)}) copy-start(f32[8,256]{1,0:T(8,128)} %get-tuple-element.174) | copy-start | bytes 24580
  225.7 30.8 %copy-start.107 = (f32[8,256]{1,0:T(8,128)S(1)}, f32[8,256]{1,0:T(8,128)}, u32[]{:S(2)}) copy-start(f32[8,256]{1,0:T(8,128)} %get-tuple-element.191) | copy-start | bytes 24580
  225.7 39.9 %copy-start.83 = (s32[128]{0:T(128)S(1)}, s32[128]{0:T(128)}, u32[]{:S(2)}) copy-start(s32[128]{0:T(128)} %copy-done.82) | copy-start | bytes 1540
  226.9 29.6 %copy-start.63 = (f32[8,256]{1,0:T(8,128)S(1)}, f32[8,256]{1,0:T(8,128)}, u32[]{:S(2)}) copy-start(f32[8,256]{1,0:T(8,128)} %copy-done.62) | copy-start | bytes 24580
  228.7 22.6 %all-to-all-start.4 = ((f32[128,1,256]{2,1,0:T(1,128)}), f32[128,1,256]{2,1,0:T(1,128)S(1)}, u32[]{:S(2)}, u32[]{:S(2)}) async-start(f32[128,1,256]{2,1,0:T(1,128)} %reshape.1227), calls=%async_computation.4 | async-start | bytes 262144 | tf_op jit(solution)/shard_map/all_to_all | solution.py:208
  251.4 14.2 %all-to-all-start.5 = ((f32[128,1,256]{2,1,0:T(1,128)}), f32[128,1,256]{2,1,0:T(1,128)S(1)}, u32[]{:S(2)}, u32[]{:S(2)}) async-start(f32[128,1,256]{2,1,0:T(1,128)} %reshape.1228), calls=%async_computation.5 | async-start | bytes 262144 | tf_op jit(solution)/shard_map/all_to_all | solution.py:215
  267.7 14.7 %all-to-all-start.6 = ((f32[128,1,256]{2,1,0:T(1,128)}), f32[128,1,256]{2,1,0:T(1,128)S(1)}, u32[]{:S(2)}, u32[]{:S(2)}) async-start(f32[128,1,256]{2,1,0:T(1,128)} %copy.144), calls=%async_computation.6 | async-start | bytes 262144 | tf_op jit(solution)/shard_map/all_to_all | solution.py:45
  283.3 11.3 %copy-start.29 = (f32[8,256,256]{2,1,0:T(8,128)S(1)}, f32[8,256,256]{2,1,0:T(8,128)}, u32[]{:S(2)}) copy-start(f32[8,256,256]{2,1,0:T(8,128)} %copy-done.28) | copy-start | bytes 6291460
  311.9 14.3 %all-to-all-start.7 = ((f32[128,1,256]{2,1,0:T(1,128)}), f32[128,1,256]{2,1,0:T(1,128)S(1)}, u32[]{:S(2)}, u32[]{:S(2)}) async-start(f32[128,1,256]{2,1,0:T(1,128)} %copy.145), calls=%async_computation.7 | async-start | bytes 262144 | tf_op jit(solution)/shard_map/all_to_all | solution.py:208
  326.2 14.2 %all-to-all-start.8 = ((f32[128,1,256]{2,1,0:T(1,128)}), f32[128,1,256]{2,1,0:T(1,128)S(1)}, u32[]{:S(2)}, u32[]{:S(2)}) async-start(f32[128,1,256]{2,1,0:T(1,128)} %copy.146), calls=%async_computation.8 | async-start | bytes 262144 | tf_op jit(solution)/shard_map/all_to_all | solution.py:215
  342.5 14.4 %all-to-all-start.9 = ((f32[128,1,256]{2,1,0:T(1,128)}), f32[128,1,256]{2,1,0:T(1,128)S(1)}, u32[]{:S(2)}, u32[]{:S(2)}) async-start(f32[128,1,256]{2,1,0:T(1,128)} %copy.147), calls=%async_computation.9 | async-start | bytes 262144 | tf_op jit(solution)/shard_map/all_to_all | solution.py:45
  357.9 11.3 %copy-start.30 = (f32[8,256,256]{2,1,0:T(8,128)S(1)}, f32[8,256,256]{2,1,0:T(8,128)}, u32[]{:S(2)}) copy-start(f32[8,256,256]{2,1,0:T(8,128)} %copy-done.28) | copy-start | bytes 6291460
  384.6 30.8 %copy-start.84 = (pred[16,256]{1,0:T(8,128)(4,1)S(1)}, pred[16,256]{1,0:T(8,128)(4,1)}, u32[]{:S(2)}) copy-start(pred[16,256]{1,0:T(8,128)(4,1)} %iota_compare_fusion.1) | copy-start | bytes 12292
  386.5 14.3 %all-to-all-start.10 = ((f32[128,1,256]{2,1,0:T(1,128)}), f32[128,1,256]{2,1,0:T(1,128)S(1)}, u32[]{:S(2)}, u32[]{:S(2)}) async-start(f32[128,1,256]{2,1,0:T(1,128)} %copy.148), calls=%async_computation.10 | async-start | bytes 262144 | tf_op jit(solution)/shard_map/all_to_all | solution.py:208
  400.7 14.2 %all-to-all-start.11 = ((f32[128,1,256]{2,1,0:T(1,128)}), f32[128,1,256]{2,1,0:T(1,128)S(1)}, u32[]{:S(2)}, u32[]{:S(2)}) async-start(f32[128,1,256]{2,1,0:T(1,128)} %copy.149), calls=%async_computation.11 | async-start | bytes 262144 | tf_op jit(solution)/shard_map/all_to_all | solution.py:215
  (62 other events, 317.5 us)
where the time goes:
time: 424 us; the launch traced here: 418 us
  waiting for transfers between devices  173 us (41%)
  other arithmetic  68.8 us (16%)
  starting transfers between devices  68.8 us (16%)
  matrix products  54.7 us (13%)
  local copies, waits for them, and re-layouts  49 us (12%)
    all_to_all x1, waiting for transfers between devices, move_blocks(): lax.all_to_all(reply_coords, ('row', 'col'), split_axis=0, concat_axis=0,...  86 us
    dot_general x14, matrix products, tile_terms(): jnp.einsum('ndi,ndj->nij', row_coords, col_coords, precision=HIGHEST)  53.4 us
    reduce_sum x16, other arithmetic, tile_terms(): row_total = jnp.sum(jnp.exp(row_score - row_peak[:, :, None]), axis=2)  47.9 us
    all_to_all x3, waiting for transfers between devices, local(): lax.all_to_all(send_total.reshape(devices, capacity, members), ('row', 'c...  27.5 us
    all_to_all x3, waiting for transfers between devices, local(): lax.all_to_all(send_peak.reshape(devices, capacity, members), ('row', 'co...  22.9 us
    all_to_all x3, starting transfers between devices, local(): lax.all_to_all(send_peak.reshape(devices, capacity, members), ('row', 'co...  21.2 us
    all_to_all x3, waiting for transfers between devices, move_potentials(): lax.all_to_all(reply_potential, ('row', 'col'), split_axis=0, concat_axis...  20.8 us
    all_to_all x3, starting transfers between devices, move_potentials(): lax.all_to_all(reply_potential, ('row', 'col'), split_axis=0, concat_axis...  13.5 us
  transfers between devices with their start and end apart: 12, of which 12 were waited for; matrix products, arithmetic and copies ran while one was open for 8% of the time, Pallas kernels for 0%

commit v1 on v0

v1 whole, which is shorter than its diff:
```python
import functools

import jax
import jax.numpy as jnp
from jax import lax
from jax.experimental import pallas as pl
from jax.experimental.pallas import tpu as pltpu
from jax.sharding import PartitionSpec as P

ITERS = 3
EPSILON = 0.5
DAMPING = 2.0 / (2.0 + 0.5)
NEGATIVE = -1e30
REAL = -1e29
LOG2E = 1.4426950408889634
LN2 = 0.6931471805599453
TINY = 2.0**-90
HUGE = 2.0**90
AXES = ("row", "col")

D = 64
CS = 256
CL = 8
HALF = 128
ROWS = 2 * D + 8
GROUP = 2
BF16 = jnp.bfloat16
F32 = jnp.float32


def lists(cross, xself, yself):
    for table, kind in ((cross, 0), (xself, 1), (yself, 2)):
        for c in range(table.shape[0]):
            for k in range(table.shape[1]):
                yield kind, c, k, table[c, k]


def bias_of(weight, half, potential):
    return LOG2E * (weight + (potential - half) / EPSILON)


def push_kernel(
    cross, xself, yself, x_sizes, y_sizes, x_ref, y_ref, x_mass, y_mass,
    send, weight_ref, half_ref, bias_ref, aux, sems,
):
    devices = send.shape[0]
    requests = list(lists(cross, xself, yself))
    for kind, c, _, named in requests:
        owner = named // CL
        source = y_ref if kind == 2 else x_ref
        for h in range(2):
            pltpu.make_async_copy(
                source.at[:, pl.ds(c * CS + h * HALF, HALF)],
                send.at[owner, pl.ds(h * D, D), :],
                sems.at[0],
            ).start()
    row = lax.broadcasted_iota(jnp.int32, (2 * CL, HALF), 0)
    position = (row % 2) * HALF + lax.broadcasted_iota(jnp.int32, (2 * CL, HALF), 1)
    for side, (points, sizes, mass) in enumerate(
        ((x_ref, x_sizes, x_mass), (y_ref, y_sizes, y_mass))
    ):
        count = jnp.zeros((2 * CL, HALF), jnp.int32)
        for c in range(CL):
            count = jnp.where(row // 2 == c, sizes[0, c], count)
        base = side * 2 * CL
        weight_ref[base : base + 2 * CL, :] = jnp.where(position < count, mass[...], NEGATIVE)
        for t in range(2 * CL):
            piece = points[:, t * HALF : (t + 1) * HALF]
            half_ref[base + t : base + t + 1, :] = 0.5 * jnp.sum(piece * piece, axis=0, keepdims=True)
    bias = bias_of(weight_ref[...], half_ref[...], 0.0)
    bias_ref[0 : 4 * CL, :] = bias
    bias_ref[4 * CL : 8 * CL, :] = bias
    aux[...] = jnp.zeros_like(aux)
    for kind, c, _, named in requests:
        owner = named // CL
        base = (2 * CL if kind == 2 else 0) + 2 * c
        aux[owner, 0:2, :] = bias_ref[base : base + 2, :]
        code = (kind * CL + named % CL + 1).astype(F32)
        aux[owner, 2:3, :] = jnp.full((1, HALF), code, F32)
    tail = pltpu.make_async_copy(aux, send.at[:, pl.ds(2 * D, 8), :], sems.at[1])
    tail.start()
    tail.wait()
    sent = send.at[pl.ds(0, len(requests)), pl.ds(0, 2 * D), :]
    pltpu.make_async_copy(sent, sent, sems.at[0]).wait()


def push(cross, xself, yself, x_sizes, y_sizes, x, y, x_mass, y_mass, devices):
    smem = pl.BlockSpec(memory_space=pltpu.SMEM)
    vmem = pl.BlockSpec(memory_space=pltpu.VMEM)
    return pl.pallas_call(
        push_kernel,
        out_shape=(
            jax.ShapeDtypeStruct((devices, ROWS, HALF), F32),
            jax.ShapeDtypeStruct((4 * CL, HALF), F32),
            jax.ShapeDtypeStruct((4 * CL, HALF), F32),
            jax.ShapeDtypeStruct((8 * CL, HALF), F32),
        ),
        in_specs=[smem] * 5 + [vmem] * 4,
        out_specs=(pl.BlockSpec(memory_space=pl.ANY), vmem, vmem, vmem),
        scratch_shapes=[
            pltpu.VMEM((devices, 8, HALF), F32),
            pltpu.SemaphoreType.DMA((2,)),
        ],
        name="push",
    )(cross, xself, yself, x_sizes, y_sizes, x, y, x_mass, y_mass)


def split2(value):
    high = value.astype(BF16)
    return high, (value - high.astype(F32)).astype(BF16)


def split3(value):
    high = value.astype(BF16).astype(F32)
    rest = value - high
    middle = rest.astype(BF16).astype(F32)
    return high, middle, rest - middle


def left_kernel(x_ref, y_ref, left_ref):
    for side, points in enumerate((x_ref, y_ref)):
        for c in range(CL):
            scaled = points[:, c * CS : (c + 1) * CS] * (LOG2E / EPSILON)
            turned = jnp.transpose(jnp.concatenate([scaled, scaled], axis=0))
            high = turned.astype(BF16).astype(F32)
            low = turned - high
            left_ref[side * CL + c, :, 0:HALF] = high.astype(BF16)
            lane = lax.broadcasted_iota(jnp.int32, (CS, HALF), 1)
            left_ref[side * CL + c, :, HALF:CS] = jnp.where(lane < D, low, 0.0).astype(BF16)


def left_side(x, y):
    vmem = pl.BlockSpec(memory_space=pltpu.VMEM)
    return pl.pallas_call(
        left_kernel,
        out_shape=jax.ShapeDtypeStruct((2 * CL, CS, CS), BF16),
        in_specs=[vmem, vmem],
        out_specs=vmem,
        name="left_side",
    )(x, y)


def tile_kernel(first, *refs):
    if first:
        (codes, moved, x_ref, y_ref, left, bias, back, log_cols, log_own,
         held, left2, acc, top, sums, own, count, slots, targets, rows, state, sems) = refs
        message = None
    else:
        (codes, moved, message, x_ref, y_ref, left, bias, back, log_cols, log_own,
         held, left2, acc, top, sums, own, count, slots, targets, rows, state, sems) = refs
    devices = moved.shape[0]
    pieces = sems.shape[0]
    step = devices // pieces

    def fetch(i):
        part = pl.ds(i * step, step)
        return pltpu.make_async_copy(moved.at[part], held.at[part], sems.at[i])

    for i in range(pieces):
        fetch(i).start()

    row8 = lax.broadcasted_iota(jnp.int32, (8, HALF), 0)
    ones = jnp.where(row8 < 3, 1.0, 0.0)
    for t in range(3):
        for h in range(2):
            high, middle, low = split3(bias[pl.ds((t + 1) * 2 * CL + h, CL, stride=2), :])
            stack = jnp.concatenate(
                [jnp.zeros((D, HALF), F32), high, middle, low, ones, jnp.zeros((32, HALF), F32)], axis=0
            )
            turned = jnp.transpose(stack).astype(BF16)
            for e in range(CL):
                cluster = e if t == 1 else CL + e
                here = pl.ds(h * HALF, HALF)
                left2[t * CL + e, here, :] = left[cluster, here, pl.ds(HALF, HALF)] + turned

    def clear(te, _):
        count[te] = 1
        return 0

    lax.fori_loop(0, 3 * CL, clear, 0)

    def gather(s, n):
        code = codes[s]

        @pl.when(code > 0)
        def _():
            slots[n] = s
            targets[n] = code - 1
            rows[n] = 2 * s

        return n + (code > 0).astype(jnp.int32)

    live = lax.fori_loop(0, devices, gather, 0)
    for i in range(GROUP - 1):
        slots[live + i] = slots[0]
        targets[live + i] = 0
        rows[live + i] = 2 * devices

    def scores(coords, a, te, e, cluster):
        high, low = split2(coords)
        a1, a2, a3 = split3(a)
        row = lax.broadcasted_iota(jnp.int32, (8, CS), 0)
        pick = jnp.where(row == e, 1.0, 0.0)
        mine = jnp.where(row == 0, a1, jnp.where(row == 1, a2, jnp.where(row == 2, a3, 0.0)))
        tail = jnp.concatenate([pick, pick, pick, mine], axis=0).astype(BF16)
        right = jnp.concatenate([high, low, high, tail, jnp.zeros((32, CS), BF16)], axis=0)
        return jnp.dot(
            jnp.concatenate([left[cluster, :, 0:HALF], left2[te]], axis=1),
            right,
            preferred_element_type=F32,
        )

    def fast(z, a, te, out, at):
        value = jnp.exp2(z)
        row_sum = jnp.where(a > REAL, jnp.sum(value, axis=0, keepdims=True), 1.0)
        out[pl.ds(at, 1), :] = row_sum[:, 0:HALF]
        out[pl.ds(at + 1, 1), :] = row_sum[:, HALF:CS]
        acc[te] = acc[te] + (value[:, 0:HALF] + value[:, HALF:CS])

    def slow(z, a, te, out, at):
        peak = jnp.max(z, axis=0, keepdims=True)
        total = jnp.sum(jnp.exp2(z - peak), axis=0, keepdims=True)
        log_sum = peak + jnp.log(total) * LOG2E
        out[pl.ds(at, 1), :] = log_sum[:, 0:HALF]
        out[pl.ds(at + 1, 1), :] = log_sum[:, HALF:CS]
        peak = jnp.max(z, axis=1, keepdims=True)
        total = jnp.sum(jnp.exp2(z - peak), axis=1, keepdims=True)
        before = top[te]
        now = jnp.maximum(before, peak)
        acc[te] = acc[te] * jnp.exp2(before - now) + total * jnp.exp2(peak - now)
        top[te] = now

    def sweep_local(finish):
        for t in range(3):
            points = y_ref if t == 2 else x_ref
            base = (0, 2, 3)[t] * 2 * CL

            def one(e, _):
                at = base + 2 * e
                a = jnp.concatenate([bias[pl.ds(at, 1), :], bias[pl.ds(at + 1, 1), :]], axis=1)
                z = scores(
                    points[:, pl.ds(pl.multiple_of(e * CS, CS), CS)], a, t * CL + e, e,
                    e if t == 1 else CL + e,
                )
                finish(z, a, t * CL + e, own, t * 2 * CL + 2 * e)
                return 0

            lax.fori_loop(0, CL, one, 0)

    def sweep_moved(finish):
        def some(i, _):
            for j in range(GROUP):
                n = i * GROUP + j
                s, te, at = slots[n], targets[n], rows[n]
                e = te % CL
                cluster = jnp.where(te // CL == 1, e, CL + e)
                coords = jnp.concatenate([held[s, 0:D, :], held[s, D : 2 * D, :]], axis=1)
                if first:
                    a = jnp.concatenate(
                        [held[s, 2 * D : 2 * D + 1, :], held[s, 2 * D + 1 : 2 * D + 2, :]], axis=1
                    )
                else:
                    a = jnp.concatenate(
                        [message[pl.ds(2 * s, 1), :], message[pl.ds(2 * s + 1, 1), :]], axis=1
                    )
                a = jnp.where(at < 2 * devices, a, LOG2E * NEGATIVE)
                finish(scores(coords, a, te, e, cluster), a, te, sums, at)
            return 0

        lax.fori_loop(0, pl.cdiv(live, GROUP), some, 0)

    def columns(log_domain):
        lane = lax.broadcasted_iota(jnp.int32, (CS, HALF), 1)

        def one(te, packed):
            if log_domain:
                value = jnp.max(top[te] + jnp.log(acc[te]) * LOG2E, axis=1, keepdims=True)
            else:
                value = jnp.sum(acc[te], axis=1, keepdims=True)
            return jnp.where(lane == te, value, packed)

        packed = lax.fori_loop(0, 3 * CL, one, jnp.zeros((CS, HALF), F32))
        for h in range(2):
            turned = jnp.transpose(packed[h * HALF : (h + 1) * HALF, :])
            for t in range(3):
                log_cols[pl.ds(t * 2 * CL + h, CL, stride=2), :] = turned[t * CL : (t + 1) * CL, :]

    acc[...] = jnp.zeros_like(acc)
    sums[...] = jnp.ones_like(sums)
    sweep_local(fast)
    for i in range(pieces):
        fetch(i).wait()
    sweep_moved(fast)
    columns(False)
    col = log_cols[...]
    real = bias[2 * CL : 8 * CL, :] > REAL
    col_ok = jnp.where(real, col, 1.0)
    lowest = jnp.minimum(jnp.min(sums[...]), jnp.minimum(jnp.min(own[...]), jnp.min(col_ok)))
    highest = jnp.maximum(jnp.max(sums[...]), jnp.maximum(jnp.max(own[...]), jnp.max(col_ok)))
    within = jnp.logical_and(lowest > TINY, highest < HUGE)

    @pl.when(within)
    def _():
        back[...] = jnp.log(sums[0 : 2 * devices, :]) * LOG2E
        log_own[...] = jnp.log(own[0 : 2 * CL, :]) * LOG2E
        log_cols[...] = jnp.log(col_ok) * LOG2E

    @pl.when(jnp.logical_not(within))
    def _():
        acc[...] = jnp.zeros_like(acc)
        top[...] = jnp.full_like(top, 3.0 * NEGATIVE)
        sweep_local(slow)
        sweep_moved(slow)
        columns(True)
        back[...] = sums[0 : 2 * devices, :]
        log_own[...] = own[0 : 2 * CL, :]


def tiles(codes, moved, message, x, y, left, bias):
    first = message is None
    devices = moved.shape[0]
    smem = pl.BlockSpec(memory_space=pltpu.SMEM)
    vmem = pl.BlockSpec(memory_space=pltpu.VMEM)
    hbm = pl.BlockSpec(memory_space=pl.ANY)
    args = (codes, moved) + (() if first else (message,)) + (x, y, left, bias)
    return pl.pallas_call(
        functools.partial(tile_kernel, first),
        out_shape=(
            jax.ShapeDtypeStruct((2 * devices, HALF), F32),
            jax.ShapeDtypeStruct((6 * CL, HALF), F32),
            jax.ShapeDtypeStruct((2 * CL, HALF), F32),
        ),
        in_specs=[smem, hbm] + [vmem] * (4 if first else 5),
        out_specs=(vmem, vmem, vmem),
        scratch_shapes=[
            pltpu.VMEM((devices, ROWS, HALF), F32),
            pltpu.VMEM((3 * CL, CS, HALF), BF16),
            pltpu.VMEM((3 * CL, CS, HALF), F32),
            pltpu.VMEM((3 * CL, CS, HALF), F32),
            pltpu.VMEM((2 * devices + 8, HALF), F32),
            pltpu.VMEM((6 * CL, HALF), F32),
            pltpu.SMEM((3 * CL,), jnp.int32),
            pltpu.SMEM((devices + GROUP,), jnp.int32),
            pltpu.SMEM((devices + GROUP,), jnp.int32),
            pltpu.SMEM((devices + GROUP,), jnp.int32),
            pltpu.SMEM((1,), jnp.int32),
            pltpu.SemaphoreType.DMA((16,)),
        ],
        name="tiles_first" if first else "tiles",
    )(*args)


def log_sum(values):
    peak = functools.reduce(jnp.maximum, values)
    total = functools.reduce(jnp.add, [jnp.exp2(value - peak) for value in values])
    return peak + jnp.log(total) * LOG2E


def update_kernel(
    last, cross, xself, yself, back, log_cols, log_own, weight, half, potential, bias, *refs
):
    if last:
        new, parts = refs
    else:
        new, new_bias, message, parts = refs
    counts = (cross.shape[1], xself.shape[1], yself.shape[1])
    offsets = (0, counts[0], counts[0] + counts[1])
    requests = list(lists(cross, xself, yself))
    for kind, c, k, named in requests:
        at = pl.multiple_of(2 * (named // CL), 2)
        parts[offsets[kind] + k, 2 * c : 2 * c + 2, :] = back[pl.ds(at, 2), :]
    span = 2 * CL
    answers = [[parts[offsets[t] + k] for k in range(counts[t])] for t in range(3)]
    totals = (
        log_sum([log_own[...]] + answers[0]),
        log_cols[0:span, :],
        log_sum([log_cols[span : 2 * span, :]] + answers[1]),
        log_sum([log_cols[2 * span : 3 * span, :]] + answers[2]),
    )
    for i, total in enumerate(totals):
        here = slice(i * span, (i + 1) * span)
        side = slice((i % 2) * span, (i % 2 + 1) * span)
        log_total = LN2 * (total - bias[here, :]) - half[side, :] / EPSILON
        fresh = 0.5 * (potential[here, :] - DAMPING * EPSILON * log_total)
        fresh = jnp.where(weight[side, :] > REAL, fresh, 0.0)
        new[here, :] = fresh
        if not last:
            new_bias[here, :] = bias_of(weight[side, :], half[side, :], fresh)
    if last:
        return
    for kind, c, _, named in requests:
        at = pl.multiple_of(2 * (named // CL), 2)
        base = (0, 2 * span, 3 * span)[kind] + 2 * c
        message[pl.ds(at, 2), :] = new_bias[base : base + 2, :]


def update(last, cross, xself, yself, back, log_cols, log_own, weight, half, potential, bias):
    smem = pl.BlockSpec(memory_space=pltpu.SMEM)
    vmem = pl.BlockSpec(memory_space=pltpu.VMEM)
    small = jax.ShapeDtypeStruct((8 * CL, HALF), F32)
    shapes = (small,) if last else (small, small, jax.ShapeDtypeStruct(back.shape, F32))
    listed = cross.shape[1] + xself.shape[1] + yself.shape[1]
    return pl.pallas_call(
        functools.partial(update_kernel, last),
        out_shape=shapes,
        in_specs=[smem] * 3 + [vmem] * 7,
        out_specs=(vmem,) * len(shapes),
        scratch_shapes=[pltpu.VMEM((listed, 2 * CL, HALF), F32)],
        name="update",
    )(cross, xself, yself, back, log_cols, log_own, weight, half, potential, bias)


def exchange(blocks):
    return lax.all_to_all(blocks, AXES, split_axis=0, concat_axis=0, tiled=True)


def exchange_rows(rows, devices):
    return exchange(rows.reshape(devices, 2, HALF)).reshape(2 * devices, HALF)


def local(x, y, x_logmass, y_logmass, x_sizes, y_sizes, cross, xself, yself):
    devices = lax.axis_size(AXES)
    send, weight, half, bias = push(
        cross, xself, yself, x_sizes, y_sizes, x, y,
        x_logmass.reshape(2 * CL, HALF), y_logmass.reshape(2 * CL, HALF), devices,
    )
    moved = exchange(send)
    left = left_side(x, y)
    codes = moved[:, 2 * D + 2, 0].astype(jnp.int32)
    potential = jnp.zeros((8 * CL, HALF), F32)
    message = None
    for iteration in range(ITERS):
        last = iteration == ITERS - 1
        back, log_cols, log_own = tiles(codes, moved, message, x, y, left, bias)
        back = exchange_rows(back, devices)
        out = update(last, cross, xself, yself, back, log_cols, log_own, weight, half, potential, bias)
        if last:
            (potential,) = out
        else:
            potential, bias, message = out
            message = exchange_rows(message, devices)
    parts = potential.reshape(4, 2 * CL * HALF)
    return parts[0], parts[1], parts[2], parts[3]


def solution(mesh):
    flat, table = P(AXES), P(AXES, None)
    points = P(None, AXES)
    return jax.shard_map(
        local,
        mesh=mesh,
        in_specs=(points, points, flat, flat, table, table, table, table, table),
        out_specs=(flat, flat, flat, flat),
        check_vma=False,
    )
```

time: 424 us -> 409 us (0.965); the launches traced: 418 us -> 408 us
  Pallas kernels: 0 us -> 191 us
  blocking collectives: 0 us -> 93.7 us
  waiting for transfers between devices: 173 us -> 102 us
  other arithmetic: 68.8 us -> 3.91 us
  starting transfers between devices: 68.8 us -> 11.9 us
  matrix products: 54.7 us -> 0 us
  local copies, waits for them, and re-layouts: 49 us -> 4.67 us
    pallas_call x0 -> x8, Pallas kernels: none -> 191 us  [the longest x3 177 us: tiles(): pl.pallas_call(functools.partial(tile_kernel, first), out_shape=(jax.Shap...]
    all_to_all x0 -> x5, blocking collectives: none -> 93.7 us  [exchange(): return lax.all_to_all(blocks, AXES, split_axis=0, concat_axis=0, tiled=True)]
    all_to_all x12 -> x1, waiting for transfers between devices: 173 us -> 102 us  [exchange(): return lax.all_to_all(blocks, AXES, split_axis=0, concat_axis=0, tiled=True)]
    all_to_all x12 -> x1, starting transfers between devices: 68.8 us -> 11.9 us  [exchange(): return lax.all_to_all(blocks, AXES, split_axis=0, concat_axis=0, tiled=True)]
    dot_general x20 -> x0, matrix products: 54.7 us -> none  [the longest x14 53.4 us: tile_terms(): jnp.einsum('ndi,ndj->nij', row_coords, col_coords, precision=HIGHEST)]
    reduce_sum x28 -> x0, other arithmetic: 53 us -> none  [the longest x16 47.9 us: tile_terms(): row_total = jnp.sum(jnp.exp(row_score - row_peak[:, :, None]), axis=2)]
    gather x10 -> x0, local copies, waits for them, and re-layouts: 17.4 us -> none  [the longest x1 6.85 us: local(): fetched_coords[order_slots]]
    reduce_max x18 -> x0, other arithmetic: 10.8 us -> none  [the longest x2 4.45 us: tile_terms(): row_peak = jnp.max(row_score, axis=2)]
  transfers between devices with their start and end apart: 12 -> 1, of which waited for: 12 -> 1; matrix products, arithmetic and copies ran while one was open for 8% -> 0% of each run, Pallas kernels for 0% -> 1%
where the time goes in v1:
time: 409 us; the launch traced here: 408 us
  Pallas kernels  191 us (47%)
  waiting for transfers between devices  102 us (25%)
  blocking collectives  93.7 us (23%)
  starting transfers between devices  11.9 us (3%)
  local copies, waits for them, and re-layouts  4.67 us (1%)
    pallas_call x3, Pallas kernels, tiles(): pl.pallas_call(functools.partial(tile_kernel, first), out_shape=(jax.Shap...  177 us
    all_to_all x1, waiting for transfers between devices, exchange(): return lax.all_to_all(blocks, AXES, split_axis=0, concat_axis=0, tiled=True)  102 us
    all_to_all x5, blocking collectives, exchange(): return lax.all_to_all(blocks, AXES, split_axis=0, concat_axis=0, tiled=True)  93.7 us
    all_to_all x1, starting transfers between devices, exchange(): return lax.all_to_all(blocks, AXES, split_axis=0, concat_axis=0, tiled=True)  11.9 us
  transfers between devices with their start and end apart: 1, of which 1 were waited for; matrix products, arithmetic and copies ran while one was open for 0% of the time, Pallas kernels for 1%

profile of v1, /device:TPU:1, one launch (start us, length us, event | category | flops | bytes accessed | tf_op | source)
XLA Modules:
  0.0 408.3 jit_solution(1332204058166651745)
XLA Ops:
  0.6 1.3 copy.27.xself
  2.0 1.3 copy.28.yself
  3.3 4.5 %push.1 = (f32[128,136,128]{2,1,0:T(8,128)}, f32[32,128]{1,0:T(8,128)}, f32[32,128]{1,0:T(8,128)}, f32[64,128]{1,0:T(8,128)}) custom-call(s32[8,7]{1,0:T(8,128)} %cross.7, s32[8,2]{1,0:T(8,128)} %copy.27.xself, s32[8,2]{1,0:T(8,128)} %copy.28.yself, s32[1,8]{1,0:T(1,128)} %x_sizes.1, s32[1,8]{1,0:T(1,128)} %y_sizes.1, f32[64,2048]{1,0:T(8,128)} %refs_3_.5, ...), custom_call_target="tpu_custom_call" | custom-call | tf_op jit(solution)/shard_map/push/pallas_call | solution.py:90
  7.8 11.9 %all-to-all-start = ((f32[128,136,128]{2,1,0:T(8,128)}), f32[128,136,128]{2,1,0:T(8,128)}, u32[]{:S(2)}, u32[]{:S(2)}) async-start(f32[128,136,128]{2,1,0:T(8,128)} %get-tuple-element.23), calls=%async_computation | async-start | bytes 17825792 | tf_op jit(solution)/shard_map/all_to_all | solution.py:414
  19.7 3.2 left_side.1.refs_4_.refs_5_
  22.9 102.2 %all-to-all-done.refs_1_ = f32[128,136,128]{2,1,0:T(8,128)} async-done(((f32[128,136,128]{2,1,0:T(8,128)}), f32[128,136,128]{2,1,0:T(8,128)}, u32[]{:S(2)}, u32[]{:S(2)}) %all-to-all-start) | async-done | bytes 8912928 | tf_op jit(solution)/shard_map/all_to_all | solution.py:414
  125.1 3.9 fusion.refs_0_
  129.0 59.0 %tiles_first.1 = (f32[256,128]{1,0:T(8,128)}, f32[48,128]{1,0:T(8,128)}, f32[16,128]{1,0:T(8,128)}) custom-call(s32[128]{0:T(128)} %fusion.refs_0_, f32[128,136,128]{2,1,0:T(8,128)} %all-to-all-done.refs_1_, f32[64,2048]{1,0:T(8,128)} %refs_3_.5, f32[64,2048]{1,0:T(8,128)} %refs_4_.3, bf16[16,256,256]{2,1,0:T(8,128)(2,1)} %left_side.1.refs_4_.refs_5_, ...), custom_call_target="tpu_custom_call" | custom-call | tf_op jit(solution)/shard_map/tiles_first/pallas_call | solution.py:326
  188.0 27.4 %all_to_all.30 = f32[128,2,128]{2,1,0:T(2,128)} all-to-all(f32[128,2,128]{2,1,0:T(2,128)} %bitcast.29), channel_id=1, replica_groups=mesh['row'=16,'col'=8] {'row','col'}, dimensions={0} | all-to-all | bytes 262144 | tf_op jit(solution)/shard_map/all_to_all | solution.py:414
  215.4 0.6 broadcast_in_dim.3.potential
  216.0 2.3 update.3
  218.3 15.2 %all_to_all.31 = f32[128,2,128]{2,1,0:T(2,128)} all-to-all(f32[128,2,128]{2,1,0:T(2,128)} %bitcast.25), channel_id=1, replica_groups=mesh['row'=16,'col'=8] {'row','col'}, dimensions={0} | all-to-all | bytes 262144 | tf_op jit(solution)/shard_map/all_to_all | solution.py:414
  233.4 59.0 %tiles.2 = (f32[256,128]{1,0:T(8,128)}, f32[48,128]{1,0:T(8,128)}, f32[16,128]{1,0:T(8,128)}) custom-call(s32[128]{0:T(128)} %fusion.refs_0_, f32[128,136,128]{2,1,0:T(8,128)} %all-to-all-done.refs_1_, f32[256,128]{1,0:T(8,128)} %bitcast.21, f32[64,2048]{1,0:T(8,128)} %refs_3_.5, f32[64,2048]{1,0:T(8,128)} %refs_4_.3, ...), custom_call_target="tpu_custom_call" | custom-call | tf_op jit(solution)/shard_map/tiles/pallas_call | solution.py:326
  292.4 18.0 %all_to_all.32 = f32[128,2,128]{2,1,0:T(2,128)} all-to-all(f32[128,2,128]{2,1,0:T(2,128)} %bitcast.28), channel_id=1, replica_groups=mesh['row'=16,'col'=8] {'row','col'}, dimensions={0} | all-to-all | bytes 262144 | tf_op jit(solution)/shard_map/all_to_all | solution.py:414
  310.4 2.2 update.4
  312.7 15.2 %all_to_all.33 = f32[128,2,128]{2,1,0:T(2,128)} all-to-all(f32[128,2,128]{2,1,0:T(2,128)} %bitcast.26), channel_id=1, replica_groups=mesh['row'=16,'col'=8] {'row','col'}, dimensions={0} | all-to-all | bytes 262144 | tf_op jit(solution)/shard_map/all_to_all | solution.py:414
  327.8 59.0 %tiles.3 = (f32[256,128]{1,0:T(8,128)}, f32[48,128]{1,0:T(8,128)}, f32[16,128]{1,0:T(8,128)}) custom-call(s32[128]{0:T(128)} %fusion.refs_0_, f32[128,136,128]{2,1,0:T(8,128)} %all-to-all-done.refs_1_, f32[256,128]{1,0:T(8,128)} %bitcast.20, f32[64,2048]{1,0:T(8,128)} %refs_3_.5, f32[64,2048]{1,0:T(8,128)} %refs_4_.3, ...), custom_call_target="tpu_custom_call" | custom-call | tf_op jit(solution)/shard_map/tiles/pallas_call | solution.py:326
  386.8 18.0 %all_to_all.34 = f32[128,2,128]{2,1,0:T(2,128)} all-to-all(f32[128,2,128]{2,1,0:T(2,128)} %bitcast.27), channel_id=1, replica_groups=mesh['row'=16,'col'=8] {'row','col'}, dimensions={0} | all-to-all | bytes 262144 | tf_op jit(solution)/shard_map/all_to_all | solution.py:414
  404.8 2.1 update.5
  406.9 1.4 slice_bitcast_fusion
Async XLA Ops:
  7.8 117.2 %all-to-all-start = ((f32[128,136,128]{2,1,0:T(8,128)}), f32[128,136,128]{2,1,0:T(8,128)}, u32[]{:S(2)}, u32[]{:S(2)}) async-start(f32[128,136,128]{2,1,0:T(8,128)} %get-tuple-element.23), calls=%async_computation | async-start | bytes 17825792 | tf_op jit(solution)/shard_map/all_to_all | solution.py:414

commit v2 on v1

v2 whole, which is shorter than its diff:
```python
import functools

import jax
import jax.numpy as jnp
from jax import lax
from jax.experimental import pallas as pl
from jax.experimental.pallas import tpu as pltpu
from jax.sharding import PartitionSpec as P

ITERS = 3
EPSILON = 0.5
DAMPING = 2.0 / (2.0 + 0.5)
NEGATIVE = -1e30
REAL = -1e29
LOG2E = 1.4426950408889634
LN2 = 0.6931471805599453
TINY = 2.0**-90
HUGE = 2.0**90
AXES = ("row", "col")

D = 64
CS = 256
CL = 8
HALF = 128
ROWS = 2 * D + 8
GROUP = 8
LOCAL_GROUP = 4
PIECES = 8
BF16 = jnp.bfloat16
F32 = jnp.float32


def lists(cross, xself, yself):
    for c in range(cross.shape[0]):
        for k in range(cross.shape[1]):
            yield 0, c, k, cross[c, k]
    for table, kind in ((xself, 1), (yself, 2)):
        for c in range(table.shape[1]):
            for k in range(table.shape[0]):
                yield kind, c, k, table[k, c]


def bias_of(weight, half, potential):
    return LOG2E * (weight + (potential - half) / EPSILON)


def push_kernel(
    cross, xself, yself, x_sizes, y_sizes, x_ref, y_ref, x_mass, y_mass,
    send, weight_ref, half_ref, bias_g_ref, bias_ref, aux, sems,
):
    devices = send.shape[0]
    requests = list(lists(cross, xself, yself))
    for kind, c, _, named in requests:
        owner = named // CL
        source = y_ref if kind == 2 else x_ref
        for h in range(2):
            pltpu.make_async_copy(
                source.at[:, pl.ds(c * CS + h * HALF, HALF)],
                send.at[owner, pl.ds(h * D, D), :],
                sems.at[0],
            ).start()
    row = lax.broadcasted_iota(jnp.int32, (2 * CL, HALF), 0)
    position = (row % 2) * HALF + lax.broadcasted_iota(jnp.int32, (2 * CL, HALF), 1)
    for side, (points, sizes, mass) in enumerate(
        ((x_ref, x_sizes, x_mass), (y_ref, y_sizes, y_mass))
    ):
        count = jnp.zeros((2 * CL, HALF), jnp.int32)
        for c in range(CL):
            count = jnp.where(row // 2 == c, sizes[0, c], count)
        base = side * 2 * CL
        weight_ref[base : base + 2 * CL, :] = jnp.where(position < count, mass[...], NEGATIVE)
        for t in range(2 * CL):
            piece = points[:, t * HALF : (t + 1) * HALF]
            half_ref[base + t : base + t + 1, :] = 0.5 * jnp.sum(piece * piece, axis=0, keepdims=True)
    bias = bias_of(weight_ref[...], half_ref[...], 0.0)
    bias_ref[0 : 2 * CL, :] = bias[0 : 2 * CL, :]
    bias_ref[2 * CL : 6 * CL, :] = bias
    bias_g_ref[...] = bias[2 * CL : 4 * CL, :]
    aux[...] = jnp.zeros_like(aux)
    for kind, c, _, named in requests:
        owner = named // CL
        base = kind * 2 * CL + 2 * c
        aux[owner, 0:2, :] = bias_ref[base : base + 2, :]
        code = (kind * CL + named % CL + 1).astype(F32)
        aux[owner, 2:3, :] = jnp.full((1, HALF), code, F32)
    tail = pltpu.make_async_copy(aux, send.at[:, pl.ds(2 * D, 8), :], sems.at[1])
    tail.start()
    tail.wait()
    sent = send.at[pl.ds(0, len(requests)), pl.ds(0, 2 * D), :]
    pltpu.make_async_copy(sent, sent, sems.at[0]).wait()


def push(cross, xself, yself, x_sizes, y_sizes, x, y, x_mass, y_mass, devices):
    smem = pl.BlockSpec(memory_space=pltpu.SMEM)
    vmem = pl.BlockSpec(memory_space=pltpu.VMEM)
    return pl.pallas_call(
        push_kernel,
        out_shape=(
            jax.ShapeDtypeStruct((devices, ROWS, HALF), F32),
            jax.ShapeDtypeStruct((4 * CL, HALF), F32),
            jax.ShapeDtypeStruct((4 * CL, HALF), F32),
            jax.ShapeDtypeStruct((2 * CL, HALF), F32),
            jax.ShapeDtypeStruct((6 * CL, HALF), F32),
        ),
        in_specs=[smem] * 5 + [vmem] * 4,
        out_specs=(pl.BlockSpec(memory_space=pl.ANY), vmem, vmem, vmem, vmem),
        scratch_shapes=[
            pltpu.VMEM((devices, 8, HALF), F32),
            pltpu.SemaphoreType.DMA((2,)),
        ],
        name="push",
    )(cross, xself, yself, x_sizes, y_sizes, x, y, x_mass, y_mass)


def split2(value):
    high = value.astype(BF16)
    return high, (value - high.astype(F32)).astype(BF16)


def split3(value):
    high = value.astype(BF16).astype(F32)
    rest = value - high
    middle = rest.astype(BF16).astype(F32)
    return high, middle, rest - middle


def left_kernel(x_ref, y_ref, left_ref, right_ref):
    lane = lax.broadcasted_iota(jnp.int32, (CS, HALF), 1)
    for side, points in enumerate((x_ref, y_ref)):
        for c in range(CL):
            piece = points[:, c * CS : (c + 1) * CS]
            scaled = piece * (LOG2E / EPSILON)
            turned = jnp.transpose(jnp.concatenate([scaled, scaled], axis=0))
            high, low = split2(turned)
            left_ref[side * CL + c, :, 0:HALF] = high
            low = jnp.where(lane < D, low.astype(F32), 0.0)
            left_ref[side * CL + c, :, HALF:CS] = low.astype(BF16)
            high, low = split2(piece)
            right_ref[side * CL + c, 0:D, :] = high
            right_ref[side * CL + c, D:HALF, :] = low


def left_side(x, y):
    vmem = pl.BlockSpec(memory_space=pltpu.VMEM)
    return pl.pallas_call(
        left_kernel,
        out_shape=(
            jax.ShapeDtypeStruct((2 * CL, CS, CS), BF16),
            jax.ShapeDtypeStruct((2 * CL, HALF, CS), BF16),
        ),
        in_specs=[vmem, vmem],
        out_specs=(vmem, vmem),
        name="left_side",
    )(x, y)


def scores(left_high, left_rest, high, low, a, e):
    a1, a2, a3 = split3(a)
    row = lax.broadcasted_iota(jnp.int32, (8, CS), 0)
    pick = jnp.where(row == e, 1.0, 0.0)
    mine = jnp.where(row == 0, a1, jnp.where(row == 1, a2, jnp.where(row == 2, a3, 0.0)))
    tail = jnp.concatenate([pick, pick, pick, mine], axis=0).astype(BF16)
    right = jnp.concatenate([high, low, high, tail, jnp.zeros((32, CS), BF16)], axis=0)
    return jnp.dot(
        jnp.concatenate([left_high, left_rest], axis=1), right, preferred_element_type=F32
    )


def put_row(out, at, value):
    out[pl.ds(at, 1), :] = value[:, 0:HALF]
    out[pl.ds(at + 1, 1), :] = value[:, HALF:CS]


def row_sum(value, a):
    return jnp.where(a > REAL, jnp.sum(value, axis=0, keepdims=True), 1.0)


def fold(value):
    return value[:, 0:HALF] + value[:, HALF:CS]


def row_log_sum(z):
    peak = jnp.max(z, axis=0, keepdims=True)
    total = jnp.sum(jnp.exp2(z - peak), axis=0, keepdims=True)
    return peak + jnp.log(total) * LOG2E


def merge_columns(z, te, acc, top):
    peak = jnp.max(z, axis=1, keepdims=True)
    total = jnp.sum(jnp.exp2(z - peak), axis=1, keepdims=True)
    before = top[te]
    now = jnp.maximum(before, peak)
    acc[te] = acc[te] * jnp.exp2(before - now) + total * jnp.exp2(peak - now)
    top[te] = now


def columns(acc, top, cols):
    lane = lax.broadcasted_iota(jnp.int32, (CS, HALF), 1)
    batch = 1 if top is not None else 8

    def some(i, packed):
        for j in range(batch):
            te = i * batch + j
            if top is not None:
                value = jnp.max(top[te] + jnp.log(acc[te]) * LOG2E, axis=1, keepdims=True)
            else:
                value = jnp.sum(acc[te], axis=1, keepdims=True)
            packed = jnp.where(lane == te, value, packed)
        return packed

    packed = lax.fori_loop(0, 3 * CL // batch, some, jnp.zeros((CS, HALF), F32))
    for h in range(2):
        turned = jnp.transpose(packed[h * HALF : (h + 1) * HALF, :])
        for t in range(3):
            cols[pl.ds(t * 2 * CL + h, CL, stride=2), :] = turned[t * CL : (t + 1) * CL, :]


def in_range(*values):
    lowest = functools.reduce(jnp.minimum, [jnp.min(value) for value in values])
    highest = functools.reduce(jnp.maximum, [jnp.max(value) for value in values])
    return jnp.logical_and(lowest > TINY, highest < HUGE)


def local_kernel(left, right, bias_g, bias, left2, log_cols, log_own, acc, top, own):
    row8 = lax.broadcasted_iota(jnp.int32, (8, HALF), 0)
    ones = jnp.where(row8 < 3, 1.0, 0.0)
    span = 2 * CL
    for t in range(3):
        for h in range(2):
            if t == 0:
                value = bias_g[pl.ds(h, CL, stride=2), :]
            else:
                value = bias[pl.ds(t * span + h, CL, stride=2), :]
            high, middle, low = split3(value)
            stack = jnp.concatenate(
                [jnp.zeros((D, HALF), F32), high, middle, low, ones, jnp.zeros((32, HALF), F32)], axis=0
            )
            turned = jnp.transpose(stack).astype(BF16)
            for e in range(CL):
                cluster = e if t == 1 else CL + e
                here = pl.ds(h * HALF, HALF)
                left2[t * CL + e, here, :] = left[cluster, here, pl.ds(HALF, HALF)] + turned

    def sweep(finish):
        for t in range(3):

            def some(i, _):
                for j in range(LOCAL_GROUP):
                    e = i * LOCAL_GROUP + j
                    at = t * span + 2 * e
                    a = jnp.concatenate([bias[pl.ds(at, 1), :], bias[pl.ds(at + 1, 1), :]], axis=1)
                    source = CL + e if t == 2 else e
                    z = scores(
                        left[e if t == 1 else CL + e, :, 0:HALF], left2[t * CL + e],
                        right[source, 0:D, :], right[source, D:HALF, :], a, e,
                    )
                    finish(z, a, t, e)
                return 0

            lax.fori_loop(0, CL // LOCAL_GROUP, some, 0)

    def fast(z, a, t, e):
        value = jnp.exp2(z)
        if t == 0:
            put_row(own, 2 * e, row_sum(value, a))
        acc[t * CL + e] = fold(value)

    def slow(z, a, t, e):
        if t == 0:
            put_row(own, 2 * e, row_log_sum(z))
        merge_columns(z, t * CL + e, acc, top)

    sweep(fast)
    columns(acc, None, log_cols)
    real = jnp.concatenate([bias_g[...], bias[span : 3 * span, :]], axis=0) > REAL
    cols = jnp.where(real, log_cols[...], 1.0)
    within = in_range(own[...], cols)

    @pl.when(within)
    def _():
        log_own[...] = jnp.log(own[...]) * LOG2E
        log_cols[...] = jnp.log(cols) * LOG2E

    @pl.when(jnp.logical_not(within))
    def _():
        acc[...] = jnp.zeros_like(acc)
        top[...] = jnp.full_like(top, 3.0 * NEGATIVE)
        sweep(slow)
        columns(acc, top, log_cols)
        log_own[...] = own[...]


def local_tiles(left, right, bias_g, bias):
    vmem = pl.BlockSpec(memory_space=pltpu.VMEM)
    return pl.pallas_call(
        local_kernel,
        out_shape=(
            jax.ShapeDtypeStruct((3 * CL, CS, HALF), BF16),
            jax.ShapeDtypeStruct((6 * CL, HALF), F32),
            jax.ShapeDtypeStruct((2 * CL, HALF), F32),
        ),
        in_specs=[vmem] * 4,
        out_specs=(vmem,) * 3,
        scratch_shapes=[
            pltpu.VMEM((3 * CL, CS, HALF), F32),
            pltpu.VMEM((3 * CL, CS, HALF), F32),
            pltpu.VMEM((2 * CL, HALF), F32),
        ],
        name="local_tiles",
    )(left, right, bias_g, bias)


def tile_kernel(first, *refs):
    if first:
        (moved, left, left2, bias_g, bias, back, log_cols, slots, targets, bounds, listed,
         held, acc, top, sums, codes, count, sems) = refs
        message = None
    else:
        (moved, message, left, left2, bias_g, bias, slots, targets, bounds, listed,
         back, log_cols, held, acc, top, sums, sems) = refs
    devices = moved.shape[0]
    step = devices // PIECES

    def fetch(i):
        part = pl.ds(i * step, step)
        return pltpu.make_async_copy(moved.at[part], held.at[part], sems.at[i])

    if first:
        tags = pltpu.make_async_copy(moved.at[:, pl.ds(2 * D + 2, 1), :], codes, sems.at[PIECES])
        tags.start()
    for i in range(PIECES):
        fetch(i).start()
    acc[...] = jnp.zeros_like(acc)
    sums[...] = jnp.ones_like(sums)
    if first:
        tags.wait()
        for te in range(3 * CL):
            count[te] = 0

        def gather(s, n):
            code = codes[s, 0, 0].astype(jnp.int32)

            @pl.when(code > 0)
            def _():
                slots[n] = s
                targets[n] = code - 1
                count[code - 1] = 1

            n = n + (code > 0).astype(jnp.int32)
            bounds[s] = n
            return n

        lax.fori_loop(0, devices, gather, 0, unroll=8)
        row = lax.broadcasted_iota(jnp.int32, listed.shape, 0) // 2
        some_listed = jnp.zeros(listed.shape, jnp.int32)
        for te in range(3 * CL):
            some_listed = jnp.where(row == te, count[te], some_listed)
        listed[...] = some_listed
    live = bounds[devices - 1]
    if first:
        for i in range(GROUP):
            slots[live + i] = slots[0]
            targets[live + i] = 0

    def group(finish):
        def run(i, _):
            for j in range(GROUP):
                n = i * GROUP + j
                s, te = slots[n], targets[n]
                e = te % CL
                cluster = jnp.where(te // CL == 1, e, CL + e)
                at = jnp.where(n < live, 2 * s, 2 * devices)
                high, low = split2(jnp.concatenate([held[s, 0:D, :], held[s, D : 2 * D, :]], axis=1))
                if first:
                    pair = held[s, 2 * D : 2 * D + 1, :], held[s, 2 * D + 1 : 2 * D + 2, :]
                else:
                    pair = message[pl.ds(2 * s, 1), :], message[pl.ds(2 * s + 1, 1), :]
                a = jnp.where(n < live, jnp.concatenate(pair, axis=1), LOG2E * NEGATIVE)
                z = scores(left[cluster, :, 0:HALF], left2[te], high, low, a, e)
                finish(z, a, te, at)
            return 0

        return run

    def fast(z, a, te, at):
        value = jnp.exp2(z)
        put_row(sums, at, row_sum(value, a))
        acc[te] = acc[te] + fold(value)

    def slow(z, a, te, at):
        put_row(sums, at, row_log_sum(z))
        merge_columns(z, te, acc, top)

    def piece(i, start):
        fetch(i).wait()
        ready = bounds[(i + 1) * step - 1]
        stop = jnp.where(i == PIECES - 1, (live + GROUP - 1) // GROUP, ready // GROUP)
        lax.fori_loop(start, stop, group(fast), 0)
        return stop

    lax.fori_loop(0, PIECES, piece, 0)
    columns(acc, None, log_cols)
    real = jnp.concatenate([bias_g[...], bias[2 * CL : 6 * CL, :]], axis=0) > REAL
    named = listed[...] > 0
    cols = jnp.where(jnp.logical_and(real, named), log_cols[...], 1.0)
    within = in_range(sums[...], cols)

    @pl.when(within)
    def _():
        back[...] = jnp.log(sums[0 : 2 * devices, :]) * LOG2E
        log_cols[...] = jnp.where(named, jnp.log(cols) * LOG2E, NEGATIVE)

    @pl.when(jnp.logical_not(within))
    def _():
        acc[...] = jnp.zeros_like(acc)
        top[...] = jnp.full_like(top, 3.0 * NEGATIVE)
        lax.fori_loop(0, (live + GROUP - 1) // GROUP, group(slow), 0)
        columns(acc, top, log_cols)
        log_cols[...] = jnp.where(named, log_cols[...], NEGATIVE)
        back[...] = sums[0 : 2 * devices, :]


def tiles(moved, message, left, left2, bias_g, bias, index):
    first = index is None
    devices = moved.shape[0]
    smem = pl.BlockSpec(memory_space=pltpu.SMEM)
    vmem = pl.BlockSpec(memory_space=pltpu.VMEM)
    hbm = pl.BlockSpec(memory_space=pl.ANY)
    outs = [
        jax.ShapeDtypeStruct((2 * devices, HALF), F32),
        jax.ShapeDtypeStruct((6 * CL, HALF), F32),
    ]
    index_shapes = [
        jax.ShapeDtypeStruct((devices + GROUP,), jnp.int32),
        jax.ShapeDtypeStruct((devices + GROUP,), jnp.int32),
        jax.ShapeDtypeStruct((devices,), jnp.int32),
        jax.ShapeDtypeStruct((6 * CL, HALF), jnp.int32),
    ]
    index_specs = [smem, smem, smem, vmem]
    scratch = [
        pltpu.VMEM((devices, ROWS, HALF), F32),
        pltpu.VMEM((3 * CL, CS, HALF), F32),
        pltpu.VMEM((3 * CL, CS, HALF), F32),
        pltpu.VMEM((2 * devices + 8, HALF), F32),
    ]
    if first:
        scratch += [pltpu.SMEM((devices, 1, HALF), F32), pltpu.SMEM((3 * CL,), jnp.int32)]
    scratch += [pltpu.SemaphoreType.DMA((PIECES + 1,))]
    out = pl.pallas_call(
        functools.partial(tile_kernel, first),
        out_shape=outs + (index_shapes if first else []),
        in_specs=[hbm] + [vmem] * (4 if first else 5) + ([] if first else index_specs),
        out_specs=[vmem, vmem] + (index_specs if first else []),
        scratch_shapes=scratch,
        name="tiles_first" if first else "tiles",
    )(*((moved, left, left2, bias_g, bias) if first else (moved, message, left, left2, bias_g, bias, *index)))
    return out[0], out[1], out[2:] if first else index


def log_sum(values):
    peak = functools.reduce(jnp.maximum, values)
    total = functools.reduce(jnp.add, [jnp.exp2(value - peak) for value in values])
    return peak + jnp.log(total) * LOG2E


def fresh(total, bias, weight, half, potential):
    log_total = LN2 * (total - bias) - half / EPSILON
    value = 0.5 * (potential - DAMPING * EPSILON * log_total)
    return jnp.where(weight > REAL, value, 0.0)


def update_g_kernel(cols_local, cols_moved, weight, half, bias, potential, new, *new_bias):
    side = slice(2 * CL, 4 * CL)
    span = slice(0, 2 * CL)
    total = log_sum([cols_local[span, :], cols_moved[span, :]])
    value = fresh(total, bias[...], weight[side, :], half[side, :], potential[...])
    new[...] = value
    for ref in new_bias:
        ref[...] = bias_of(weight[side, :], half[side, :], value)


def update_g(last, *args):
    vmem = pl.BlockSpec(memory_space=pltpu.VMEM)
    shapes = (jax.ShapeDtypeStruct((2 * CL, HALF), F32),) * (1 if last else 2)
    return pl.pallas_call(
        update_g_kernel,
        out_shape=shapes,
        in_specs=[vmem] * 6,
        out_specs=(vmem,) * len(shapes),
        name="update_g",
    )(*args)


def update_kernel(
    last, cross, xself, yself, back, cols_local, cols_moved, log_own, weight, half, potential, bias, *refs
):
    if last:
        *new, parts = refs
    else:
        new, new_bias, message, parts = refs
    counts = (cross.shape[1], xself.shape[0], yself.shape[0])
    offsets = (0, counts[0], counts[0] + counts[1])
    requests = list(lists(cross, xself, yself))
    for kind, c, k, named in requests:
        at = pl.multiple_of(2 * (named // CL), 2)
        parts[offsets[kind] + k, 2 * c : 2 * c + 2, :] = back[pl.ds(at, 2), :]
    span = 2 * CL
    answers = [[parts[offsets[t] + k] for k in range(counts[t])] for t in range(3)]
    p, q = slice(span, 2 * span), slice(2 * span, 3 * span)
    totals = (
        log_sum([log_own[...]] + answers[0]),
        log_sum([cols_local[p, :], cols_moved[p, :]] + answers[1]),
        log_sum([cols_local[q, :], cols_moved[q, :]] + answers[2]),
    )
    for i, total in enumerate(totals):
        here = slice(i * span, (i + 1) * span)
        side = slice(span, 2 * span) if i == 2 else slice(0, span)
        value = fresh(total, bias[here, :], weight[side, :], half[side, :], potential[here, :])
        if last:
            new[i][...] = value
        else:
            new[here, :] = value
            new_bias[here, :] = bias_of(weight[side, :], half[side, :], value)
    if last:
        return
    for kind, c, _, named in requests:
        at = pl.multiple_of(2 * (named // CL), 2)
        base = kind * span + 2 * c
        message[pl.ds(at, 2), :] = new_bias[base : base + 2, :]


def update(last, cross, xself, yself, back, *args):
    smem = pl.BlockSpec(memory_space=pltpu.SMEM)
    vmem = pl.BlockSpec(memory_space=pltpu.VMEM)
    one = jax.ShapeDtypeStruct((2 * CL, HALF), F32)
    three = jax.ShapeDtypeStruct((6 * CL, HALF), F32)
    shapes = (one,) * 3 if last else (three, three, jax.ShapeDtypeStruct(back.shape, F32))
    listed = cross.shape[1] + xself.shape[0] + yself.shape[0]
    return pl.pallas_call(
        functools.partial(update_kernel, last),
        out_shape=shapes,
        in_specs=[smem] * 3 + [vmem] * 8,
        out_specs=(vmem,) * len(shapes),
        scratch_shapes=[pltpu.VMEM((listed, 2 * CL, HALF), F32)],
        name="update",
    )(cross, xself, yself, back, *args)


def exchange(blocks):
    return lax.all_to_all(blocks, AXES, split_axis=0, concat_axis=0, tiled=True)


def exchange_rows(rows, devices):
    return exchange(rows.reshape(devices, 2, HALF)).reshape(2 * devices, HALF)


def local(x, y, x_logmass, y_logmass, x_sizes, y_sizes, cross, xself, yself):
    devices = lax.axis_size(AXES)
    xself, yself = xself.T, yself.T
    send, weight, half, bias_g, bias = push(
        cross, xself, yself, x_sizes, y_sizes, x, y,
        x_logmass.reshape(2 * CL, HALF), y_logmass.reshape(2 * CL, HALF), devices,
    )
    moved = exchange(send)
    left, right = left_side(x, y)
    potential_g = jnp.zeros((2 * CL, HALF), F32)
    potential = jnp.zeros((6 * CL, HALF), F32)
    message = index = None
    for iteration in range(ITERS):
        last = iteration == ITERS - 1
        left2, cols_local, log_own = local_tiles(left, right, bias_g, bias)
        back, cols_moved, index = tiles(moved, message, left, left2, bias_g, bias, index)
        back = exchange_rows(back, devices)
        out_g = update_g(last, cols_local, cols_moved, weight, half, bias_g, potential_g)
        out = update(
            last, cross, xself, yself, back, cols_local, cols_moved, log_own, weight, half, potential, bias
        )
        if not last:
            potential_g, bias_g = out_g
            potential, bias, message = out
            message = exchange_rows(message, devices)
    f, p, q = out
    return tuple(part.reshape(2 * CL * HALF) for part in (f, out_g[0], p, q))


def solution(mesh):
    flat, table = P(AXES), P(AXES, None)
    points = P(None, AXES)
    return jax.shard_map(
        local,
        mesh=mesh,
        in_specs=(points, points, flat, flat, table, table, table, table, table),
        out_specs=(flat, flat, flat, flat),
        check_vma=False,
    )
```

time: 409 us -> 335 us (0.82)
  blocking collectives: 93.7 us -> 45 us
  Pallas kernels: 191 us -> 157 us
  starting transfers between devices: 11.9 us -> 30.6 us
  waiting for transfers between devices: 102 us -> 96.7 us
    all_to_all x5 -> x2, blocking collectives: 93.7 us -> 45 us  [exchange(): return lax.all_to_all(blocks, AXES, split_axis=0, concat_axis=0, tiled=True)]
    pallas_call x4 -> x10, Pallas kernels: 180 us -> 146 us  [the longest x3 96.1 us: tiles(): pl.pallas_call(functools.partial(tile_kernel, first), out_shape=outs + (i...]
    all_to_all x1 -> x4, starting transfers between devices: 11.9 us -> 30.6 us  [exchange(): return lax.all_to_all(blocks, AXES, split_axis=0, concat_axis=0, tiled=True)]
    all_to_all x1 -> x4, waiting for transfers between devices: 102 us -> 96.7 us  [exchange(): return lax.all_to_all(blocks, AXES, split_axis=0, concat_axis=0, tiled=True)]
  transfers between devices with their start and end apart: 1 -> 4, of which waited for: 1 -> 2; matrix products, arithmetic and copies ran while one was open for 0% -> 0% of each run, Pallas kernels for 1% -> 15%
where the time goes in v2:
time: 335 us; the launch traced here: 333 us
  Pallas kernels  157 us (47%)
  waiting for transfers between devices  96.7 us (29%)
  blocking collectives  45 us (13%)
  starting transfers between devices  30.6 us (9%)
    all_to_all x4, waiting for transfers between devices, exchange(): return lax.all_to_all(blocks, AXES, split_axis=0, concat_axis=0, tiled=True)  96.7 us
    pallas_call x3, Pallas kernels, tiles(): pl.pallas_call(functools.partial(tile_kernel, first), out_shape=outs + (i...  96.1 us
    all_to_all x2, blocking collectives, exchange(): return lax.all_to_all(blocks, AXES, split_axis=0, concat_axis=0, tiled=True)  45 us
    pallas_call x3, Pallas kernels, local_tiles(): pl.pallas_call(local_kernel, out_shape=(jax.ShapeDtypeStruct((3 * CL, CS,...  42 us
    all_to_all x4, starting transfers between devices, exchange(): return lax.all_to_all(blocks, AXES, split_axis=0, concat_axis=0, tiled=True)  30.6 us
  transfers between devices with their start and end apart: 4, of which 2 were waited for; matrix products, arithmetic and copies ran while one was open for 0% of the time, Pallas kernels for 15%

profile of v2, /device:TPU:1, one launch (start us, length us, event | category | flops | bytes accessed | tf_op | source)
XLA Modules:
  0.0 332.8 jit_solution(11598047315957826526)
XLA Ops:
  0.6 4.6 %push.1 = (f32[128,136,128]{2,1,0:T(8,128)}, f32[32,128]{1,0:T(8,128)}, f32[32,128]{1,0:T(8,128)}, f32[16,128]{1,0:T(8,128)}, f32[48,128]{1,0:T(8,128)}) custom-call(s32[8,7]{1,0:T(8,128)} %cross.7, s32[2,8]{1,0:T(2,128)} %bitcast.28, s32[2,8]{1,0:T(2,128)} %bitcast.32, s32[1,8]{1,0:T(1,128)} %x_sizes.1, s32[1,8]{1,0:T(1,128)} %y_sizes.1, f32[64,2048]{1,0:T(8,128)} %x_ref.3, ...), custom_call_target="tpu_custom_call" | custom-call | tf_op jit(solution)/shard_map/push/pallas_call | solution.py:96
  5.2 11.8 %all-to-all-start = ((f32[128,136,128]{2,1,0:T(8,128)}), f32[128,136,128]{2,1,0:T(8,128)}, u32[]{:S(2)}, u32[]{:S(2)}) async-start(f32[128,136,128]{2,1,0:T(8,128)} %get-tuple-element.43), calls=%async_computation | async-start | bytes 17825792 | tf_op jit(solution)/shard_map/all_to_all | solution.py:550
  17.1 3.3 left_side.1
  20.3 13.9 %local_tiles.3 = (bf16[24,256,128]{2,1,0:T(8,128)(2,1)}, f32[48,128]{1,0:T(8,128)}, f32[16,128]{1,0:T(8,128)}) custom-call(bf16[16,256,256]{2,1,0:T(8,128)(2,1)} %get-tuple-element.44.left.refs_1_.refs_2_, bf16[16,128,256]{2,1,0:T(8,128)(2,1)} %get-tuple-element.45.right, f32[16,128]{1,0:T(8,128)} %get-tuple-element.46.bias_g.refs_3_.bias, ...), custom_call_target="tpu_custom_call" | custom-call | tf_op jit(solution)/shard_map/local_tiles/pallas_call | solution.py:295
  34.3 88.1 %all-to-all-done.refs_0_ = f32[128,136,128]{2,1,0:T(8,128)} async-done(((f32[128,136,128]{2,1,0:T(8,128)}), f32[128,136,128]{2,1,0:T(8,128)}, u32[]{:S(2)}, u32[]{:S(2)}) %all-to-all-start) | async-done | bytes 8912928 | tf_op jit(solution)/shard_map/all_to_all | solution.py:550
  122.4 32.9 %tiles_first.1 = (f32[256,128]{1,0:T(8,128)}, f32[48,128]{1,0:T(8,128)}, s32[136]{0:T(256)}, s32[136]{0:T(256)}, s32[128]{0:T(128)}, /*index=5*/s32[48,128]{1,0:T(8,128)}) custom-call(f32[128,136,128]{2,1,0:T(8,128)} %all-to-all-done.refs_0_, bf16[16,256,256]{2,1,0:T(8,128)(2,1)} %get-tuple-element.44.left.refs_1_.refs_2_, ...), custom_call_target="tpu_custom_call" | custom-call | tf_op jit(solution)/shard_map/tiles_first/pallas_call | solution.py:449
  155.3 25.0 %all_to_all.30 = f32[128,2,128]{2,1,0:T(2,128)} all-to-all(f32[128,2,128]{2,1,0:T(2,128)} %bitcast.26), channel_id=1, replica_groups=mesh['row'=16,'col'=8] {'row','col'}, dimensions={0} | all-to-all | bytes 262144 | tf_op jit(solution)/shard_map/all_to_all | solution.py:550
  180.3 0.6 broadcast_in_dim.6.potential
  180.9 2.2 update.3
  183.1 4.5 %all-to-all-start.2 = ((f32[128,2,128]{2,1,0:T(2,128)}), f32[128,2,128]{2,1,0:T(2,128)S(1)}, u32[]{:S(2)}, u32[]{:S(2)}) async-start(f32[128,2,128]{2,1,0:T(2,128)} %bitcast.23), calls=%async_computation.2 | async-start | bytes 262144 | tf_op jit(solution)/shard_map/all_to_all | solution.py:550
  187.7 0.6 broadcast_in_dim.7.potential
  188.3 1.4 update_g.3
  189.7 13.9 %local_tiles.4 = (bf16[24,256,128]{2,1,0:T(8,128)(2,1)}, f32[48,128]{1,0:T(8,128)}, f32[16,128]{1,0:T(8,128)}) custom-call(bf16[16,256,256]{2,1,0:T(8,128)(2,1)} %get-tuple-element.44.left.refs_1_.refs_2_, bf16[16,128,256]{2,1,0:T(8,128)(2,1)} %get-tuple-element.45.right, f32[16,128]{1,0:T(8,128)} %get-tuple-element.56.bias_g.refs_4_.bias, ...), custom_call_target="tpu_custom_call" | custom-call | tf_op jit(solution)/shard_map/local_tiles/pallas_call | solution.py:295
  203.6 0.0 all-to-all-done.2
  203.6 0.0 copy-start.1
  203.6 0.6 copy-done.1
  204.2 31.6 %tiles.2 = (f32[256,128]{1,0:T(8,128)}, f32[48,128]{1,0:T(8,128)}) custom-call(f32[128,136,128]{2,1,0:T(8,128)} %all-to-all-done.refs_0_, f32[256,128]{1,0:T(8,128)} %bitcast.19, bf16[16,256,256]{2,1,0:T(8,128)(2,1)} %get-tuple-element.44.left.refs_1_.refs_2_, bf16[24,256,128]{2,1,0:T(8,128)(2,1)} %get-tuple-element.58.refs_3_, ...), custom_call_target="tpu_custom_call" | custom-call | tf_op jit(solution)/shard_map/tiles/pallas_call | solution.py:449
  235.8 20.0 %all_to_all.31 = f32[128,2,128]{2,1,0:T(2,128)} all-to-all(f32[128,2,128]{2,1,0:T(2,128)} %bitcast.27), channel_id=1, replica_groups=mesh['row'=16,'col'=8] {'row','col'}, dimensions={0} | all-to-all | bytes 262144 | tf_op jit(solution)/shard_map/all_to_all | solution.py:550
  255.8 2.2 update.4
  258.0 4.5 %all-to-all-start.4 = ((f32[128,2,128]{2,1,0:T(2,128)}), f32[128,2,128]{2,1,0:T(2,128)S(1)}, u32[]{:S(2)}, u32[]{:S(2)}) async-start(f32[128,2,128]{2,1,0:T(2,128)} %bitcast.24), calls=%async_computation.4 | async-start | bytes 262144 | tf_op jit(solution)/shard_map/all_to_all | solution.py:550
  262.5 1.4 update_g.4
  263.9 14.2 %local_tiles.5 = (bf16[24,256,128]{2,1,0:T(8,128)(2,1)}, f32[48,128]{1,0:T(8,128)}, f32[16,128]{1,0:T(8,128)}) custom-call(bf16[16,256,256]{2,1,0:T(8,128)(2,1)} %get-tuple-element.44.left.refs_1_.refs_2_, bf16[16,128,256]{2,1,0:T(8,128)(2,1)} %get-tuple-element.45.right, f32[16,128]{1,0:T(8,128)} %get-tuple-element.70.bias_g.refs_4_.bias, ...), custom_call_target="tpu_custom_call" | custom-call | tf_op jit(solution)/shard_map/local_tiles/pallas_call | solution.py:295
  278.1 0.0 all-to-all-done.4
  278.1 0.0 copy-start
  278.1 0.7 copy-done
  278.7 31.6 %tiles.3 = (f32[256,128]{1,0:T(8,128)}, f32[48,128]{1,0:T(8,128)}) custom-call(f32[128,136,128]{2,1,0:T(8,128)} %all-to-all-done.refs_0_, f32[256,128]{1,0:T(8,128)} %bitcast.18, bf16[16,256,256]{2,1,0:T(8,128)(2,1)} %get-tuple-element.44.left.refs_1_.refs_2_, bf16[24,256,128]{2,1,0:T(8,128)(2,1)} %get-tuple-element.72.refs_3_, ...), custom_call_target="tpu_custom_call" | custom-call | tf_op jit(solution)/shard_map/tiles/pallas_call | solution.py:449
  310.3 9.8 %all-to-all-start.5 = ((f32[128,2,128]{2,1,0:T(2,128)}), f32[128,2,128]{2,1,0:T(2,128)S(1)}, u32[]{:S(2)}, u32[]{:S(2)}) async-start(f32[128,2,128]{2,1,0:T(2,128)} %bitcast.25), calls=%async_computation.5 | async-start | bytes 262144 | tf_op jit(solution)/shard_map/all_to_all | solution.py:550
  320.1 1.4 update_g.5
  321.5 8.6 %all-to-all-done.5 = f32[128,2,128]{2,1,0:T(2,128)S(1)} async-done(((f32[128,2,128]{2,1,0:T(2,128)}), f32[128,2,128]{2,1,0:T(2,128)S(1)}, u32[]{:S(2)}, u32[]{:S(2)}) %all-to-all-start.5) | async-done | bytes 131104 | tf_op jit(solution)/shard_map/all_to_all | solution.py:550
  330.1 0.0 copy-start.2
  330.1 0.6 copy-done.2
  330.7 2.1 update.5
Async XLA Ops:
  5.2 117.2 %all-to-all-start = ((f32[128,136,128]{2,1,0:T(8,128)}), f32[128,136,128]{2,1,0:T(8,128)}, u32[]{:S(2)}, u32[]{:S(2)}) async-start(f32[128,136,128]{2,1,0:T(8,128)} %get-tuple-element.43), calls=%async_computation | async-start | bytes 17825792 | tf_op jit(solution)/shard_map/all_to_all | solution.py:550
  183.1 20.4 %all-to-all-start.2 = ((f32[128,2,128]{2,1,0:T(2,128)}), f32[128,2,128]{2,1,0:T(2,128)S(1)}, u32[]{:S(2)}, u32[]{:S(2)}) async-start(f32[128,2,128]{2,1,0:T(2,128)} %bitcast.23), calls=%async_computation.2 | async-start | bytes 262144 | tf_op jit(solution)/shard_map/all_to_all | solution.py:550
  203.6 0.6 copy-start.1
  258.0 20.1 %all-to-all-start.4 = ((f32[128,2,128]{2,1,0:T(2,128)}), f32[128,2,128]{2,1,0:T(2,128)S(1)}, u32[]{:S(2)}, u32[]{:S(2)}) async-start(f32[128,2,128]{2,1,0:T(2,128)} %bitcast.24), calls=%async_computation.4 | async-start | bytes 262144 | tf_op jit(solution)/shard_map/all_to_all | solution.py:550
  278.1 0.7 copy-start
  310.3 19.8 %all-to-all-start.5 = ((f32[128,2,128]{2,1,0:T(2,128)}), f32[128,2,128]{2,1,0:T(2,128)S(1)}, u32[]{:S(2)}, u32[]{:S(2)}) async-start(f32[128,2,128]{2,1,0:T(2,128)} %bitcast.25), calls=%async_computation.5 | async-start | bytes 262144 | tf_op jit(solution)/shard_map/all_to_all | solution.py:550
  330.1 0.7 copy-start.2

commit v3 on v2

--- a/solution.py
+++ b/solution.py
@@ -26,6 +26,7 @@
 GROUP = 8
 LOCAL_GROUP = 4
 PIECES = 8
+SPAN = 16
 BF16 = jnp.bfloat16
 F32 = jnp.float32
 
@@ -221,16 +222,15 @@
     return jnp.logical_and(lowest > TINY, highest < HUGE)
 
 
-def local_kernel(left, right, bias_g, bias, left2, log_cols, log_own, acc, top, own):
+def build_left2(left, bias_g, bias, left2):
     row8 = lax.broadcasted_iota(jnp.int32, (8, HALF), 0)
     ones = jnp.where(row8 < 3, 1.0, 0.0)
-    span = 2 * CL
     for t in range(3):
         for h in range(2):
             if t == 0:
                 value = bias_g[pl.ds(h, CL, stride=2), :]
             else:
-                value = bias[pl.ds(t * span + h, CL, stride=2), :]
+                value = bias[pl.ds(t * SPAN + h, CL, stride=2), :]
             high, middle, low = split3(value)
             stack = jnp.concatenate(
                 [jnp.zeros((D, HALF), F32), high, middle, low, ones, jnp.zeros((32, HALF), F32)], axis=0
@@ -240,6 +240,11 @@
                 cluster = e if t == 1 else CL + e
                 here = pl.ds(h * HALF, HALF)
                 left2[t * CL + e, here, :] = left[cluster, here, pl.ds(HALF, HALF)] + turned
+
+
+def local_kernel(left, right, bias_g, bias, left2, log_cols, log_own, acc, top, own):
+    span = SPAN
+    build_left2(left, bias_g, bias, left2)
 
     def sweep(finish):
         for t in range(3):
@@ -310,151 +315,185 @@
     )(left, right, bias_g, bias)
 
 
-def tile_kernel(first, *refs):
-    if first:
-        (moved, left, left2, bias_g, bias, back, log_cols, slots, targets, bounds, listed,
-         held, acc, top, sums, codes, count, sems) = refs
-        message = None
-    else:
-        (moved, message, left, left2, bias_g, bias, slots, targets, bounds, listed,
-         back, log_cols, held, acc, top, sums, sems) = refs
-    devices = moved.shape[0]
-    step = devices // PIECES
+def fetch_all(moved, held, sems):
+    step = moved.shape[0] // PIECES
 
     def fetch(i):
         part = pl.ds(i * step, step)
         return pltpu.make_async_copy(moved.at[part], held.at[part], sems.at[i])
 
-    if first:
-        tags = pltpu.make_async_copy(moved.at[:, pl.ds(2 * D + 2, 1), :], codes, sems.at[PIECES])
-        tags.start()
     for i in range(PIECES):
         fetch(i).start()
+    return fetch
+
+
+class Tiles:
+    def __init__(self, held, left, slots, targets, bounds):
+        self.held, self.left = held, left
+        self.slots, self.targets, self.bounds = slots, targets, bounds
+        self.devices = held.shape[0]
+        self.live = bounds[self.devices - 1]
+
+    def run(self, size, left2, inbox, finish):
+        held, left = self.held, self.left
+
+        def body(i, _):
+            for j in range(size):
+                n = i * size + j
+                s, te = self.slots[n], self.targets[n]
+                e = te % CL
+                cluster = jnp.where(te // CL == 1, e, CL + e)
+                spot = jnp.where(n < self.live, s, self.devices)
+                high, low = split2(jnp.concatenate([held[s, 0:D, :], held[s, D : 2 * D, :]], axis=1))
+                if inbox is None:
+                    pair = held[s, 2 * D : 2 * D + 1, :], held[s, 2 * D + 1 : 2 * D + 2, :]
+                else:
+                    pair = inbox[pl.ds(4 * s + 2, 1), :], inbox[pl.ds(4 * s + 3, 1), :]
+                a = jnp.where(n < self.live, jnp.concatenate(pair, axis=1), LOG2E * NEGATIVE)
+                z = scores(left[cluster, :, 0:HALF], left2[te], high, low, a, e)
+                finish(z, a, te, spot)
+            return 0
+
+        return body
+
+    def sweep(self, left2, inbox, finish, fetch=None):
+        run = self.run(GROUP, left2, inbox, finish)
+        groups = (self.live + GROUP - 1) // GROUP
+        if fetch is None:
+            lax.fori_loop(0, groups, run, 0)
+            return
+        step = self.devices // PIECES
+
+        def piece(i, start):
+            fetch(i).wait()
+            ready = self.bounds[(i + 1) * step - 1]
+            stop = jnp.where(i == PIECES - 1, groups, ready // GROUP)
+            lax.fori_loop(start, stop, run, 0)
+            return stop
+
+        lax.fori_loop(0, PIECES, piece, 0)
+
+    def slow_sweep(self, left2, inbox, finish):
+        lax.fori_loop(0, self.live, self.run(1, left2, inbox, finish), 0)
+
+
+def column_pass(tiles, left2, inbox, fetch, acc, top, cols, start_g, start, named, sums=None):
+    def fast(z, a, te, spot):
+        value = jnp.exp2(z)
+        if sums is not None:
+            put_row(sums, 2 * spot, row_sum(value, a))
+        acc[te] = acc[te] + fold(value)
+
+    def slow(z, a, te, spot):
+        if sums is not None:
+            put_row(sums, 2 * spot, row_log_sum(z))
+        merge_columns(z, te, acc, top)
+
+    tiles.sweep(left2, inbox, fast, fetch)
+    columns(acc, None, cols)
+    real = jnp.concatenate([start_g[...], start[SPAN : 3 * SPAN, :]], axis=0) > REAL
+    linear = jnp.where(jnp.logical_and(real, named), cols[...], 1.0)
+    within = in_range(linear) if sums is None else in_range(sums[...], linear)
+
+    @pl.when(within)
+    def _():
+        cols[...] = jnp.where(named, jnp.log(linear) * LOG2E, NEGATIVE)
+
+    @pl.when(jnp.logical_not(within))
+    def _():
+        acc[...] = jnp.zeros_like(acc)
+        top[...] = jnp.full_like(top, 3.0 * NEGATIVE)
+        tiles.slow_sweep(left2, inbox, slow)
+        columns(acc, top, cols)
+        cols[...] = jnp.where(named, cols[...], NEGATIVE)
+
+    return within
+
+
+def first_kernel(
+    moved, left, left2, start_g, start, back, log_cols, slots, targets, bounds, listed,
+    held, acc, top, sums, codes, count, sems,
+):
+    devices = moved.shape[0]
+    tags = pltpu.make_async_copy(moved.at[:, pl.ds(2 * D + 2, 1), :], codes, sems.at[PIECES])
+    tags.start()
+    fetch = fetch_all(moved, held, sems)
     acc[...] = jnp.zeros_like(acc)
     sums[...] = jnp.ones_like(sums)
-    if first:
-        tags.wait()
-        for te in range(3 * CL):
-            count[te] = 0
-
-        def gather(s, n):
-            code = codes[s, 0, 0].astype(jnp.int32)
-
-            @pl.when(code > 0)
-            def _():
-                slots[n] = s
-                targets[n] = code - 1
-                count[code - 1] = 1
-
-            n = n + (code > 0).astype(jnp.int32)
-            bounds[s] = n
-            return n
-
-        lax.fori_loop(0, devices, gather, 0, unroll=8)
-        row = lax.broadcasted_iota(jnp.int32, listed.shape, 0) // 2
-        some_listed = jnp.zeros(listed.shape, jnp.int32)
-        for te in range(3 * CL):
-            some_listed = jnp.where(row == te, count[te], some_listed)
-        listed[...] = some_listed
-    live = bounds[devices - 1]
-    if first:
-        for i in range(GROUP):
-            slots[live + i] = slots[0]
-            targets[live + i] = 0
-
-    def group(finish):
-        def run(i, _):
-            for j in range(GROUP):
-                n = i * GROUP + j
-                s, te = slots[n], targets[n]
-                e = te % CL
-                cluster = jnp.where(te // CL == 1, e, CL + e)
-                at = jnp.where(n < live, 2 * s, 2 * devices)
-                high, low = split2(jnp.concatenate([held[s, 0:D, :], held[s, D : 2 * D, :]], axis=1))
-                if first:
-                    pair = held[s, 2 * D : 2 * D + 1, :], held[s, 2 * D + 1 : 2 * D + 2, :]
-                else:
-                    pair = message[pl.ds(2 * s, 1), :], message[pl.ds(2 * s + 1, 1), :]
-                a = jnp.where(n < live, jnp.concatenate(pair, axis=1), LOG2E * NEGATIVE)
-                z = scores(left[cluster, :, 0:HALF], left2[te], high, low, a, e)
-                finish(z, a, te, at)
-            return 0
-
-        return run
-
-    def fast(z, a, te, at):
-        value = jnp.exp2(z)
-        put_row(sums, at, row_sum(value, a))
-        acc[te] = acc[te] + fold(value)
-
-    def slow(z, a, te, at):
-        put_row(sums, at, row_log_sum(z))
-        merge_columns(z, te, acc, top)
-
-    def piece(i, start):
-        fetch(i).wait()
-        ready = bounds[(i + 1) * step - 1]
-        stop = jnp.where(i == PIECES - 1, (live + GROUP - 1) // GROUP, ready // GROUP)
-        lax.fori_loop(start, stop, group(fast), 0)
-        return stop
-
-    lax.fori_loop(0, PIECES, piece, 0)
-    columns(acc, None, log_cols)
-    real = jnp.concatenate([bias_g[...], bias[2 * CL : 6 * CL, :]], axis=0) > REAL
-    named = listed[...] > 0
-    cols = jnp.where(jnp.logical_and(real, named), log_cols[...], 1.0)
-    within = in_range(sums[...], cols)
+    for te in range(3 * CL):
+        count[te] = 0
+    tags.wait()
+
+    def gather(s, n):
+        code = codes[s, 0, 0].astype(jnp.int32)
+
+        @pl.when(code > 0)
+        def _():
+            slots[n] = s
+            targets[n] = code - 1
+            count[code - 1] = 1
+
+        n = n + (code > 0).astype(jnp.int32)
+        bounds[s] = n
+        return n
+
+    live = lax.fori_loop(0, devices, gather, 0, unroll=8)
+    row = lax.broadcasted_iota(jnp.int32, listed.shape, 0) // 2
+    some_listed = jnp.zeros(listed.shape, jnp.int32)
+    for te in range(3 * CL):
+        some_listed = jnp.where(row == te, count[te], some_listed)
+    listed[...] = some_listed
+    for i in range(GROUP):
+        slots[live + i] = slots[0]
+        targets[live + i] = 0
+    tiles = Tiles(held, left, slots, targets, bounds)
+    named = some_listed > 0
+    within = column_pass(tiles, left2, None, fetch, acc, top, log_cols, start_g, start, named, sums)
 
     @pl.when(within)
     def _():
         back[...] = jnp.log(sums[0 : 2 * devices, :]) * LOG2E
-        log_cols[...] = jnp.where(named, jnp.log(cols) * LOG2E, NEGATIVE)
 
     @pl.when(jnp.logical_not(within))
     def _():
-        acc[...] = jnp.zeros_like(acc)
-        top[...] = jnp.full_like(top, 3.0 * NEGATIVE)
-        lax.fori_loop(0, (live + GROUP - 1) // GROUP, group(slow), 0)
-        columns(acc, top, log_cols)
-        log_cols[...] = jnp.where(named, log_cols[...], NEGATIVE)
         back[...] = sums[0 : 2 * devices, :]
 
 
-def tiles(moved, message, left, left2, bias_g, bias, index):
-    first = index is None
+SMEM = pl.BlockSpec(memory_space=pltpu.SMEM)
+VMEM = pl.BlockSpec(memory_space=pltpu.VMEM)
+HBM = pl.BlockSpec(memory_space=pl.ANY)
+
+
+def shape(*dims, dtype=F32):
+    return jax.ShapeDtypeStruct(dims, dtype)
+
+
+def first_tiles(moved, left, left2, start_g, start):
     devices = moved.shape[0]
-    smem = pl.BlockSpec(memory_space=pltpu.SMEM)
-    vmem = pl.BlockSpec(memory_space=pltpu.VMEM)
-    hbm = pl.BlockSpec(memory_space=pl.ANY)
-    outs = [
-        jax.ShapeDtypeStruct((2 * devices, HALF), F32),
-        jax.ShapeDtypeStruct((6 * CL, HALF), F32),
-    ]
-    index_shapes = [
-        jax.ShapeDtypeStruct((devices + GROUP,), jnp.int32),
-        jax.ShapeDtypeStruct((devices + GROUP,), jnp.int32),
-        jax.ShapeDtypeStruct((devices,), jnp.int32),
-        jax.ShapeDtypeStruct((6 * CL, HALF), jnp.int32),
-    ]
-    index_specs = [smem, smem, smem, vmem]
-    scratch = [
-        pltpu.VMEM((devices, ROWS, HALF), F32),
-        pltpu.VMEM((3 * CL, CS, HALF), F32),
-        pltpu.VMEM((3 * CL, CS, HALF), F32),
-        pltpu.VMEM((2 * devices + 8, HALF), F32),
-    ]
-    if first:
-        scratch += [pltpu.SMEM((devices, 1, HALF), F32), pltpu.SMEM((3 * CL,), jnp.int32)]
-    scratch += [pltpu.SemaphoreType.DMA((PIECES + 1,))]
     out = pl.pallas_call(
-        functools.partial(tile_kernel, first),
-        out_shape=outs + (index_shapes if first else []),
-        in_specs=[hbm] + [vmem] * (4 if first else 5) + ([] if first else index_specs),
-        out_specs=[vmem, vmem] + (index_specs if first else []),
-        scratch_shapes=scratch,
-        name="tiles_first" if first else "tiles",
-    )(*((moved, left, left2, bias_g, bias) if first else (moved, message, left, left2, bias_g, bias, *index)))
-    return out[0], out[1], out[2:] if first else index
+        first_kernel,
+        out_shape=(
+            shape(2 * devices, HALF),
+            shape(3 * SPAN, HALF),
+            shape(devices + GROUP, dtype=jnp.int32),
+            shape(devices + GROUP, dtype=jnp.int32),
+            shape(devices, dtype=jnp.int32),
+            shape(3 * SPAN, HALF, dtype=jnp.int32),
+        ),
+        in_specs=[HBM] + [VMEM] * 4,
+        out_specs=(VMEM, VMEM, SMEM, SMEM, SMEM, VMEM),
+        scratch_shapes=[
+            pltpu.VMEM((devices, ROWS, HALF), F32),
+            pltpu.VMEM((3 * CL, CS, HALF), F32),
+            pltpu.VMEM((3 * CL, CS, HALF), F32),
+            pltpu.VMEM((2 * devices + 8, HALF), F32),
+            pltpu.SMEM((devices, 1, HALF), F32),
+            pltpu.SMEM((3 * CL,), jnp.int32),
+            pltpu.SemaphoreType.DMA((PIECES + 1,)),
+        ],
+        name="first_tiles",
+    )(moved, left, left2, start_g, start)
+    return out[0], out[1], out[2:5], out[5]
 
 
 def log_sum(values):
@@ -463,87 +502,147 @@
     return peak + jnp.log(total) * LOG2E
 
 
-def fresh(total, bias, weight, half, potential):
-    log_total = LN2 * (total - bias) - half / EPSILON
-    value = 0.5 * (potential - DAMPING * EPSILON * log_total)
+def fresh(total, weight, half, potential):
+    value = 0.5 * (potential - DAMPING * EPSILON * (LN2 * total - half / EPSILON))
     return jnp.where(weight > REAL, value, 0.0)
 
 
-def update_g_kernel(cols_local, cols_moved, weight, half, bias, potential, new, *new_bias):
-    side = slice(2 * CL, 4 * CL)
-    span = slice(0, 2 * CL)
-    total = log_sum([cols_local[span, :], cols_moved[span, :]])
-    value = fresh(total, bias[...], weight[side, :], half[side, :], potential[...])
+def update_g_kernel(cols_local, cols_moved, weight, half, start_g, new, new_bias):
+    side, span = slice(SPAN, 2 * SPAN), slice(0, SPAN)
+    total = log_sum([cols_local[span, :], cols_moved[span, :]]) - start_g[...]
+    value = fresh(total, weight[side, :], half[side, :], 0.0)
     new[...] = value
-    for ref in new_bias:
-        ref[...] = bias_of(weight[side, :], half[side, :], value)
-
-
-def update_g(last, *args):
-    vmem = pl.BlockSpec(memory_space=pltpu.VMEM)
-    shapes = (jax.ShapeDtypeStruct((2 * CL, HALF), F32),) * (1 if last else 2)
+    new_bias[...] = bias_of(weight[side, :], half[side, :], value)
+
+
+def update_g(*args):
     return pl.pallas_call(
         update_g_kernel,
-        out_shape=shapes,
-        in_specs=[vmem] * 6,
-        out_specs=(vmem,) * len(shapes),
+        out_shape=(shape(SPAN, HALF),) * 2,
+        in_specs=[VMEM] * 5,
+        out_specs=(VMEM,) * 2,
         name="update_g",
     )(*args)
 
 
-def update_kernel(
-    last, cross, xself, yself, back, cols_local, cols_moved, log_own, weight, half, potential, bias, *refs
-):
-    if last:
-        *new, parts = refs
+def step_kernel(has_columns, has_rows, *refs):
+    refs = list(refs)
+    take = lambda n: [refs.pop(0) for _ in range(n)]
+    cross, xself, yself, slots, targets, bounds, moved = take(7)
+    inbox, cols_local, log_own, cols_moved, weight, half, start_g, start, left = take(9)
+    if has_columns:
+        listed = cols_moved
+        bias_g, bias, potential_g, potential, left2_start = take(5)
     else:
-        new, new_bias, message, parts = refs
+        bias = start
+        (new_bias_g,) = take(1)
+    if not has_rows:
+        new_f, new_g, new_p, new_q = take(4)
+    else:
+        new_g, new_bias_g = take(2) if has_columns else (None, new_bias_g)
+        new, new_bias, outbox = take(3)
+    held, parts, sems = take(3)
+    if has_columns:
+        acc, top, cols_moved = take(3)
+    if has_rows:
+        left2, sums = take(2)
+    devices = moved.shape[0]
+    fetch = fetch_all(moved, held, sems)
     counts = (cross.shape[1], xself.shape[0], yself.shape[0])
     offsets = (0, counts[0], counts[0] + counts[1])
     requests = list(lists(cross, xself, yself))
-    for kind, c, k, named in requests:
-        at = pl.multiple_of(2 * (named // CL), 2)
-        parts[offsets[kind] + k, 2 * c : 2 * c + 2, :] = back[pl.ds(at, 2), :]
-    span = 2 * CL
-    answers = [[parts[offsets[t] + k] for k in range(counts[t])] for t in range(3)]
-    p, q = slice(span, 2 * span), slice(2 * span, 3 * span)
-    totals = (
-        log_sum([log_own[...]] + answers[0]),
-        log_sum([cols_local[p, :], cols_moved[p, :]] + answers[1]),
-        log_sum([cols_local[q, :], cols_moved[q, :]] + answers[2]),
-    )
+    width = inbox.shape[0] // devices
+    for kind, c, k, wanted in requests:
+        at = pl.multiple_of(width * (wanted // CL), width)
+        parts[offsets[kind] + k, 2 * c : 2 * c + 2, :] = inbox[pl.ds(at, 2), :]
+    if has_rows:
+        sums[...] = jnp.ones_like(sums)
+    tiles = Tiles(held, left, slots, targets, bounds)
+    if has_columns:
+        acc[...] = jnp.zeros_like(acc)
+        column_pass(
+            tiles, left2_start, inbox, fetch, acc, top, cols_moved, start_g, start, listed[...] > 0
+        )
+    f, p, q = (slice(i * SPAN, (i + 1) * SPAN) for i in range(3))
+    answers = [
+        [parts[offsets[t] + k] - start[t * SPAN : (t + 1) * SPAN, :] for k in range(counts[t])]
+        for t in range(3)
+    ]
+    totals = [log_sum([log_own[...] - bias[f, :]] + answers[0])]
+    for here, answer in ((p, answers[1]), (q, answers[2])):
+        totals.append(
+            log_sum([cols_local[here, :] - bias[here, :], cols_moved[here, :] - start[here, :]] + answer)
+        )
     for i, total in enumerate(totals):
-        here = slice(i * span, (i + 1) * span)
-        side = slice(span, 2 * span) if i == 2 else slice(0, span)
-        value = fresh(total, bias[here, :], weight[side, :], half[side, :], potential[here, :])
-        if last:
-            new[i][...] = value
-        else:
+        here = (f, p, q)[i]
+        side = slice(SPAN, 2 * SPAN) if i == 2 else slice(0, SPAN)
+        before = potential[here, :] if has_columns else 0.0
+        value = fresh(total, weight[side, :], half[side, :], before)
+        if has_rows:
             new[here, :] = value
             new_bias[here, :] = bias_of(weight[side, :], half[side, :], value)
-    if last:
+        else:
+            (new_f, new_p, new_q)[i][...] = value
+    if has_columns:
+        side = slice(SPAN, 2 * SPAN)
+        total = log_sum([cols_local[f, :] - bias_g[...], cols_moved[f, :] - start_g[...]])
+        value = fresh(total, weight[side, :], half[side, :], potential_g[...])
+        new_g[...] = value
+        if has_rows:
+            new_bias_g[...] = bias_of(weight[side, :], half[side, :], value)
+    if not has_rows:
         return
-    for kind, c, _, named in requests:
-        at = pl.multiple_of(2 * (named // CL), 2)
-        base = kind * span + 2 * c
-        message[pl.ds(at, 2), :] = new_bias[base : base + 2, :]
-
-
-def update(last, cross, xself, yself, back, *args):
-    smem = pl.BlockSpec(memory_space=pltpu.SMEM)
-    vmem = pl.BlockSpec(memory_space=pltpu.VMEM)
-    one = jax.ShapeDtypeStruct((2 * CL, HALF), F32)
-    three = jax.ShapeDtypeStruct((6 * CL, HALF), F32)
-    shapes = (one,) * 3 if last else (three, three, jax.ShapeDtypeStruct(back.shape, F32))
-    listed = cross.shape[1] + xself.shape[0] + yself.shape[0]
+    for kind, c, _, wanted in requests:
+        at = pl.multiple_of(4 * (wanted // CL) + 2, 2)
+        base = kind * SPAN + 2 * c
+        outbox[pl.ds(at, 2), :] = new_bias[base : base + 2, :]
+    build_left2(left, new_bias_g, new_bias, left2)
+
+    def fast(z, a, te, spot):
+        put_row(sums, 4 * spot, row_sum(jnp.exp2(z), a))
+
+    def slow(z, a, te, spot):
+        put_row(sums, 4 * spot, row_log_sum(z))
+
+    tiles.sweep(left2, None, fast, None if has_columns else fetch)
+    within = in_range(sums[...])
+    answer_row = lax.broadcasted_iota(jnp.int32, outbox.shape, 0) % 4 < 2
+
+    @pl.when(within)
+    def _():
+        outbox[...] = jnp.where(answer_row, jnp.log(sums[0 : 4 * devices, :]) * LOG2E, outbox[...])
+
+    @pl.when(jnp.logical_not(within))
+    def _():
+        tiles.slow_sweep(left2, None, slow)
+        outbox[...] = jnp.where(answer_row, sums[0 : 4 * devices, :], outbox[...])
+
+
+def step(has_columns, has_rows, tables, index, moved, *args):
+    devices = moved.shape[0]
+    listed = tables[0].shape[1] + tables[1].shape[0] + tables[2].shape[0]
+    one, three = shape(SPAN, HALF), shape(3 * SPAN, HALF)
+    if has_rows:
+        outs = ([one, one] if has_columns else []) + [three, three, shape(4 * devices, HALF)]
+    else:
+        outs = [one] * 4
+    scratch = [
+        pltpu.VMEM((devices, ROWS, HALF), F32),
+        pltpu.VMEM((listed, SPAN, HALF), F32),
+        pltpu.SemaphoreType.DMA((PIECES,)),
+    ]
+    if has_columns:
+        scratch += [pltpu.VMEM((3 * CL, CS, HALF), F32)] * 2 + [pltpu.VMEM((3 * SPAN, HALF), F32)]
+    if has_rows:
+        scratch += [pltpu.VMEM((3 * CL, CS, HALF), BF16), pltpu.VMEM((4 * devices + 8, HALF), F32)]
     return pl.pallas_call(
-        functools.partial(update_kernel, last),
-        out_shape=shapes,
-        in_specs=[smem] * 3 + [vmem] * 8,
-        out_specs=(vmem,) * len(shapes),
-        scratch_shapes=[pltpu.VMEM((listed, 2 * CL, HALF), F32)],
-        name="update",
-    )(cross, xself, yself, back, *args)
+        functools.partial(step_kernel, has_columns, has_rows),
+        out_shape=outs,
+        in_specs=[SMEM] * 6 + [HBM] + [VMEM] * len(args),
+        out_specs=[VMEM] * len(outs),
+        scratch_shapes=scratch,
+        name="step_" + "c" * has_columns + "r" * has_rows,
+    )(*tables, *index, moved, *args)
 
 
 def exchange(blocks):
@@ -551,36 +650,39 @@
 
 
 def exchange_rows(rows, devices):
-    return exchange(rows.reshape(devices, 2, HALF)).reshape(2 * devices, HALF)
+    wide = rows.reshape(devices, rows.shape[0] // devices, HALF)
+    return exchange(wide).reshape(rows.shape)
 
 
 def local(x, y, x_logmass, y_logmass, x_sizes, y_sizes, cross, xself, yself):
     devices = lax.axis_size(AXES)
-    xself, yself = xself.T, yself.T
-    send, weight, half, bias_g, bias = push(
-        cross, xself, yself, x_sizes, y_sizes, x, y,
-        x_logmass.reshape(2 * CL, HALF), y_logmass.reshape(2 * CL, HALF), devices,
+    tables = (cross, xself.T, yself.T)
+    send, weight, half, start_g, start = push(
+        *tables, x_sizes, y_sizes, x, y,
+        x_logmass.reshape(SPAN, HALF), y_logmass.reshape(SPAN, HALF), devices,
     )
     moved = exchange(send)
     left, right = left_side(x, y)
-    potential_g = jnp.zeros((2 * CL, HALF), F32)
-    potential = jnp.zeros((6 * CL, HALF), F32)
-    message = index = None
-    for iteration in range(ITERS):
+    left2, cols_local, log_own = local_tiles(left, right, start_g, start)
+    back, cols_moved, index, listed = first_tiles(moved, left, left2, start_g, start)
+    inbox = exchange_rows(back, devices)
+    potential_g, bias_g = update_g(cols_local, cols_moved, weight, half, start_g)
+    potential, bias, outbox = step(
+        False, True, tables, index, moved,
+        inbox, cols_local, log_own, cols_moved, weight, half, start_g, start, left, bias_g,
+    )
+    for iteration in range(1, ITERS):
         last = iteration == ITERS - 1
-        left2, cols_local, log_own = local_tiles(left, right, bias_g, bias)
-        back, cols_moved, index = tiles(moved, message, left, left2, bias_g, bias, index)
-        back = exchange_rows(back, devices)
-        out_g = update_g(last, cols_local, cols_moved, weight, half, bias_g, potential_g)
-        out = update(
-            last, cross, xself, yself, back, cols_local, cols_moved, log_own, weight, half, potential, bias
+        inbox = exchange_rows(outbox, devices)
+        _, cols_local, log_own = local_tiles(left, right, bias_g, bias)
+        out = step(
+            True, not last, tables, index, moved,
+            inbox, cols_local, log_own, listed, weight, half, start_g, start, left,
+            bias_g, bias, potential_g, potential, left2,
         )
         if not last:
-            potential_g, bias_g = out_g
-            potential, bias, message = out
-            message = exchange_rows(message, devices)
-    f, p, q = out
-    return tuple(part.reshape(2 * CL * HALF) for part in (f, out_g[0], p, q))
+            potential_g, bias_g, potential, bias, outbox = out
+    return tuple(part.reshape(SPAN * HALF) for part in out)
 
 
 def solution(mesh):

time: 335 us -> 418 us (1.25)
  Pallas kernels: 157 us -> 263 us
  blocking collectives: 45 us -> 0 us
  starting transfers between devices: 30.6 us -> 53.2 us
    pallas_call x9 -> x5, Pallas kernels: 107 us -> 213 us  [the longest x3 162 us: step(): pl.pallas_call(functools.partial(step_kernel, has_columns, has_rows), out...]
    all_to_all x2 -> x0, blocking collectives: 45 us -> none  [exchange(): return lax.all_to_all(blocks, AXES, split_axis=0, concat_axis=0, tiled=True)]
    all_to_all x4, starting transfers between devices: 30.6 us -> 53.2 us  [exchange(): return lax.all_to_all(blocks, AXES, split_axis=0, concat_axis=0, tiled=True)]
  transfers between devices with their start and end apart: 4 -> 4, of which waited for: 2 -> 2; matrix products, arithmetic and copies ran while one was open for 0% -> 0% of each run, Pallas kernels for 15% -> 11%
where the time goes in v3:
time: 418 us; the launch traced here: 416 us
  Pallas kernels  263 us (63%)
  waiting for transfers between devices  96.7 us (23%)
  starting transfers between devices  53.2 us (13%)
    pallas_call x3, Pallas kernels, step(): pl.pallas_call(functools.partial(step_kernel, has_columns, has_rows), out...  162 us
    all_to_all x4, waiting for transfers between devices, exchange(): return lax.all_to_all(blocks, AXES, split_axis=0, concat_axis=0, tiled=True)  96.7 us
    all_to_all x4, starting transfers between devices, exchange(): return lax.all_to_all(blocks, AXES, split_axis=0, concat_axis=0, tiled=True)  53.2 us
    pallas_call x1, Pallas kernels, first_tiles(): pl.pallas_call(first_kernel, out_shape=(shape(2 * devices, HALF), shape(3...  50 us
    pallas_call x3, Pallas kernels, local_tiles(): pl.pallas_call(local_kernel, out_shape=(jax.ShapeDtypeStruct((3 * CL, CS,...  41.7 us
  transfers between devices with their start and end apart: 4, of which 2 were waited for; matrix products, arithmetic and copies ran while one was open for 0% of the time, Pallas kernels for 11%

profile of v3, /device:TPU:1, one launch (start us, length us, event | category | flops | bytes accessed | tf_op | source)
XLA Modules:
  0.0 415.5 jit_solution(12634580558293556191)
XLA Ops:
  0.6 4.5 %push.1 = (f32[128,136,128]{2,1,0:T(8,128)}, f32[32,128]{1,0:T(8,128)}, f32[32,128]{1,0:T(8,128)}, f32[16,128]{1,0:T(8,128)}, f32[48,128]{1,0:T(8,128)}) custom-call(s32[8,7]{1,0:T(8,128)} %refs_0_.5, s32[2,8]{1,0:T(2,128)} %bitcast.20, s32[2,8]{1,0:T(2,128)} %bitcast.24, s32[1,8]{1,0:T(1,128)} %x_sizes.1, s32[1,8]{1,0:T(1,128)} %y_sizes.1, ...), custom_call_target="tpu_custom_call" | custom-call | tf_op jit(solution)/shard_map/push/pallas_call | solution.py:97
  5.2 11.9 %all-to-all-start = ((f32[128,136,128]{2,1,0:T(8,128)}), f32[128,136,128]{2,1,0:T(8,128)}, u32[]{:S(2)}, u32[]{:S(2)}) async-start(f32[128,136,128]{2,1,0:T(8,128)} %get-tuple-element.38), calls=%async_computation | async-start | bytes 17825792 | tf_op jit(solution)/shard_map/all_to_all | solution.py:649
  17.1 3.3 left_side.1
  20.4 13.9 %local_tiles.3 = (bf16[24,256,128]{2,1,0:T(8,128)(2,1)}, f32[48,128]{1,0:T(8,128)}, f32[16,128]{1,0:T(8,128)}) custom-call(bf16[16,256,256]{2,1,0:T(8,128)(2,1)} %get-tuple-element.39.left.refs_15_, bf16[16,128,256]{2,1,0:T(8,128)(2,1)} %get-tuple-element.40.right, f32[16,128]{1,0:T(8,128)} %get-tuple-element.41.bias_g.start_g.refs_13_, ...), custom_call_target="tpu_custom_call" | custom-call | tf_op jit(solution)/shard_map/local_tiles/pallas_call | solution.py:300
  34.3 88.1 %all-to-all-done.moved.refs_6_ = f32[128,136,128]{2,1,0:T(8,128)} async-done(((f32[128,136,128]{2,1,0:T(8,128)}), f32[128,136,128]{2,1,0:T(8,128)}, u32[]{:S(2)}, u32[]{:S(2)}) %all-to-all-start) | async-done | bytes 8912928 | tf_op jit(solution)/shard_map/all_to_all | solution.py:649
  122.4 50.0 %first_tiles.1 = (f32[256,128]{1,0:T(8,128)}, f32[48,128]{1,0:T(8,128)}, s32[136]{0:T(256)}, s32[136]{0:T(256)}, s32[128]{0:T(128)}, /*index=5*/s32[48,128]{1,0:T(8,128)}) custom-call(f32[128,136,128]{2,1,0:T(8,128)} %all-to-all-done.moved.refs_6_, bf16[16,256,256]{2,1,0:T(8,128)(2,1)} %get-tuple-element.39.left.refs_15_, ...), custom_call_target="tpu_custom_call" | custom-call | tf_op jit(solution)/shard_map/first_tiles/pallas_call | solution.py:473
  172.4 17.9 %all-to-all-start.1 = ((f32[128,2,128]{2,1,0:T(2,128)}), f32[128,2,128]{2,1,0:T(2,128)S(1)}, u32[]{:S(2)}, u32[]{:S(2)}) async-start(f32[128,2,128]{2,1,0:T(2,128)} %bitcast.19), calls=%async_computation.1 | async-start | bytes 262144 | tf_op jit(solution)/shard_map/all_to_all | solution.py:649
  190.3 1.4 update_g.1
  191.7 8.6 %all-to-all-done.1 = f32[128,2,128]{2,1,0:T(2,128)S(1)} async-done(((f32[128,2,128]{2,1,0:T(2,128)}), f32[128,2,128]{2,1,0:T(2,128)S(1)}, u32[]{:S(2)}, u32[]{:S(2)}) %all-to-all-start.1) | async-done | bytes 131104 | tf_op jit(solution)/shard_map/all_to_all | solution.py:649
  200.3 0.0 copy-start.2
  200.3 0.7 copy-done.2
  201.0 35.1 %step_r.1 = (f32[48,128]{1,0:T(8,128)}, f32[48,128]{1,0:T(8,128)}, f32[512,128]{1,0:T(8,128)}) custom-call(s32[8,7]{1,0:T(8,128)} %refs_0_.5, s32[2,8]{1,0:T(2,128)} %bitcast.21, s32[2,8]{1,0:T(2,128)} %bitcast.25, s32[136]{0:T(256)} %get-tuple-element.44.refs_3_, s32[136]{0:T(256)} %get-tuple-element.45.refs_4_, s32[128]{0:T(128)} %get-tuple-element.46.refs_5_, ...), custom_call_target="tpu_custom_call" | custom-call | tf_op jit(solution)/shard_map/step_r/pallas_call | solution.py:638
  236.1 7.1 %all-to-all-start.2 = ((f32[128,4,128]{2,1,0:T(4,128)}), f32[128,4,128]{2,1,0:T(4,128)S(1)}, u32[]{:S(2)}, u32[]{:S(2)}) async-start(f32[128,4,128]{2,1,0:T(4,128)} %bitcast.18), calls=%async_computation.2 | async-start | bytes 524288 | tf_op jit(solution)/shard_map/all_to_all | solution.py:649
  243.2 13.9 %local_tiles.4 = (bf16[24,256,128]{2,1,0:T(8,128)(2,1)}, f32[48,128]{1,0:T(8,128)}, f32[16,128]{1,0:T(8,128)}) custom-call(bf16[16,256,256]{2,1,0:T(8,128)(2,1)} %get-tuple-element.39.left.refs_15_, bf16[16,128,256]{2,1,0:T(8,128)(2,1)} %get-tuple-element.40.right, f32[16,128]{1,0:T(8,128)} %get-tuple-element.53.refs_16_.bias_g, ...), custom_call_target="tpu_custom_call" | custom-call | tf_op jit(solution)/shard_map/local_tiles/pallas_call | solution.py:300
  257.1 0.0 all-to-all-done.2
  257.1 0.0 copy-start.1
  257.1 0.7 copy-done.1
  257.8 78.7 %step_cr.1 = (f32[16,128]{1,0:T(8,128)}, f32[16,128]{1,0:T(8,128)}, f32[48,128]{1,0:T(8,128)}, f32[48,128]{1,0:T(8,128)}, f32[512,128]{1,0:T(8,128)}) custom-call(s32[8,7]{1,0:T(8,128)} %refs_0_.5, s32[2,8]{1,0:T(2,128)} %bitcast.22, s32[2,8]{1,0:T(2,128)} %bitcast.26, s32[136]{0:T(256)} %get-tuple-element.44.refs_3_, s32[136]{0:T(256)} %get-tuple-element.45.refs_4_, ...), custom_call_target="tpu_custom_call" | custom-call | tf_op jit(solution)/shard_map/step_cr/pallas_call | solution.py:638
  336.5 16.3 %all-to-all-start.3 = ((f32[128,4,128]{2,1,0:T(4,128)}), f32[128,4,128]{2,1,0:T(4,128)S(1)}, u32[]{:S(2)}, u32[]{:S(2)}) async-start(f32[128,4,128]{2,1,0:T(4,128)} %bitcast.17), calls=%async_computation.3 | async-start | bytes 524288 | tf_op jit(solution)/shard_map/all_to_all | solution.py:649
  352.8 13.9 %local_tiles.5 = (bf16[24,256,128]{2,1,0:T(8,128)(2,1)}, f32[48,128]{1,0:T(8,128)}, f32[16,128]{1,0:T(8,128)}) custom-call(bf16[16,256,256]{2,1,0:T(8,128)(2,1)} %get-tuple-element.39.left.refs_15_, bf16[16,128,256]{2,1,0:T(8,128)(2,1)} %get-tuple-element.40.right, f32[16,128]{1,0:T(8,128)} %get-tuple-element.62.bias_g.refs_16_, ...), custom_call_target="tpu_custom_call" | custom-call | tf_op jit(solution)/shard_map/local_tiles/pallas_call | solution.py:300
  366.7 0.0 all-to-all-done.3
  366.7 0.0 copy-start
  366.7 0.7 copy-done
  367.4 47.9 %step_c.1 = (f32[16,128]{1,0:T(8,128)}, f32[16,128]{1,0:T(8,128)}, f32[16,128]{1,0:T(8,128)}, f32[16,128]{1,0:T(8,128)}) custom-call(s32[8,7]{1,0:T(8,128)} %refs_0_.5, s32[2,8]{1,0:T(2,128)} %bitcast.23, s32[2,8]{1,0:T(2,128)} %bitcast.27, s32[136]{0:T(256)} %get-tuple-element.44.refs_3_, s32[136]{0:T(256)} %get-tuple-element.45.refs_4_, ...), custom_call_target="tpu_custom_call" | custom-call | tf_op jit(solution)/shard_map/step_c/pallas_call | solution.py:638
Async XLA Ops:
  5.2 117.3 %all-to-all-start = ((f32[128,136,128]{2,1,0:T(8,128)}), f32[128,136,128]{2,1,0:T(8,128)}, u32[]{:S(2)}, u32[]{:S(2)}) async-start(f32[128,136,128]{2,1,0:T(8,128)} %get-tuple-element.38), calls=%async_computation | async-start | bytes 17825792 | tf_op jit(solution)/shard_map/all_to_all | solution.py:649
  172.4 27.9 %all-to-all-start.1 = ((f32[128,2,128]{2,1,0:T(2,128)}), f32[128,2,128]{2,1,0:T(2,128)S(1)}, u32[]{:S(2)}, u32[]{:S(2)}) async-start(f32[128,2,128]{2,1,0:T(2,128)} %bitcast.19), calls=%async_computation.1 | async-start | bytes 262144 | tf_op jit(solution)/shard_map/all_to_all | solution.py:649
  200.3 0.7 copy-start.2
  236.1 21.0 %all-to-all-start.2 = ((f32[128,4,128]{2,1,0:T(4,128)}), f32[128,4,128]{2,1,0:T(4,128)S(1)}, u32[]{:S(2)}, u32[]{:S(2)}) async-start(f32[128,4,128]{2,1,0:T(4,128)} %bitcast.18), calls=%async_computation.2 | async-start | bytes 524288 | tf_op jit(solution)/shard_map/all_to_all | solution.py:649
  257.1 0.7 copy-start.1
  336.5 30.2 %all-to-all-start.3 = ((f32[128,4,128]{2,1,0:T(4,128)}), f32[128,4,128]{2,1,0:T(4,128)S(1)}, u32[]{:S(2)}, u32[]{:S(2)}) async-start(f32[128,4,128]{2,1,0:T(4,128)} %bitcast.17), calls=%async_computation.3 | async-start | bytes 524288 | tf_op jit(solution)/shard_map/all_to_all | solution.py:649
  366.7 0.7 copy-start

commit v4 on v3

--- a/solution.py
+++ b/solution.py
@@ -327,6 +327,13 @@
     return fetch
 
 
+def bring(pairs, sems, base):
+    copies = [pltpu.make_async_copy(a, b, sems.at[base + i]) for i, (a, b) in enumerate(pairs)]
+    for copy in copies:
+        copy.start()
+    return copies
+
+
 class Tiles:
     def __init__(self, held, left, slots, targets, bounds):
         self.held, self.left = held, left
@@ -411,12 +418,13 @@
 
 
 def first_kernel(
-    moved, left, left2, start_g, start, back, log_cols, slots, targets, bounds, listed,
-    held, acc, top, sums, codes, count, sems,
+    moved, left_hbm, left2_hbm, start_g, start, back, log_cols, slots, targets, bounds, listed,
+    held, acc, top, sums, codes, count, sems, left, left2,
 ):
     devices = moved.shape[0]
     tags = pltpu.make_async_copy(moved.at[:, pl.ds(2 * D + 2, 1), :], codes, sems.at[PIECES])
     tags.start()
+    sides = bring(((left_hbm, left), (left2_hbm, left2)), sems, PIECES + 1)
     fetch = fetch_all(moved, held, sems)
     acc[...] = jnp.zeros_like(acc)
     sums[...] = jnp.ones_like(sums)
@@ -448,6 +456,8 @@
         targets[live + i] = 0
     tiles = Tiles(held, left, slots, targets, bounds)
     named = some_listed > 0
+    for copy in sides:
+        copy.wait()
     within = column_pass(tiles, left2, None, fetch, acc, top, log_cols, start_g, start, named, sums)
 
     @pl.when(within)
@@ -480,7 +490,7 @@
             shape(devices, dtype=jnp.int32),
             shape(3 * SPAN, HALF, dtype=jnp.int32),
         ),
-        in_specs=[HBM] + [VMEM] * 4,
+        in_specs=[HBM] * 3 + [VMEM] * 2,
         out_specs=(VMEM, VMEM, SMEM, SMEM, SMEM, VMEM),
         scratch_shapes=[
             pltpu.VMEM((devices, ROWS, HALF), F32),
@@ -489,7 +499,9 @@
             pltpu.VMEM((2 * devices + 8, HALF), F32),
             pltpu.SMEM((devices, 1, HALF), F32),
             pltpu.SMEM((3 * CL,), jnp.int32),
-            pltpu.SemaphoreType.DMA((PIECES + 1,)),
+            pltpu.SemaphoreType.DMA((PIECES + 3,)),
+            pltpu.VMEM((2 * CL, CS, CS), BF16),
+            pltpu.VMEM((3 * CL, CS, HALF), BF16),
         ],
         name="first_tiles",
     )(moved, left, left2, start_g, start)
@@ -529,24 +541,26 @@
     refs = list(refs)
     take = lambda n: [refs.pop(0) for _ in range(n)]
     cross, xself, yself, slots, targets, bounds, moved = take(7)
-    inbox, cols_local, log_own, cols_moved, weight, half, start_g, start, left = take(9)
+    inbox, cols_local, log_own, cols_moved, weight, half, start_g, start = take(8)
     if has_columns:
         listed = cols_moved
-        bias_g, bias, potential_g, potential, left2_start = take(5)
+        bias_g, bias, potential_g, potential, left_hbm, left2_hbm = take(6)
     else:
         bias = start
-        (new_bias_g,) = take(1)
+        new_bias_g, left_hbm = take(2)
     if not has_rows:
         new_f, new_g, new_p, new_q = take(4)
     else:
         new_g, new_bias_g = take(2) if has_columns else (None, new_bias_g)
         new, new_bias, outbox = take(3)
-    held, parts, sems = take(3)
+    held, parts, sems, left = take(4)
     if has_columns:
-        acc, top, cols_moved = take(3)
+        acc, top, cols_moved, left2_start = take(4)
     if has_rows:
         left2, sums = take(2)
     devices = moved.shape[0]
+    pairs = ((left_hbm, left), (left2_hbm, left2_start)) if has_columns else ((left_hbm, left),)
+    sides = bring(pairs, sems, PIECES)
     fetch = fetch_all(moved, held, sems)
     counts = (cross.shape[1], xself.shape[0], yself.shape[0])
     offsets = (0, counts[0], counts[0] + counts[1])
@@ -560,6 +574,9 @@
     tiles = Tiles(held, left, slots, targets, bounds)
     if has_columns:
         acc[...] = jnp.zeros_like(acc)
+    for copy in sides:
+        copy.wait()
+    if has_columns:
         column_pass(
             tiles, left2_start, inbox, fetch, acc, top, cols_moved, start_g, start, listed[...] > 0
         )
@@ -622,6 +639,7 @@
     devices = moved.shape[0]
     listed = tables[0].shape[1] + tables[1].shape[0] + tables[2].shape[0]
     one, three = shape(SPAN, HALF), shape(3 * SPAN, HALF)
+    sides = 2 if has_columns else 1
     if has_rows:
         outs = ([one, one] if has_columns else []) + [three, three, shape(4 * devices, HALF)]
     else:
@@ -629,16 +647,18 @@
     scratch = [
         pltpu.VMEM((devices, ROWS, HALF), F32),
         pltpu.VMEM((listed, SPAN, HALF), F32),
-        pltpu.SemaphoreType.DMA((PIECES,)),
+        pltpu.SemaphoreType.DMA((PIECES + 2,)),
+        pltpu.VMEM((2 * CL, CS, CS), BF16),
     ]
     if has_columns:
-        scratch += [pltpu.VMEM((3 * CL, CS, HALF), F32)] * 2 + [pltpu.VMEM((3 * SPAN, HALF), F32)]
+        scratch += [pltpu.VMEM((3 * CL, CS, HALF), F32)] * 2
+        scratch += [pltpu.VMEM((3 * SPAN, HALF), F32), pltpu.VMEM((3 * CL, CS, HALF), BF16)]
     if has_rows:
         scratch += [pltpu.VMEM((3 * CL, CS, HALF), BF16), pltpu.VMEM((4 * devices + 8, HALF), F32)]
     return pl.pallas_call(
         functools.partial(step_kernel, has_columns, has_rows),
         out_shape=outs,
-        in_specs=[SMEM] * 6 + [HBM] + [VMEM] * len(args),
+        in_specs=[SMEM] * 6 + [HBM] + [VMEM] * (len(args) - sides) + [HBM] * sides,
         out_specs=[VMEM] * len(outs),
         scratch_shapes=scratch,
         name="step_" + "c" * has_columns + "r" * has_rows,
@@ -651,7 +671,7 @@
 
 def exchange_rows(rows, devices):
     wide = rows.reshape(devices, rows.shape[0] // devices, HALF)
-    return exchange(wide).reshape(rows.shape)
+    return pltpu.with_memory_space_constraint(exchange(wide).reshape(rows.shape), pltpu.VMEM)
 
 
 def local(x, y, x_logmass, y_logmass, x_sizes, y_sizes, cross, xself, yself):
@@ -669,7 +689,7 @@
     potential_g, bias_g = update_g(cols_local, cols_moved, weight, half, start_g)
     potential, bias, outbox = step(
         False, True, tables, index, moved,
-        inbox, cols_local, log_own, cols_moved, weight, half, start_g, start, left, bias_g,
+        inbox, cols_local, log_own, cols_moved, weight, half, start_g, start, bias_g, left,
     )
     for iteration in range(1, ITERS):
         last = iteration == ITERS - 1
@@ -677,8 +697,8 @@
         _, cols_local, log_own = local_tiles(left, right, bias_g, bias)
         out = step(
             True, not last, tables, index, moved,
-            inbox, cols_local, log_own, listed, weight, half, start_g, start, left,
-            bias_g, bias, potential_g, potential, left2,
+            inbox, cols_local, log_own, listed, weight, half, start_g, start,
+            bias_g, bias, potential_g, potential, left, left2,
         )
         if not last:
             potential_g, bias_g, potential, bias, outbox = out

time: 418 us -> 410 us (0.981)
  Pallas kernels: 263 us -> 252 us
    pallas_call x3, Pallas kernels: 162 us -> 154 us  [step(): pl.pallas_call(functools.partial(step_kernel, has_columns, has_rows), out...]
where the time goes in v4:
time: 410 us; the launch traced here: 406 us
  Pallas kernels  252 us (61%)
  waiting for transfers between devices  96.7 us (24%)
  starting transfers between devices  56.9 us (14%)
    pallas_call x3, Pallas kernels, step(): pl.pallas_call(functools.partial(step_kernel, has_columns, has_rows), out...  154 us
    all_to_all x4, waiting for transfers between devices, exchange(): return lax.all_to_all(blocks, AXES, split_axis=0, concat_axis=0, tiled=True)  96.7 us
    all_to_all x4, starting transfers between devices, exchange(): return lax.all_to_all(blocks, AXES, split_axis=0, concat_axis=0, tiled=True)  56.9 us
    pallas_call x1, Pallas kernels, first_tiles(): pl.pallas_call(first_kernel, out_shape=(shape(2 * devices, HALF), shape(3...  46.7 us
    pallas_call x3, Pallas kernels, local_tiles(): pl.pallas_call(local_kernel, out_shape=(jax.ShapeDtypeStruct((3 * CL, CS,...  41.7 us
  transfers between devices with their start and end apart: 4, of which 2 were waited for; matrix products, arithmetic and copies ran while one was open for 0% of the time, Pallas kernels for 11%

profile of v4, /device:TPU:1, one launch (start us, length us, event | category | flops | bytes accessed | tf_op | source)
XLA Modules:
  0.0 406.2 jit_solution(9280003146716607870)
XLA Ops:
  0.6 4.6 %push.1 = (f32[128,136,128]{2,1,0:T(8,128)}, f32[32,128]{1,0:T(8,128)}, f32[32,128]{1,0:T(8,128)}, f32[16,128]{1,0:T(8,128)}, f32[48,128]{1,0:T(8,128)}) custom-call(s32[8,7]{1,0:T(8,128)} %refs_0_.5, s32[2,8]{1,0:T(2,128)} %bitcast.20, s32[2,8]{1,0:T(2,128)} %bitcast.24, s32[1,8]{1,0:T(1,128)} %x_sizes.1, s32[1,8]{1,0:T(1,128)} %y_sizes.1, ...), custom_call_target="tpu_custom_call" | custom-call | tf_op jit(solution)/shard_map/push/pallas_call | solution.py:97
  5.3 11.9 %all-to-all-start = ((f32[128,136,128]{2,1,0:T(8,128)}), f32[128,136,128]{2,1,0:T(8,128)}, u32[]{:S(2)}, u32[]{:S(2)}) async-start(f32[128,136,128]{2,1,0:T(8,128)} %get-tuple-element.38), calls=%async_computation | async-start | bytes 17825792 | tf_op jit(solution)/shard_map/all_to_all | solution.py:669
  17.1 3.3 left_side.1
  20.4 13.9 %local_tiles.3 = (bf16[24,256,128]{2,1,0:T(8,128)(2,1)}, f32[48,128]{1,0:T(8,128)}, f32[16,128]{1,0:T(8,128)}) custom-call(bf16[16,256,256]{2,1,0:T(8,128)(2,1)} %get-tuple-element.39.left.left_hbm.refs_16_.refs_19_, bf16[16,128,256]{2,1,0:T(8,128)(2,1)} %get-tuple-element.40.right, f32[16,128]{1,0:T(8,128)} %get-tuple-element.41.bias_g.start_g.refs_13_, ...), custom_call_target="tpu_custom_call" | custom-call | tf_op jit(solution)/shard_map/local_tiles/pallas_call | solution.py:300
  34.4 88.1 %all-to-all-done.moved.refs_6_ = f32[128,136,128]{2,1,0:T(8,128)} async-done(((f32[128,136,128]{2,1,0:T(8,128)}), f32[128,136,128]{2,1,0:T(8,128)}, u32[]{:S(2)}, u32[]{:S(2)}) %all-to-all-start) | async-done | bytes 8912928 | tf_op jit(solution)/shard_map/all_to_all | solution.py:669
  122.5 46.7 %first_tiles.1 = (f32[256,128]{1,0:T(8,128)}, f32[48,128]{1,0:T(8,128)}, s32[136]{0:T(256)}, s32[136]{0:T(256)}, s32[128]{0:T(128)}, /*index=5*/s32[48,128]{1,0:T(8,128)}) custom-call(f32[128,136,128]{2,1,0:T(8,128)} %all-to-all-done.moved.refs_6_, bf16[16,256,256]{2,1,0:T(8,128)(2,1)} %get-tuple-element.39.left.left_hbm.refs_16_.refs_19_, ...), custom_call_target="tpu_custom_call" | custom-call | tf_op jit(solution)/shard_map/first_tiles/pallas_call | solution.py:483
  169.2 19.6 %all-to-all-start.1 = ((f32[128,2,128]{2,1,0:T(2,128)}), f32[128,2,128]{2,1,0:T(2,128)S(1)}, u32[]{:S(2)}, u32[]{:S(2)}) async-start(f32[128,2,128]{2,1,0:T(2,128)} %bitcast.19), calls=%async_computation.1 | async-start | bytes 262144 | tf_op jit(solution)/shard_map/all_to_all | solution.py:669
  188.8 1.4 update_g.1
  190.2 8.6 %all-to-all-done.1 = f32[128,2,128]{2,1,0:T(2,128)S(1)} async-done(((f32[128,2,128]{2,1,0:T(2,128)}), f32[128,2,128]{2,1,0:T(2,128)S(1)}, u32[]{:S(2)}, u32[]{:S(2)}) %all-to-all-start.1) | async-done | bytes 131104 | tf_op jit(solution)/shard_map/all_to_all | solution.py:669
  198.8 32.7 %step_r.1 = (f32[48,128]{1,0:T(8,128)}, f32[48,128]{1,0:T(8,128)}, f32[512,128]{1,0:T(8,128)}) custom-call(s32[8,7]{1,0:T(8,128)} %refs_0_.5, s32[2,8]{1,0:T(2,128)} %bitcast.21, s32[2,8]{1,0:T(2,128)} %bitcast.25, s32[136]{0:T(256)} %get-tuple-element.44.refs_3_, s32[136]{0:T(256)} %get-tuple-element.45.refs_4_, s32[128]{0:T(128)} %get-tuple-element.46.refs_5_, ...), custom_call_target="tpu_custom_call" | custom-call | tf_op jit(solution)/shard_map/step_r/pallas_call | solution.py:658
  231.5 7.0 %all-to-all-start.2 = ((f32[128,4,128]{2,1,0:T(4,128)}), f32[128,4,128]{2,1,0:T(4,128)S(1)}, u32[]{:S(2)}, u32[]{:S(2)}) async-start(f32[128,4,128]{2,1,0:T(4,128)} %bitcast.18), calls=%async_computation.2 | async-start | bytes 524288 | tf_op jit(solution)/shard_map/all_to_all | solution.py:669
  238.5 13.9 %local_tiles.4 = (bf16[24,256,128]{2,1,0:T(8,128)(2,1)}, f32[48,128]{1,0:T(8,128)}, f32[16,128]{1,0:T(8,128)}) custom-call(bf16[16,256,256]{2,1,0:T(8,128)(2,1)} %get-tuple-element.39.left.left_hbm.refs_16_.refs_19_, bf16[16,128,256]{2,1,0:T(8,128)(2,1)} %get-tuple-element.40.right, f32[16,128]{1,0:T(8,128)} %get-tuple-element.53.refs_15_.bias_g, ...), custom_call_target="tpu_custom_call" | custom-call | tf_op jit(solution)/shard_map/local_tiles/pallas_call | solution.py:300
  252.4 0.0 all-to-all-done.2
  252.4 75.3 %step_cr.1 = (f32[16,128]{1,0:T(8,128)}, f32[16,128]{1,0:T(8,128)}, f32[48,128]{1,0:T(8,128)}, f32[48,128]{1,0:T(8,128)}, f32[512,128]{1,0:T(8,128)}) custom-call(s32[8,7]{1,0:T(8,128)} %refs_0_.5, s32[2,8]{1,0:T(2,128)} %bitcast.22, s32[2,8]{1,0:T(2,128)} %bitcast.26, s32[136]{0:T(256)} %get-tuple-element.44.refs_3_, s32[136]{0:T(256)} %get-tuple-element.45.refs_4_, ...), custom_call_target="tpu_custom_call" | custom-call | tf_op jit(solution)/shard_map/step_cr/pallas_call | solution.py:658
  327.7 18.4 %all-to-all-start.3 = ((f32[128,4,128]{2,1,0:T(4,128)}), f32[128,4,128]{2,1,0:T(4,128)S(1)}, u32[]{:S(2)}, u32[]{:S(2)}) async-start(f32[128,4,128]{2,1,0:T(4,128)} %bitcast.17), calls=%async_computation.3 | async-start | bytes 524288 | tf_op jit(solution)/shard_map/all_to_all | solution.py:669
  346.1 13.9 %local_tiles.5 = (bf16[24,256,128]{2,1,0:T(8,128)(2,1)}, f32[48,128]{1,0:T(8,128)}, f32[16,128]{1,0:T(8,128)}) custom-call(bf16[16,256,256]{2,1,0:T(8,128)(2,1)} %get-tuple-element.39.left.left_hbm.refs_16_.refs_19_, bf16[16,128,256]{2,1,0:T(8,128)(2,1)} %get-tuple-element.40.right, f32[16,128]{1,0:T(8,128)} %get-tuple-element.62.bias_g.refs_15_, ...), custom_call_target="tpu_custom_call" | custom-call | tf_op jit(solution)/shard_map/local_tiles/pallas_call | solution.py:300
  360.0 0.0 all-to-all-done.3
  360.0 46.0 %step_c.1 = (f32[16,128]{1,0:T(8,128)}, f32[16,128]{1,0:T(8,128)}, f32[16,128]{1,0:T(8,128)}, f32[16,128]{1,0:T(8,128)}) custom-call(s32[8,7]{1,0:T(8,128)} %refs_0_.5, s32[2,8]{1,0:T(2,128)} %bitcast.23, s32[2,8]{1,0:T(2,128)} %bitcast.27, s32[136]{0:T(256)} %get-tuple-element.44.refs_3_, s32[136]{0:T(256)} %get-tuple-element.45.refs_4_, ...), custom_call_target="tpu_custom_call" | custom-call | tf_op jit(solution)/shard_map/step_c/pallas_call | solution.py:658
Async XLA Ops:
  5.3 117.2 %all-to-all-start = ((f32[128,136,128]{2,1,0:T(8,128)}), f32[128,136,128]{2,1,0:T(8,128)}, u32[]{:S(2)}, u32[]{:S(2)}) async-start(f32[128,136,128]{2,1,0:T(8,128)} %get-tuple-element.38), calls=%async_computation | async-start | bytes 17825792 | tf_op jit(solution)/shard_map/all_to_all | solution.py:669
  169.2 29.6 %all-to-all-start.1 = ((f32[128,2,128]{2,1,0:T(2,128)}), f32[128,2,128]{2,1,0:T(2,128)S(1)}, u32[]{:S(2)}, u32[]{:S(2)}) async-start(f32[128,2,128]{2,1,0:T(2,128)} %bitcast.19), calls=%async_computation.1 | async-start | bytes 262144 | tf_op jit(solution)/shard_map/all_to_all | solution.py:669
  231.5 20.9 %all-to-all-start.2 = ((f32[128,4,128]{2,1,0:T(4,128)}), f32[128,4,128]{2,1,0:T(4,128)S(1)}, u32[]{:S(2)}, u32[]{:S(2)}) async-start(f32[128,4,128]{2,1,0:T(4,128)} %bitcast.18), calls=%async_computation.2 | async-start | bytes 524288 | tf_op jit(solution)/shard_map/all_to_all | solution.py:669
  327.7 32.4 %all-to-all-start.3 = ((f32[128,4,128]{2,1,0:T(4,128)}), f32[128,4,128]{2,1,0:T(4,128)S(1)}, u32[]{:S(2)}, u32[]{:S(2)}) async-start(f32[128,4,128]{2,1,0:T(4,128)} %bitcast.17), calls=%async_computation.3 | async-start | bytes 524288 | tf_op jit(solution)/shard_map/all_to_all | solution.py:669

commit v5 on v4

--- a/solution.py
+++ b/solution.py
@@ -222,10 +222,10 @@
     return jnp.logical_and(lowest > TINY, highest < HUGE)
 
 
-def build_left2(left, bias_g, bias, left2):
+def build_left2(left, bias_g, bias, left2, kinds=(0, 1, 2)):
     row8 = lax.broadcasted_iota(jnp.int32, (8, HALF), 0)
     ones = jnp.where(row8 < 3, 1.0, 0.0)
-    for t in range(3):
+    for t in kinds:
         for h in range(2):
             if t == 0:
                 value = bias_g[pl.ds(h, CL, stride=2), :]
@@ -335,11 +335,10 @@
 
 
 class Tiles:
-    def __init__(self, held, left, slots, targets, bounds):
+    def __init__(self, held, left, slots, targets, live, bounds=None):
         self.held, self.left = held, left
-        self.slots, self.targets, self.bounds = slots, targets, bounds
+        self.slots, self.targets, self.live, self.bounds = slots, targets, live, bounds
         self.devices = held.shape[0]
-        self.live = bounds[self.devices - 1]
 
     def run(self, size, left2, inbox, finish):
         held, left = self.held, self.left
@@ -417,6 +416,26 @@
     return within
 
 
+def row_pass(tiles, left2, sums, fetch=None):
+    def fast(z, a, te, spot):
+        put_row(sums, 4 * spot, row_sum(jnp.exp2(z), a))
+
+    def slow(z, a, te, spot):
+        put_row(sums, 4 * spot, row_log_sum(z))
+
+    tiles.sweep(left2, None, fast, fetch)
+    within = in_range(sums[...])
+
+    @pl.when(within)
+    def _():
+        sums[...] = jnp.log(sums[...]) * LOG2E
+
+    @pl.when(jnp.logical_not(within))
+    def _():
+        sums[...] = jnp.zeros_like(sums)
+        tiles.slow_sweep(left2, None, slow)
+
+
 def first_kernel(
     moved, left_hbm, left2_hbm, start_g, start, back, log_cols, slots, targets, bounds, listed,
     held, acc, top, sums, codes, count, sems, left, left2,
@@ -454,7 +473,7 @@
     for i in range(GROUP):
         slots[live + i] = slots[0]
         targets[live + i] = 0
-    tiles = Tiles(held, left, slots, targets, bounds)
+    tiles = Tiles(held, left, slots, targets, live, bounds)
     named = some_listed > 0
     for copy in sides:
         copy.wait()
@@ -519,22 +538,81 @@
     return jnp.where(weight > REAL, value, 0.0)
 
 
-def update_g_kernel(cols_local, cols_moved, weight, half, start_g, new, new_bias):
+def cross_kernel(
+    slots, targets, bounds, moved, left_hbm, cols_local, cols_moved, weight, half, start_g,
+    new, new_bias, partial, self_slots, self_targets, self_bounds,
+    held, left, left2, sums, cross_slots, cross_targets, sems,
+):
+    devices = moved.shape[0]
+    sides = bring(((left_hbm, left),), sems, PIECES)
+    fetch = fetch_all(moved, held, sems)
     side, span = slice(SPAN, 2 * SPAN), slice(0, SPAN)
     total = log_sum([cols_local[span, :], cols_moved[span, :]]) - start_g[...]
     value = fresh(total, weight[side, :], half[side, :], 0.0)
     new[...] = value
     new_bias[...] = bias_of(weight[side, :], half[side, :], value)
 
-
-def update_g(*args):
-    return pl.pallas_call(
-        update_g_kernel,
-        out_shape=(shape(SPAN, HALF),) * 2,
-        in_specs=[VMEM] * 5,
-        out_specs=(VMEM,) * 2,
-        name="update_g",
-    )(*args)
+    def sort(n, found):
+        s, te = slots[n], targets[n]
+        mine = te < CL
+
+        @pl.when(mine)
+        def _():
+            cross_slots[found] = s
+            cross_targets[found] = te
+
+        @pl.when(jnp.logical_not(mine))
+        def _():
+            self_slots[n - found] = s
+            self_targets[n - found] = te
+
+        return found + mine.astype(jnp.int32)
+
+    live = bounds[devices - 1]
+    found = lax.fori_loop(0, live, sort, 0)
+    self_bounds[devices - 1] = live - found
+    for i in range(GROUP):
+        cross_slots[found + i] = cross_slots[0]
+        cross_targets[found + i] = 0
+        self_slots[live - found + i] = self_slots[0]
+        self_targets[live - found + i] = 0
+    sums[...] = jnp.ones_like(sums)
+    for copy in sides:
+        copy.wait()
+    build_left2(left, new_bias, None, left2, (0,))
+    for i in range(PIECES):
+        fetch(i).wait()
+    row_pass(Tiles(held, left, cross_slots, cross_targets, found), left2, sums)
+    partial[...] = sums[0 : 4 * devices, :]
+
+
+def cross_rows(index, moved, left, *args):
+    devices = moved.shape[0]
+    many = devices + GROUP
+    out = pl.pallas_call(
+        cross_kernel,
+        out_shape=(
+            shape(SPAN, HALF),
+            shape(SPAN, HALF),
+            shape(4 * devices, HALF),
+            shape(many, dtype=jnp.int32),
+            shape(many, dtype=jnp.int32),
+            shape(devices, dtype=jnp.int32),
+        ),
+        in_specs=[SMEM] * 3 + [HBM] * 2 + [VMEM] * 5,
+        out_specs=(VMEM,) * 3 + (SMEM,) * 3,
+        scratch_shapes=[
+            pltpu.VMEM((devices, ROWS, HALF), F32),
+            pltpu.VMEM((2 * CL, CS, CS), BF16),
+            pltpu.VMEM((CL, CS, HALF), BF16),
+            pltpu.VMEM((4 * devices + 8, HALF), F32),
+            pltpu.SMEM((many,), jnp.int32),
+            pltpu.SMEM((many,), jnp.int32),
+            pltpu.SemaphoreType.DMA((PIECES + 1,)),
+        ],
+        name="cross_rows",
+    )(*index, moved, left, *args)
+    return out[0], out[1], out[2], out[3:]
 
 
 def step_kernel(has_columns, has_rows, *refs):
@@ -547,7 +625,7 @@
         bias_g, bias, potential_g, potential, left_hbm, left2_hbm = take(6)
     else:
         bias = start
-        new_bias_g, left_hbm = take(2)
+        new_bias_g, partial, left_hbm = take(3)
     if not has_rows:
         new_f, new_g, new_p, new_q = take(4)
     else:
@@ -571,11 +649,14 @@
         parts[offsets[kind] + k, 2 * c : 2 * c + 2, :] = inbox[pl.ds(at, 2), :]
     if has_rows:
         sums[...] = jnp.ones_like(sums)
-    tiles = Tiles(held, left, slots, targets, bounds)
+    tiles = Tiles(held, left, slots, targets, bounds[devices - 1], bounds)
     if has_columns:
         acc[...] = jnp.zeros_like(acc)
     for copy in sides:
         copy.wait()
+    if not has_columns:
+        for i in range(PIECES):
+            fetch(i).wait()
     if has_columns:
         column_pass(
             tiles, left2_start, inbox, fetch, acc, top, cols_moved, start_g, start, listed[...] > 0
@@ -613,26 +694,14 @@
         at = pl.multiple_of(4 * (wanted // CL) + 2, 2)
         base = kind * SPAN + 2 * c
         outbox[pl.ds(at, 2), :] = new_bias[base : base + 2, :]
-    build_left2(left, new_bias_g, new_bias, left2)
-
-    def fast(z, a, te, spot):
-        put_row(sums, 4 * spot, row_sum(jnp.exp2(z), a))
-
-    def slow(z, a, te, spot):
-        put_row(sums, 4 * spot, row_log_sum(z))
-
-    tiles.sweep(left2, None, fast, None if has_columns else fetch)
-    within = in_range(sums[...])
+    build_left2(left, new_bias_g, new_bias, left2, (0, 1, 2) if has_columns else (1, 2))
+
+    row_pass(tiles, left2, sums)
+    answer = sums[0 : 4 * devices, :]
+    if not has_columns:
+        answer = answer + partial[...]
     answer_row = lax.broadcasted_iota(jnp.int32, outbox.shape, 0) % 4 < 2
-
-    @pl.when(within)
-    def _():
-        outbox[...] = jnp.where(answer_row, jnp.log(sums[0 : 4 * devices, :]) * LOG2E, outbox[...])
-
-    @pl.when(jnp.logical_not(within))
-    def _():
-        tiles.slow_sweep(left2, None, slow)
-        outbox[...] = jnp.where(answer_row, sums[0 : 4 * devices, :], outbox[...])
+    outbox[...] = jnp.where(answer_row, answer, outbox[...])
 
 
 def step(has_columns, has_rows, tables, index, moved, *args):
@@ -686,10 +755,12 @@
     left2, cols_local, log_own = local_tiles(left, right, start_g, start)
     back, cols_moved, index, listed = first_tiles(moved, left, left2, start_g, start)
     inbox = exchange_rows(back, devices)
-    potential_g, bias_g = update_g(cols_local, cols_moved, weight, half, start_g)
+    potential_g, bias_g, partial, self_index = cross_rows(
+        index, moved, left, cols_local, cols_moved, weight, half, start_g
+    )
     potential, bias, outbox = step(
-        False, True, tables, index, moved,
-        inbox, cols_local, log_own, cols_moved, weight, half, start_g, start, bias_g, left,
+        False, True, tables, self_index, moved,
+        inbox, cols_local, log_own, cols_moved, weight, half, start_g, start, bias_g, partial, left,
     )
     for iteration in range(1, ITERS):
         last = iteration == ITERS - 1

time: 410 us -> 417 us (1.017)
  Pallas kernels: 252 us -> 268 us
  waiting for transfers between devices: 96.7 us -> 88.1 us
    pallas_call x1, Pallas kernels: 1.41 us -> 25.3 us  [cross_rows(): pl.pallas_call(cross_kernel, out_shape=(shape(SPAN, HALF), shape(SPAN, HA...]
    pallas_call x3, Pallas kernels: 154 us -> 145 us  [step(): pl.pallas_call(functools.partial(step_kernel, has_columns, has_rows), out...]
    all_to_all x4, waiting for transfers between devices: 96.7 us -> 88.1 us  [exchange(): return lax.all_to_all(blocks, AXES, split_axis=0, concat_axis=0, tiled=True)]
  transfers between devices with their start and end apart: 4 -> 4, of which waited for: 2 -> 1; matrix products, arithmetic and copies ran while one was open for 0% -> 0% of each run, Pallas kernels for 11% -> 17%
where the time goes in v5:
time: 417 us; the launch traced here: 411 us
  Pallas kernels  268 us (64%)
  waiting for transfers between devices  88.1 us (21%)
  starting transfers between devices  54.1 us (13%)
    pallas_call x3, Pallas kernels, step(): pl.pallas_call(functools.partial(step_kernel, has_columns, has_rows), out...  145 us
    all_to_all x4, waiting for transfers between devices, exchange(): return lax.all_to_all(blocks, AXES, split_axis=0, concat_axis=0, tiled=True)  88.1 us
    all_to_all x4, starting transfers between devices, exchange(): return lax.all_to_all(blocks, AXES, split_axis=0, concat_axis=0, tiled=True)  54.1 us
    pallas_call x1, Pallas kernels, first_tiles(): pl.pallas_call(first_kernel, out_shape=(shape(2 * devices, HALF), shape(3...  48.7 us
    pallas_call x3, Pallas kernels, local_tiles(): pl.pallas_call(local_kernel, out_shape=(jax.ShapeDtypeStruct((3 * CL, CS,...  41.7 us
    pallas_call x1, Pallas kernels, cross_rows(): pl.pallas_call(cross_kernel, out_shape=(shape(SPAN, HALF), shape(SPAN, HA...  25.3 us
  transfers between devices with their start and end apart: 4, of which 1 were waited for; matrix products, arithmetic and copies ran while one was open for 0% of the time, Pallas kernels for 17%

profile of v5, /device:TPU:1, one launch (start us, length us, event | category | flops | bytes accessed | tf_op | source)
XLA Modules:
  0.0 411.4 jit_solution(15873704334680801900)
XLA Ops:
  0.6 4.6 %push.1 = (f32[128,136,128]{2,1,0:T(8,128)}, f32[32,128]{1,0:T(8,128)}, f32[32,128]{1,0:T(8,128)}, f32[16,128]{1,0:T(8,128)}, f32[48,128]{1,0:T(8,128)}) custom-call(s32[8,7]{1,0:T(8,128)} %refs_0_.5, s32[2,8]{1,0:T(2,128)} %bitcast.20, s32[2,8]{1,0:T(2,128)} %bitcast.24, s32[1,8]{1,0:T(1,128)} %x_sizes.1, s32[1,8]{1,0:T(1,128)} %y_sizes.1, ...), custom_call_target="tpu_custom_call" | custom-call | tf_op jit(solution)/shard_map/push/pallas_call | solution.py:97
  5.2 11.8 %all-to-all-start = ((f32[128,136,128]{2,1,0:T(8,128)}), f32[128,136,128]{2,1,0:T(8,128)}, u32[]{:S(2)}, u32[]{:S(2)}) async-start(f32[128,136,128]{2,1,0:T(8,128)} %get-tuple-element.42), calls=%async_computation | async-start | bytes 17825792 | tf_op jit(solution)/shard_map/all_to_all | solution.py:738
  17.1 3.3 left_side.1
  20.4 13.9 %local_tiles.3 = (bf16[24,256,128]{2,1,0:T(8,128)(2,1)}, f32[48,128]{1,0:T(8,128)}, f32[16,128]{1,0:T(8,128)}) custom-call(bf16[16,256,256]{2,1,0:T(8,128)(2,1)} %get-tuple-element.43.left.left_hbm.refs_17_.refs_19_, bf16[16,128,256]{2,1,0:T(8,128)(2,1)} %get-tuple-element.44.right, f32[16,128]{1,0:T(8,128)} %get-tuple-element.45.bias_g.start_g.refs_13_, ...), custom_call_target="tpu_custom_call" | custom-call | tf_op jit(solution)/shard_map/local_tiles/pallas_call | solution.py:300
  34.3 88.1 %all-to-all-done.moved.refs_6_ = f32[128,136,128]{2,1,0:T(8,128)} async-done(((f32[128,136,128]{2,1,0:T(8,128)}), f32[128,136,128]{2,1,0:T(8,128)}, u32[]{:S(2)}, u32[]{:S(2)}) %all-to-all-start) | async-done | bytes 8912928 | tf_op jit(solution)/shard_map/all_to_all | solution.py:738
  122.4 48.7 %first_tiles.1 = (f32[256,128]{1,0:T(8,128)}, f32[48,128]{1,0:T(8,128)}, s32[136]{0:T(256)}, s32[136]{0:T(256)}, s32[128]{0:T(128)}, /*index=5*/s32[48,128]{1,0:T(8,128)}) custom-call(f32[128,136,128]{2,1,0:T(8,128)} %all-to-all-done.moved.refs_6_, bf16[16,256,256]{2,1,0:T(8,128)(2,1)} %get-tuple-element.43.left.left_hbm.refs_17_.refs_19_, ...), custom_call_target="tpu_custom_call" | custom-call | tf_op jit(solution)/shard_map/first_tiles/pallas_call | solution.py:502
  171.1 16.4 %all-to-all-start.1 = ((f32[128,2,128]{2,1,0:T(2,128)}), f32[128,2,128]{2,1,0:T(2,128)S(1)}, u32[]{:S(2)}, u32[]{:S(2)}) async-start(f32[128,2,128]{2,1,0:T(2,128)} %bitcast.19), calls=%async_computation.1 | async-start | bytes 262144 | tf_op jit(solution)/shard_map/all_to_all | solution.py:738
  187.5 25.3 %cross_rows.1 = (f32[16,128]{1,0:T(8,128)}, f32[16,128]{1,0:T(8,128)}, f32[512,128]{1,0:T(8,128)}, s32[136]{0:T(256)}, s32[136]{0:T(256)}, /*index=5*/s32[128]{0:T(128)}) custom-call(s32[136]{0:T(256)} %get-tuple-element.48.slots.refs_3_, s32[136]{0:T(256)} %get-tuple-element.49.targets.refs_4_, s32[128]{0:T(128)} %get-tuple-element.50.bounds.refs_5_, ...), custom_call_target="tpu_custom_call" | custom-call | tf_op jit(solution)/shard_map/cross_rows/pallas_call | solution.py:592
  212.8 0.0 all-to-all-done.1
  212.8 18.0 %step_r.1 = (f32[48,128]{1,0:T(8,128)}, f32[48,128]{1,0:T(8,128)}, f32[512,128]{1,0:T(8,128)}) custom-call(s32[8,7]{1,0:T(8,128)} %refs_0_.5, s32[2,8]{1,0:T(2,128)} %bitcast.21, s32[2,8]{1,0:T(2,128)} %bitcast.25, s32[136]{0:T(256)} %get-tuple-element.55.refs_3_, s32[136]{0:T(256)} %get-tuple-element.56.refs_4_, s32[128]{0:T(128)} %get-tuple-element.57.refs_5_, ...), custom_call_target="tpu_custom_call" | custom-call | tf_op jit(solution)/shard_map/step_r/pallas_call | solution.py:727
  230.8 11.2 %all-to-all-start.2 = ((f32[128,4,128]{2,1,0:T(4,128)}), f32[128,4,128]{2,1,0:T(4,128)S(1)}, u32[]{:S(2)}, u32[]{:S(2)}) async-start(f32[128,4,128]{2,1,0:T(4,128)} %bitcast.18), calls=%async_computation.2 | async-start | bytes 524288 | tf_op jit(solution)/shard_map/all_to_all | solution.py:738
  241.9 13.9 %local_tiles.4 = (bf16[24,256,128]{2,1,0:T(8,128)(2,1)}, f32[48,128]{1,0:T(8,128)}, f32[16,128]{1,0:T(8,128)}) custom-call(bf16[16,256,256]{2,1,0:T(8,128)(2,1)} %get-tuple-element.43.left.left_hbm.refs_17_.refs_19_, bf16[16,128,256]{2,1,0:T(8,128)(2,1)} %get-tuple-element.44.right, f32[16,128]{1,0:T(8,128)} %get-tuple-element.60.refs_15_.bias_g, ...), custom_call_target="tpu_custom_call" | custom-call | tf_op jit(solution)/shard_map/local_tiles/pallas_call | solution.py:300
  255.8 0.0 all-to-all-done.2
  255.8 78.8 %step_cr.1 = (f32[16,128]{1,0:T(8,128)}, f32[16,128]{1,0:T(8,128)}, f32[48,128]{1,0:T(8,128)}, f32[48,128]{1,0:T(8,128)}, f32[512,128]{1,0:T(8,128)}) custom-call(s32[8,7]{1,0:T(8,128)} %refs_0_.5, s32[2,8]{1,0:T(2,128)} %bitcast.22, s32[2,8]{1,0:T(2,128)} %bitcast.26, s32[136]{0:T(256)} %get-tuple-element.48.slots.refs_3_, ...), custom_call_target="tpu_custom_call" | custom-call | tf_op jit(solution)/shard_map/step_cr/pallas_call | solution.py:727
  334.6 14.8 %all-to-all-start.3 = ((f32[128,4,128]{2,1,0:T(4,128)}), f32[128,4,128]{2,1,0:T(4,128)S(1)}, u32[]{:S(2)}, u32[]{:S(2)}) async-start(f32[128,4,128]{2,1,0:T(4,128)} %bitcast.17), calls=%async_computation.3 | async-start | bytes 524288 | tf_op jit(solution)/shard_map/all_to_all | solution.py:738
  349.4 13.9 %local_tiles.5 = (bf16[24,256,128]{2,1,0:T(8,128)(2,1)}, f32[48,128]{1,0:T(8,128)}, f32[16,128]{1,0:T(8,128)}) custom-call(bf16[16,256,256]{2,1,0:T(8,128)(2,1)} %get-tuple-element.43.left.left_hbm.refs_17_.refs_19_, bf16[16,128,256]{2,1,0:T(8,128)(2,1)} %get-tuple-element.44.right, f32[16,128]{1,0:T(8,128)} %get-tuple-element.70.bias_g.refs_15_, ...), custom_call_target="tpu_custom_call" | custom-call | tf_op jit(solution)/shard_map/local_tiles/pallas_call | solution.py:300
  363.3 0.0 all-to-all-done.3
  363.3 47.9 %step_c.1 = (f32[16,128]{1,0:T(8,128)}, f32[16,128]{1,0:T(8,128)}, f32[16,128]{1,0:T(8,128)}, f32[16,128]{1,0:T(8,128)}) custom-call(s32[8,7]{1,0:T(8,128)} %refs_0_.5, s32[2,8]{1,0:T(2,128)} %bitcast.23, s32[2,8]{1,0:T(2,128)} %bitcast.27, s32[136]{0:T(256)} %get-tuple-element.48.slots.refs_3_, s32[136]{0:T(256)} %get-tuple-element.49.targets.refs_4_, ...), custom_call_target="tpu_custom_call" | custom-call | tf_op jit(solution)/shard_map/step_c/pallas_call | solution.py:727
Async XLA Ops:
  5.2 117.2 %all-to-all-start = ((f32[128,136,128]{2,1,0:T(8,128)}), f32[128,136,128]{2,1,0:T(8,128)}, u32[]{:S(2)}, u32[]{:S(2)}) async-start(f32[128,136,128]{2,1,0:T(8,128)} %get-tuple-element.42), calls=%async_computation | async-start | bytes 17825792 | tf_op jit(solution)/shard_map/all_to_all | solution.py:738
  171.1 41.7 %all-to-all-start.1 = ((f32[128,2,128]{2,1,0:T(2,128)}), f32[128,2,128]{2,1,0:T(2,128)S(1)}, u32[]{:S(2)}, u32[]{:S(2)}) async-start(f32[128,2,128]{2,1,0:T(2,128)} %bitcast.19), calls=%async_computation.1 | async-start | bytes 262144 | tf_op jit(solution)/shard_map/all_to_all | solution.py:738
  230.8 25.1 %all-to-all-start.2 = ((f32[128,4,128]{2,1,0:T(4,128)}), f32[128,4,128]{2,1,0:T(4,128)S(1)}, u32[]{:S(2)}, u32[]{:S(2)}) async-start(f32[128,4,128]{2,1,0:T(4,128)} %bitcast.18), calls=%async_computation.2 | async-start | bytes 524288 | tf_op jit(solution)/shard_map/all_to_all | solution.py:738
  334.6 28.7 %all-to-all-start.3 = ((f32[128,4,128]{2,1,0:T(4,128)}), f32[128,4,128]{2,1,0:T(4,128)S(1)}, u32[]{:S(2)}, u32[]{:S(2)}) async-start(f32[128,4,128]{2,1,0:T(4,128)} %bitcast.17), calls=%async_computation.3 | async-start | bytes 524288 | tf_op jit(solution)/shard_map/all_to_all | solution.py:738
